TPU v7x, 1024 devices: a whole 4x4x32 slice. The times are simulated.
1024 devices in a mesh: expert: 16 (over z_hi, y, core), dp: 64 (over x, z_lo).
Axes of the slice: x: 4, y: 4, z: 32 (z_hi: 2, z_lo: 16; z = z_hi * 16 + z_lo), core: 2. Of those that a mesh axis runs over, the one named last changes fastest.
Arguments:
- tokens: bfloat16 [131072, 2048], P(('expert', 'dp')), may hold values from -6 to 6
- out_grad: bfloat16 [131072, 2048], P(('expert', 'dp')), may hold values from -6 to 6
- expert_ids: int32 [131072, 1], P(('expert', 'dp')), may hold values from 0 to 15; in each aligned block of 128 rows (0 to 127, 128 to 255, ...) at most 12 rows name the same one
- combine_ints: int32 [131072, 8], P(('expert', 'dp')), may hold values from 1 to 15
- w_gate: bfloat16 [16, 2048, 384], P('expert'), may hold values from -0.125 to 0.125
- w_up: bfloat16 [16, 2048, 384], P('expert'), may hold values from -0.125 to 0.125
- w_down: bfloat16 [16, 384, 2048], P('expert'), may hold values from -0.3125 to 0.3125
Outputs:
- combined: bfloat16 [131072, 2048], P(('expert', 'dp'))
- dinput: bfloat16 [131072, 2048], P(('expert', 'dp'))
- grad_down: float32 [16, 384, 2048], P('expert', None, 'dp')
Inputs may be any that keep to these rules, and one draw needn't show every extreme that they name: `expert_ids`: each row names one expert of the window. Among the 128 rows of one device no expert is named more than 12 times, and in every draw some expert is named exactly 12 times by the rows of some device.
All inputs are finite; a program needn't handle non-finite values.
Results may differ from a plain program's by a relative error of at most 0.0057.
Values may be sent and summed in bfloat16 or wider, within the bound.
No kernel may reach another device: no remote copies, remote signals or barrier semaphores. Data moves between devices by JAX's collectives and lax.ppermute only.
A program may use at most 64 MiB of HBM per device.

v0:
```python
import jax
import jax.numpy as jnp
from jax import lax
from jax.sharding import PartitionSpec as P

CAP = 12


def body(tokens, out_grad, expert_ids, combine_ints, w_gate, w_up, w_down):
    tok_rows, model_width = tokens.shape
    route_count = expert_ids.shape[1]
    groups = lax.axis_size("expert")
    local_count = w_gate.shape[0]
    experts = groups * local_count
    flat_ids = expert_ids.reshape(-1)
    onehot = (flat_ids[:, None] == jnp.arange(experts, dtype=jnp.int32)[None, :]).astype(jnp.int32)
    slot_rank = jnp.sum((jnp.cumsum(onehot, axis=0) - onehot) * onehot, axis=1)
    slot_index = flat_ids * CAP + slot_rank
    owner_row = jnp.arange(tok_rows * route_count, dtype=jnp.int32) // route_count
    all_weights = combine_ints.astype(jnp.float32)
    weights = (all_weights[:, :route_count] / jnp.sum(all_weights, axis=1, keepdims=True)).reshape(
        -1
    )
    scaled = (weights[:, None] * out_grad[owner_row].astype(jnp.float32)).astype(jnp.bfloat16)
    empty_buf = jnp.zeros((experts * CAP, model_width), jnp.bfloat16)
    send_rows = empty_buf.at[slot_index].set(tokens[owner_row])
    send_grads = empty_buf.at[slot_index].set(scaled)
    recv_rows, recv_grads = (
        lax.all_to_all(send_rows, "expert", split_axis=0, concat_axis=0, tiled=True),
        lax.all_to_all(send_grads, "expert", split_axis=0, concat_axis=0, tiled=True),
    )
    rows_four = recv_rows.reshape(groups, local_count, CAP, model_width)
    grads_four = recv_grads.reshape(groups, local_count, CAP, model_width)
    gate_act = jnp.einsum("slcd,ldf->slcf", rows_four, w_gate, preferred_element_type=jnp.float32)
    up_act = jnp.einsum("slcd,ldf->slcf", rows_four, w_up, preferred_element_type=jnp.float32)
    gate_sig = jax.nn.sigmoid(gate_act)
    gate_silu = gate_act * gate_sig
    hidden = (gate_silu * up_act).astype(jnp.bfloat16)
    result = jnp.einsum(
        "slcf,lfd->slcd", hidden, w_down, preferred_element_type=jnp.float32
    ).astype(jnp.bfloat16)
    returned = lax.all_to_all(
        result.reshape(-1, model_width), "expert", split_axis=0, concat_axis=0, tiled=True
    )
    dhidden = jnp.einsum("slcd,lfd->slcf", grads_four, w_down, preferred_element_type=jnp.float32)
    grad_gate = (dhidden * up_act * gate_sig * (1.0 + gate_act * (1.0 - gate_sig))).astype(
        jnp.bfloat16
    )
    grad_up = (dhidden * gate_silu).astype(jnp.bfloat16)
    slot_grad = (
        jnp.einsum("slcf,ldf->slcd", grad_gate, w_gate, preferred_element_type=jnp.float32)
        + jnp.einsum("slcf,ldf->slcd", grad_up, w_up, preferred_element_type=jnp.float32)
    ).astype(jnp.bfloat16)
    grad_back = lax.all_to_all(
        slot_grad.reshape(-1, model_width), "expert", split_axis=0, concat_axis=0, tiled=True
    )
    grad_term = jnp.einsum("slcf,slcd->lfd", hidden, grads_four, preferred_element_type=jnp.float32)
    grad_share = lax.psum_scatter(grad_term, "dp", scatter_dimension=2, tiled=True)
    combined = jnp.sum(
        (weights[:, None] * returned[slot_index].astype(jnp.float32)).reshape(
            tok_rows, route_count, model_width
        ),
        axis=1,
    ).astype(jnp.bfloat16)
    dinput = jnp.sum(
        grad_back[slot_index].astype(jnp.float32).reshape(tok_rows, route_count, model_width),
        axis=1,
    ).astype(jnp.bfloat16)
    return (combined, dinput, grad_share)


def solution(mesh):
    return jax.shard_map(
        body,
        mesh=mesh,
        in_specs=(
            P(("expert", "dp"), None),
            P(("expert", "dp"), None),
            P(("expert", "dp"), None),
            P(("expert", "dp"), None),
            P("expert", None, None),
            P("expert", None, None),
            P("expert", None, None),
        ),
        out_specs=(P(("expert", "dp"), None), P(("expert", "dp"), None), P("expert", None, "dp")),
        check_vma=False,
    )
```

profile of v0, /device:TPU:24, one launch (start us, length us, event | category | flops | bytes accessed | tf_op | source)
XLA Modules:
  0.0 1944.9 jit_solution(12855771325750517117)
XLA Ops:
  7.2 0.0 copy-start
  7.2 0.9 fusion.32
  8.0 0.2 reduce_window_sum.11
  8.2 0.8 select_reduce_fusion
  9.0 0.7 fusion.33
  9.7 3.7 scatter_custom_fusion
  13.4 0.0 copy-start.7
  13.5 1.2 all_to_all.24
  14.6 31.2 %all-to-all-start = ((bf16[16,12,2048]{2,1,0:T(8,128)(2,1)}), bf16[16,12,2048]{2,1,0:T(8,128)(2,1)S(1)}, u32[]{:S(2)}, u32[]{:S(2)}) async-start(bf16[16,12,2048]{2,1,0:T(8,128)(2,1)} %all_to_all.24), calls=%async_computation | async-start | bytes 2097152 | tf_op jit(solution)/shard_map/all_to_all | solution.py:29
  45.9 3.8 scatter_custom_fusion.1
  49.7 1.1 all_to_all.28
  50.8 41.1 %all-to-all-done = bf16[16,12,2048]{2,1,0:T(8,128)(2,1)S(1)} async-done(((bf16[16,12,2048]{2,1,0:T(8,128)(2,1)}), bf16[16,12,2048]{2,1,0:T(8,128)(2,1)S(1)}, u32[]{:S(2)}, u32[]{:S(2)}) %all-to-all-start) | async-done | bytes 786464 | tf_op jit(solution)/shard_map/all_to_all | solution.py:29
  91.9 5.7 all-to-all-start.2
  97.6 0.0 copy-start.1
  97.6 0.7 fusion.9
  98.3 0.7 copy-done.1
  99.0 0.7 fusion.5
  99.7 0.0 copy-start.4
  99.7 60.1 %all-to-all-done.2 = bf16[16,12,2048]{2,1,0:T(8,128)(2,1)} async-done(((bf16[16,12,2048]{2,1,0:T(8,128)(2,1)}), bf16[16,12,2048]{2,1,0:T(8,128)(2,1)}, u32[]{:S(2)}, u32[]{:S(2)}) %all-to-all-start.2) | async-done | bytes 786464 | tf_op jit(solution)/shard_map/all_to_all | solution.py:30
  159.8 2.5 fusion.1
  162.3 0.0 copy-start.2
  162.3 0.8 fusion.7
  163.1 0.5 copy-done.2
  163.7 0.8 fusion
  164.4 1.4 copy.20
  165.9 24.3 %all-to-all-start.3 = ((bf16[16,12,2048]{2,1,0:T(8,128)(2,1)}), bf16[16,12,2048]{2,1,0:T(8,128)(2,1)}, u32[]{:S(2)}, u32[]{:S(2)}) async-start(bf16[16,12,2048]{2,1,0:T(8,128)(2,1)} %copy.20), calls=%async_computation.3 | async-start | bytes 2097152 | tf_op jit(solution)/shard_map/all_to_all | solution.py:54
  190.2 1.2 fusion.27
  191.4 0.0 copy-start.5
  191.4 0.7 copy-done.5
  192.0 0.6 convolution_convert_fusion
  192.6 0.0 copy-start.6
  192.6 1.5 copy.18
  194.1 64.9 %all-to-all-done.3 = bf16[16,12,2048]{2,1,0:T(8,128)(2,1)} async-done(((bf16[16,12,2048]{2,1,0:T(8,128)(2,1)}), bf16[16,12,2048]{2,1,0:T(8,128)(2,1)}, u32[]{:S(2)}, u32[]{:S(2)}) %all-to-all-start.3) | async-done | bytes 786464 | tf_op jit(solution)/shard_map/all_to_all | solution.py:54
  258.9 5.6 all-to-all-start.1
  264.6 0.0 all-reduce.3.cloned.1.call-start
  264.6 3.7 convolution_bitcast_fusion
  268.3 8.6 copy.22
  276.9 0.0 all-reduce.3.cloned.1.call-update
  276.9 1.3 dynamic-slice
  278.8 1652.7 %all-reduce.3.cloned.1.call-done = f32[1,384,2048]{1,0,2:T(1,128)} async-done(((f32[1,384,2048]{1,0,2:T(1,128)}), f32[1,384,2048]{1,0,2:T(1,128)}) %all-reduce.3.cloned.1.call-update) | async-done | bytes 3145744
  1931.5 0.8 constant_dynamic-slice_fusion
  1932.4 0.6 copy.23
  1933.0 1.3 all_to_all.31
  1934.3 1.7 gather_fusion.1
  1936.0 0.0 all-to-all-done.1
  1936.0 0.2 all_to_all.27
  1936.2 0.9 gather_fusion
  1937.1 0.9 multiply_convert_fusion.1
  (12 shorter events, 0.1 us)
Async XLA Ops:
  7.2 90.4 %copy-start = (bf16[1,2048,384]{2,1,0:T(8,128)(2,1)S(1)}, bf16[1,2048,384]{2,1,0:T(8,128)(2,1)}, u32[]{:S(2)}) copy-start(bf16[1,2048,384]{2,1,0:T(8,128)(2,1)} %param.11) | copy-start | bytes 4718596
  13.4 32.4 %copy-start.7 = (s32[128,8]{0,1:T(8,128)S(1)}, s32[128,8]{0,1:T(8,128)}, u32[]{:S(2)}) copy-start(s32[128,8]{0,1:T(8,128)} %param.10) | copy-start | bytes 12292
  14.6 77.3 %all-to-all-start = ((bf16[16,12,2048]{2,1,0:T(8,128)(2,1)}), bf16[16,12,2048]{2,1,0:T(8,128)(2,1)S(1)}, u32[]{:S(2)}, u32[]{:S(2)}) async-start(bf16[16,12,2048]{2,1,0:T(8,128)(2,1)} %all_to_all.24), calls=%async_computation | async-start | bytes 2097152 | tf_op jit(solution)/shard_map/all_to_all | solution.py:29
  91.9 67.9 %all-to-all-start.2 = ((bf16[16,12,2048]{2,1,0:T(8,128)(2,1)}), bf16[16,12,2048]{2,1,0:T(8,128)(2,1)}, u32[]{:S(2)}, u32[]{:S(2)}) async-start(bf16[16,12,2048]{2,1,0:T(8,128)(2,1)} %all_to_all.28), calls=%async_computation.2 | async-start | bytes 2097152 | tf_op jit(solution)/shard_map/all_to_all | solution.py:30
  97.6 1.4 copy-start.1
  99.7 63.4 %copy-start.4 = (f32[16,12,384]{2,1,0:T(8,128)}, f32[16,12,384]{2,1,0:T(8,128)S(1)}, u32[]{:S(2)}) copy-start(f32[16,12,384]{2,1,0:T(8,128)S(1)} %fusion.5) | copy-start | bytes 884740
  162.3 1.4 copy-start.2
  165.9 26.2 %copy-start.3 = (bf16[1,384,2048]{2,1,0:T(8,128)(2,1)S(1)}, bf16[1,384,2048]{2,1,0:T(8,128)(2,1)}, u32[]{:S(2)}) copy-start(bf16[1,384,2048]{2,1,0:T(8,128)(2,1)} %param.13) | copy-start | bytes 4718596
  165.9 93.1 %all-to-all-start.3 = ((bf16[16,12,2048]{2,1,0:T(8,128)(2,1)}), bf16[16,12,2048]{2,1,0:T(8,128)(2,1)}, u32[]{:S(2)}, u32[]{:S(2)}) async-start(bf16[16,12,2048]{2,1,0:T(8,128)(2,1)} %copy.20), calls=%async_computation.3 | async-start | bytes 2097152 | tf_op jit(solution)/shard_map/all_to_all | solution.py:54
  191.4 0.7 copy-start.5
  192.6 72.0 %copy-start.6 = (bf16[16,12,384]{2,0,1:T(8,128)(2,1)S(1)}, bf16[16,12,384]{2,0,1:T(8,128)(2,1)}, u32[]{:S(2)}) copy-start(bf16[16,12,384]{2,0,1:T(8,128)(2,1)} %copy-done.5) | copy-start | bytes 442372
  258.9 1677.1 %all-to-all-start.1 = ((bf16[16,12,2048]{2,1,0:T(8,128)(2,1)}), bf16[16,12,2048]{2,1,0:T(8,128)(2,1)S(1)}, u32[]{:S(2)}, u32[]{:S(2)}) async-start(bf16[16,12,2048]{2,1,0:T(8,128)(2,1)} %copy.18), calls=%async_computation.1 | async-start | bytes 2097152 | tf_op jit(solution)/shard_map/all_to_all | solution.py:42
  264.6 1667.0 %all-reduce.3.cloned.1.call-start = ((), (), s32[]{:S(2)}) async-start(), calls=%async_computation.4 | async-start | bytes 6291456
Sparse Core Ops, SparseCore 0:
  277.0 1654.4 all-reduce.2
where the time goes:
time: 1950 us; the launch traced here: 1940 us
  waiting for transfers between devices  1820 us (93%)
  starting transfers between devices  66.8 us (3%)
  local copies, waits for them, and re-layouts  26.3 us (1%)
    unnamed x2, waiting for transfers between devices  1650 us
    all_to_all x1, waiting for transfers between devices, body(): lax.all_to_all(slot_grad.reshape(-1, model_width), 'expert', split_axis=0...  64.9 us
    all_to_all x1, waiting for transfers between devices, body(): lax.all_to_all(send_grads, 'expert', split_axis=0, concat_axis=0, tiled=T...  60.1 us
    all_to_all x1, waiting for transfers between devices, body(): lax.all_to_all(send_rows, 'expert', split_axis=0, concat_axis=0, tiled=True)  41.1 us
  transfers between devices with their start and end apart: 5, of which 4 were waited for; matrix products, arithmetic and copies ran while one was open for 1% of the time, Pallas kernels for 0%

commit v1 on v0

v1 whole, which is shorter than its diff:
```python
import functools

import jax
import jax.numpy as jnp
from jax import lax
from jax.experimental import pallas as pl
from jax.experimental.pallas import tpu as pltpu
from jax.sharding import Mesh, PartitionSpec as P

CAP = 12
AXES = ("zh", "y", "c", "x", "zl")
SPLIT = (2, 4, 2, 4, 16)
BF16 = jnp.bfloat16
F32 = jnp.float32


def dot(a, b, ca=1, cb=0):
    return lax.dot_general(a, b, (((ca,), (cb,)), ((), ())), preferred_element_type=F32)


def slot_onehot(ids, near, halves):
    tokens = ids.shape[1]
    experts = near * halves
    hot = (lax.broadcasted_iota(jnp.int32, (experts, tokens), 0) == ids).astype(F32)
    before = (
        lax.broadcasted_iota(jnp.int32, (tokens, tokens), 0)
        < lax.broadcasted_iota(jnp.int32, (tokens, tokens), 1)
    ).astype(BF16)
    counts = dot(hot.astype(BF16), before)
    rank = jnp.sum(hot * counts, axis=0, keepdims=True).astype(jnp.int32)
    half = sum((ids >= near * k).astype(jnp.int32) for k in range(1, halves))
    slot = (ids - near * half) * (halves * CAP) + half * CAP + rank
    return lax.broadcasted_iota(jnp.int32, (experts * CAP, tokens), 0) == slot


def token_weights(ints):
    ints = ints.astype(F32)
    return ints[0:1] / jnp.sum(ints, axis=0, keepdims=True)


def dispatch_kernel(near, halves, ids_ref, ints_ref, tok_ref, grad_ref, rows_ref, grads_ref):
    hot = slot_onehot(ids_ref[...], near, halves)
    pick = hot.astype(BF16)
    rows_ref[...] = dot(pick, tok_ref[...]).astype(BF16)
    scale = jnp.sum(jnp.where(hot, token_weights(ints_ref[...]), 0.0), axis=1, keepdims=True)
    grads_ref[...] = (scale * dot(pick, grad_ref[...])).astype(BF16)


def combine_kernel(near, halves, ids_ref, ints_ref, rows_ref, grads_ref, out_ref, din_ref):
    hot = slot_onehot(ids_ref[...], near, halves)
    pick = hot.astype(BF16)
    tokens = pick.shape[1]
    eye = lax.broadcasted_iota(jnp.int32, (tokens, tokens), 0) == lax.broadcasted_iota(
        jnp.int32, (tokens, tokens), 1
    )
    scale = jnp.sum(jnp.where(eye, token_weights(ints_ref[...]), 0.0), axis=1, keepdims=True)
    out_ref[...] = (scale * dot(pick, rows_ref[...], 0, 0)).astype(BF16)
    din_ref[...] = dot(pick, grads_ref[...], 0, 0).astype(BF16)


def pieces_kernel(at_ref, gate_ref, up_ref, down_ref, out_ref):
    rows = gate_ref.shape[0]
    lanes = down_ref.shape[1]
    shift = lax.rem(at_ref[0], lanes // rows) * rows
    pick = (
        lax.broadcasted_iota(jnp.int32, (rows, lanes), 1)
        == lax.broadcasted_iota(jnp.int32, (rows, lanes), 0) + shift
    ).astype(BF16)
    out_ref[0] = gate_ref[...]
    out_ref[1] = up_ref[...]
    out_ref[2] = dot(pick, down_ref[...], 1, 1).astype(BF16)


def expert_math(rows, grads, keep, w_gate, w_up, dh):
    gate = dot(rows, w_gate)
    up = dot(rows, w_up)
    sig = jax.nn.sigmoid(gate)
    silu = gate * sig
    zero = jnp.zeros_like(gate)
    hidden = jnp.where(keep, silu * up, zero).astype(BF16)
    dgate = jnp.where(keep, dh * up * sig * (1.0 + gate * (1.0 - sig)), zero).astype(BF16)
    dup = jnp.where(keep, dh * silu, zero).astype(BF16)
    return hidden, dgate, dup


def row_mask(half, count, halves, width):
    at = lax.broadcasted_iota(jnp.int32, (count, width), 0)
    return lax.div(lax.rem(at, halves * CAP), CAP) == half


def near_kernel(halves, half_ref, rows_ref, grads_ref, wg_ref, wu_ref, wd_ref, out_ref, dx_ref, gt_ref):
    rows, grads = rows_ref[...], grads_ref[...]
    w_gate, w_up, w_down = wg_ref[...], wu_ref[...], wd_ref[...]
    keep = row_mask(half_ref[0], rows.shape[0], halves, w_gate.shape[1])
    hidden, dgate, dup = expert_math(rows, grads, keep, w_gate, w_up, dot(grads, w_down, 1, 1))
    out_ref[...] = dot(hidden, w_down).astype(BF16)
    dx_ref[...] = (dot(dgate, w_gate, 1, 1) + dot(dup, w_up, 1, 1)).astype(BF16)
    gt_ref[...] = dot(grads, hidden, 0, 0)


def far_kernel(halves, half_ref, rows_ref, grads_ref, w_ref, o_ref, d_ref, out_ref, dx_ref, gt_ref):
    rows, grads = rows_ref[...], grads_ref[...]
    blocks, _, depth, width = w_ref.shape
    w_gate, w_up, w_down = (w_ref[:, k].reshape(blocks * depth, width) for k in range(3))
    keep = row_mask(1 - half_ref[0], rows.shape[0], halves, width)
    hidden, dgate, dup = expert_math(rows, grads, keep, w_gate, w_up, dot(grads, w_down))
    gt_ref[...] = dot(grads, hidden, 0, 0)
    out_ref[...] = dot(hidden, w_down, 1, 1).astype(BF16) + o_ref[...]
    dx_ref[...] = (dot(dgate, w_gate, 1, 1) + dot(dup, w_up, 1, 1)).astype(BF16) + d_ref[...]


def call(kernel, outs, *args, scalar=False, flops=0):
    vmem = pl.BlockSpec(memory_space=pltpu.VMEM)
    smem = pl.BlockSpec(memory_space=pltpu.SMEM)
    size = sum(a.size * a.dtype.itemsize for a in (*args, *outs))
    return pl.pallas_call(
        kernel,
        out_shape=outs,
        in_specs=[smem if scalar and k == 0 else vmem for k in range(len(args))],
        out_specs=tuple(vmem for _ in outs),
        compiler_params=pltpu.CompilerParams(vmem_limit_bytes=60 << 20),
        cost_estimate=pl.CostEstimate(flops=flops, bytes_accessed=size, transcendentals=0),
    )(*args)


def body(tokens, out_grad, expert_ids, combine_ints, w_gate, w_up, w_down):
    count, width = tokens.shape
    hidden_width = w_gate.shape[2]
    halves = lax.axis_size("zh")
    near = lax.axis_size("y") * lax.axis_size("c")
    nx, nz = lax.axis_size("x"), lax.axis_size("zl")
    shards = nx * nz
    depth = width // shards
    slots = near * halves * CAP
    half = lax.axis_index("zh").astype(jnp.int32).reshape(1)
    shard = (lax.axis_index("x") * nz + lax.axis_index("zl")).astype(jnp.int32).reshape(1)
    w_gate, w_up, w_down = w_gate[0], w_up[0], w_down[0]

    per = 128 // depth
    piece = pl.pallas_call(
        pieces_kernel,
        grid_spec=pltpu.PrefetchScalarGridSpec(
            num_scalar_prefetch=1,
            grid=(1,),
            in_specs=[
                pl.BlockSpec((depth, hidden_width), lambda i, at: (at[0], 0)),
                pl.BlockSpec((depth, hidden_width), lambda i, at: (at[0], 0)),
                pl.BlockSpec((hidden_width, 128), lambda i, at: (0, lax.div(at[0], per))),
            ],
            out_specs=pl.BlockSpec((3, depth, hidden_width), lambda i, at: (0, 0, 0)),
        ),
        out_shape=jax.ShapeDtypeStruct((3, depth, hidden_width), BF16),
    )(shard, w_gate, w_up, w_down)
    ring = lax.all_gather(
        piece.reshape(3 * depth, hidden_width), ("zh", "zl"), axis=0, tiled=True
    )
    other = lax.dynamic_slice_in_dim(
        ring, (1 - half[0]) * (nz * 3 * depth), nz * 3 * depth, axis=0
    )
    far = lax.all_gather(other, "x", axis=0, tiled=True).reshape(
        shards, 3, depth, hidden_width
    )

    ids = expert_ids.reshape(1, count)
    ints = combine_ints.T
    rows_shape = jax.ShapeDtypeStruct((slots, width), BF16)
    grad_shape = jax.ShapeDtypeStruct((width, hidden_width), F32)
    send_rows, send_grads = call(
        functools.partial(dispatch_kernel, near, halves),
        (rows_shape, rows_shape), ids, ints, tokens, out_grad,
        flops=4 * slots * count * width,
    )

    def swap(v):
        return lax.all_to_all(v, ("y", "c"), split_axis=0, concat_axis=0, tiled=True)

    rows, grads = swap(send_rows), swap(send_grads)
    work = 14 * slots * width * hidden_width
    near_out, near_dx, near_gt = call(
        functools.partial(near_kernel, halves),
        (rows_shape, rows_shape, grad_shape), half, rows, grads, w_gate, w_up, w_down,
        scalar=True, flops=work,
    )
    out, dx, far_gt = call(
        functools.partial(far_kernel, halves),
        (rows_shape, rows_shape, grad_shape), half, rows, grads, far, near_out, near_dx,
        scalar=True, flops=work,
    )

    def over_x(v):
        return lax.psum_scatter(v, "x", scatter_dimension=0, tiled=True)

    near_gx, far_gx = over_x(near_gt), over_x(far_gt)
    low = jnp.where(half[0] == 0, near_gx, far_gx)
    high = jnp.where(half[0] == 0, far_gx, near_gx)
    both = jnp.concatenate([low, high], axis=0)
    grad = lax.psum_scatter(both, ("zh", "zl"), scatter_dimension=0, tiled=True)

    combined, dinput = call(
        functools.partial(combine_kernel, near, halves),
        (jax.ShapeDtypeStruct((count, width), BF16),) * 2, ids, ints, swap(out), swap(dx),
        flops=4 * slots * count * width,
    )
    return combined, dinput, grad.T[None]


def build(mesh, split):
    fine = Mesh(mesh.devices.reshape(split), AXES)
    token = P(AXES, None)
    expert = P(("zh", "y", "c"), None, None)
    return jax.shard_map(
        body,
        mesh=fine,
        in_specs=(token, token, token, token, expert, expert, expert),
        out_specs=(token, token, P(("zh", "y", "c"), None, ("x", "zl"))),
        check_vma=False,
    )


def solution(mesh):
    return build(mesh, SPLIT)
```

time: 1950 us -> 489 us (0.25)
  waiting for transfers between devices: 1820 us -> 380 us
  starting transfers between devices: 66.8 us -> 0.21 us
  blocking collectives: 0 us -> 64.4 us
  Pallas kernels: 0 us -> 24.3 us
  local copies, waits for them, and re-layouts: 26.3 us -> 3.58 us
    unnamed x2 -> x5, waiting for transfers between devices: 1650 us -> 0.08 us
    reduce_scatter x0 -> x3, waiting for transfers between devices: none -> 213 us  [the longest x2 111 us: over_x(): return lax.psum_scatter(v, 'x', scatter_dimension=0, tiled=True)]
    all_gather x0 -> x2, waiting for transfers between devices: none -> 166 us  [the longest x1 148 us: body(): lax.all_gather(piece.reshape(3 * depth, hidden_width), ('zh', 'zl'), axis...]
    all_to_all x4 -> x0, waiting for transfers between devices: 166 us -> none  [the longest x1 64.9 us: body(): lax.all_to_all(slot_grad.reshape(-1, model_width), 'expert', split_axis=0...]
    all_to_all x4 -> x0, starting transfers between devices: 66.8 us -> none  [the longest x1 31.2 us: body(): lax.all_to_all(send_rows, 'expert', split_axis=0, concat_axis=0, tiled=True)]
    all_to_all x0 -> x4, blocking collectives: none -> 64.4 us  [swap(): lax.all_to_all(v, ('y', 'c'), split_axis=0, concat_axis=0, tiled=True)]
    pallas_call x0 -> x5, Pallas kernels: none -> 24.3 us  [the longest x4 22.6 us: call(): pl.pallas_call(kernel, out_shape=outs, in_specs=[smem if scalar and k ==...]
  transfers between devices with their start and end apart: 5 -> 5, of which waited for: 4 -> 5; matrix products, arithmetic and copies ran while one was open for 1% -> 0% of each run, Pallas kernels for 0% -> 5%
where the time goes in v1:
time: 489 us
  waiting for transfers between devices  380 us (78%)
  blocking collectives  64.4 us (13%)
  Pallas kernels  24.3 us (5%)
  between operations  13.8 us (3%)
    all_gather x1, waiting for transfers between devices, body(): lax.all_gather(piece.reshape(3 * depth, hidden_width), ('zh', 'zl'), axis...  148 us
    reduce_scatter x2, waiting for transfers between devices, over_x(): return lax.psum_scatter(v, 'x', scatter_dimension=0, tiled=True)  111 us
    reduce_scatter x1, waiting for transfers between devices, body(): grad = lax.psum_scatter(both, ('zh', 'zl'), scatter_dimension=0, tiled=True)  102 us
    all_to_all x4, blocking collectives, swap(): lax.all_to_all(v, ('y', 'c'), split_axis=0, concat_axis=0, tiled=True)  64.4 us
    pallas_call x4, Pallas kernels, call(): pl.pallas_call(kernel, out_shape=outs, in_specs=[smem if scalar and k ==...  22.6 us
    all_gather x1, waiting for transfers between devices, body(): lax.all_gather(other, 'x', axis=0, tiled=True)  18 us
  transfers between devices with their start and end apart: 5, of which 5 were waited for; matrix products, arithmetic and copies ran while one was open for 0% of the time, Pallas kernels for 5%

profile of v1, /device:TPU:24, one launch (start us, length us, event | category | flops | bytes accessed | tf_op | source)
XLA Modules:
  0.0 488.7 jit_solution(4320277595275315333)
XLA Ops:
  7.2 0.0 all-gather.3.cloned.1.call-start
  7.2 1.7 shard_map.95
  8.9 0.0 all-gather.3.cloned.1.call-update
  9.0 0.0 all-gather.5.cloned.1.call-start
  9.0 148.3 %all-gather.3.cloned.1.call-done = bf16[3072,384]{1,0:T(8,128)(2,1)} async-done(((bf16[96,384]{1,0:T(8,128)(2,1)}), bf16[3072,384]{1,0:T(8,128)(2,1)}) %all-gather.3.cloned.1.call-update) | async-done | bytes 2359312 | tf_op jit(solution)/shard_map/all_gather | solution.py:154
  157.3 2.5 constant_dynamic-slice_fusion
  159.8 0.0 all-gather.5.cloned.1.call-update
  159.8 0.0 reduce-scatter.4.cloned.1.call-start
  159.9 2.9 shard_map.94
  162.8 0.0 copy-start.2
  162.8 16.1 %all_to_all.44 = bf16[8,24,2048]{2,1,0:T(8,128)(2,1)} all-to-all(bf16[8,24,2048]{2,1,0:T(8,128)(2,1)} %bitcast.36), channel_id=1, replica_groups=mesh['zh'=2,'y'=4,'c'=2,'x'=4,'zl'=16] {'y','c'}, dimensions={0} | all-to-all | bytes 1572864 | tf_op jit(solution)/shard_map/all_to_all | solution.py:175
  178.9 0.0 copy-done.2
  178.9 16.3 %all_to_all.45 = bf16[8,24,2048]{2,1,0:T(8,128)(2,1)} all-to-all(bf16[8,24,2048]{2,1,0:T(8,128)(2,1)S(1)} %bitcast.35), channel_id=1, replica_groups=mesh['zh'=2,'y'=4,'c'=2,'x'=4,'zl'=16] {'y','c'}, dimensions={0} | all-to-all | bytes 1572864 | tf_op jit(solution)/shard_map/all_to_all | solution.py:175
  195.2 8.2 %shard_map.96 = (bf16[192,2048]{1,0:T(8,128)(2,1)}, bf16[192,2048]{1,0:T(8,128)(2,1)}, f32[2048,384]{1,0:T(8,128)}) custom-call(s32[1]{0:T(128)} %bitcast.2.half_ref, bf16[192,2048]{1,0:T(8,128)(2,1)} %bitcast.23, bf16[192,2048]{1,0:T(8,128)(2,1)} %bitcast.25, bf16[2048,384]{1,0:T(8,128)(2,1)} %bitcast.28, bf16[2048,384]{1,0:T(8,128)(2,1)} %bitcast.30, ...), custom_call_target="tpu_custom_call" | custom-call | flops 2113929216 | bytes 11010052 | tf_op jit(solution)/shard_map/pallas_call | solution.py:116
  203.3 0.0 reduce-scatter.4.cloned.1.call-update
  203.3 0.0 reduce-scatter.6.cloned.1.call-start
  203.4 18.0 %all-gather.5.cloned.1.call-done = bf16[6144,384]{1,0:T(8,128)(2,1)} async-done(((bf16[1536,384]{1,0:T(8,128)(2,1)}), bf16[6144,384]{1,0:T(8,128)(2,1)}) %all-gather.5.cloned.1.call-update) | async-done | bytes 4718608 | tf_op jit(solution)/shard_map/all_gather | solution.py:160
  221.4 8.7 %shard_map.97 = (bf16[192,2048]{1,0:T(8,128)(2,1)}, bf16[192,2048]{1,0:T(8,128)(2,1)}, f32[2048,384]{1,0:T(8,128)}) custom-call(s32[1]{0:T(128)} %bitcast.2.half_ref, bf16[192,2048]{1,0:T(8,128)(2,1)} %bitcast.24, bf16[192,2048]{1,0:T(8,128)(2,1)} %bitcast.26, bf16[64,3,32,384]{3,2,1,0:T(8,128)(2,1)} %bitcast.20, bf16[192,2048]{1,0:T(8,128)(2,1)} %get-tuple-element.15.o_ref, ...), custom_call_target="tpu_custom_call" | custom-call | flops 2113929216 | bytes 12582916 | tf_op jit(solution)/shard_map/pallas_call | solution.py:116
  230.1 0.0 reduce-scatter.6.cloned.1.call-update
  230.1 0.0 reduce-scatter.8.cloned.1.call-start
  230.2 51.4 %reduce-scatter.4.cloned.1.call-done = f32[512,384]{1,0:T(8,128)} async-done(((f32[2048,384]{1,0:T(8,128)}), f32[512,384]{1,0:T(8,128)}) %reduce-scatter.4.cloned.1.call-update) | async-done | bytes 786448 | tf_op jit(solution)/shard_map/reduce_scatter | solution.py:191
  281.6 59.4 %reduce-scatter.6.cloned.1.call-done = f32[512,384]{1,0:T(8,128)} async-done(((f32[2048,384]{1,0:T(8,128)}), f32[512,384]{1,0:T(8,128)}) %reduce-scatter.6.cloned.1.call-update) | async-done | bytes 786448 | tf_op jit(solution)/shard_map/reduce_scatter | solution.py:191
  341.0 1.5 broadcast_select_fusion.1
  342.5 1.3 pad_maximum_fusion
  343.8 0.0 copy-start.1
  343.8 0.0 copy-start
  343.8 0.0 reduce-scatter.8.cloned.1.call-update
  343.8 1.1 copy-done.1
  344.9 15.7 %all_to_all.46 = bf16[8,24,2048]{2,1,0:T(8,128)(2,1)} all-to-all(bf16[8,24,2048]{2,1,0:T(8,128)(2,1)S(1)} %bitcast.34), channel_id=1, replica_groups=mesh['zh'=2,'y'=4,'c'=2,'x'=4,'zl'=16] {'y','c'}, dimensions={0} | all-to-all | bytes 1572864 | tf_op jit(solution)/shard_map/all_to_all | solution.py:175
  360.6 0.0 copy-done
  360.6 16.2 %all_to_all.47 = bf16[8,24,2048]{2,1,0:T(8,128)(2,1)} all-to-all(bf16[8,24,2048]{2,1,0:T(8,128)(2,1)S(1)} %bitcast.33), channel_id=1, replica_groups=mesh['zh'=2,'y'=4,'c'=2,'x'=4,'zl'=16] {'y','c'}, dimensions={0} | all-to-all | bytes 1572864 | tf_op jit(solution)/shard_map/all_to_all | solution.py:175
  376.9 2.8 shard_map.98
  379.7 102.4 %reduce-scatter.8.cloned.1.call-done = f32[32,384]{1,0:T(8,128)} async-done(((f32[1024,384]{1,0:T(8,128)}), f32[32,384]{1,0:T(8,128)}) %reduce-scatter.8.cloned.1.call-update) | async-done | bytes 49168 | tf_op jit(solution)/shard_map/reduce_scatter | solution.py:197
Async XLA Ops:
  7.2 150.2 %all-gather.3.cloned.1.call-start = ((), (), s32[]{:S(2)}) async-start(), calls=%async_computation.7 | async-start | bytes 2433024 | tf_op jit(solution)/shard_map/all_gather | solution.py:154
  9.0 212.4 %all-gather.5.cloned.1.call-start = ((), (), s32[]{:S(2)}) async-start(), calls=%async_computation.8 | async-start | bytes 5898240 | tf_op jit(solution)/shard_map/all_gather | solution.py:160
  159.8 121.8 %reduce-scatter.4.cloned.1.call-start = ((), (), s32[]{:S(2)}) async-start(), calls=%async_computation.9 | async-start | bytes 3932160 | tf_op jit(solution)/shard_map/reduce_scatter | solution.py:191
  162.8 16.1 %copy-start.2 = (bf16[192,2048]{1,0:T(8,128)(2,1)S(1)}, bf16[192,2048]{1,0:T(8,128)(2,1)}, u32[]{:S(2)}) copy-start(bf16[192,2048]{1,0:T(8,128)(2,1)} %get-tuple-element.14) | copy-start | bytes 2359300
  203.3 137.7 %reduce-scatter.6.cloned.1.call-start = ((), (), s32[]{:S(2)}) async-start(), calls=%async_computation.10 | async-start | bytes 3932160 | tf_op jit(solution)/shard_map/reduce_scatter | solution.py:191
  230.1 252.1 %reduce-scatter.8.cloned.1.call-start = ((), (), s32[]{:S(2)}) async-start(), calls=%async_computation.11 | async-start | bytes 1622016 | tf_op jit(solution)/shard_map/reduce_scatter | solution.py:197
  343.8 1.1 copy-start.1
  343.8 16.9 %copy-start = (bf16[192,2048]{1,0:T(8,128)(2,1)S(1)}, bf16[192,2048]{1,0:T(8,128)(2,1)}, u32[]{:S(2)}) copy-start(bf16[192,2048]{1,0:T(8,128)(2,1)} %get-tuple-element.18) | copy-start | bytes 2359300
Sparse Core Ops, SparseCore 0:
  11.2 146.0 all-gather.2
  160.0 61.3 all-gather.4
  224.8 56.7 reduce-scatter.3
  284.9 56.1 reduce-scatter.5
  344.8 137.3 reduce-scatter.7

commit v2 on v1

v2 whole, which is shorter than its diff:
```python
import functools

import jax
import jax.numpy as jnp
from jax import lax
from jax.experimental import pallas as pl
from jax.experimental.pallas import tpu as pltpu
from jax.sharding import Mesh, PartitionSpec as P


CAP = 12
AXES = ("zh", "y", "c", "x", "a", "b")
SPLIT = (2, 4, 2, 4, 4, 4)
BF16 = jnp.bfloat16
F32 = jnp.float32


def dot(a, b, ca=1, cb=0):
    return lax.dot_general(a, b, (((ca,), (cb,)), ((), ())), preferred_element_type=F32)


def slot_onehot(ids, near, halves, me):
    tokens = ids.shape[1]
    experts = near * halves
    hot = (lax.broadcasted_iota(jnp.int32, (experts, tokens), 0) == ids).astype(F32)
    before = (
        lax.broadcasted_iota(jnp.int32, (tokens, tokens), 0)
        < lax.broadcasted_iota(jnp.int32, (tokens, tokens), 1)
    ).astype(BF16)
    counts = dot(hot.astype(BF16), before)
    rank = jnp.sum(hot * counts, axis=0, keepdims=True).astype(jnp.int32)
    half = sum((ids >= near * k).astype(jnp.int32) for k in range(1, halves))
    owner = ids - near * half
    hops = jnp.where(owner >= me, owner - me, owner - me + near)
    slot = hops * (halves * CAP) + half * CAP + rank
    return lax.broadcasted_iota(jnp.int32, (experts * CAP, tokens), 0) == slot


def token_weights(ints):
    ints = ints.astype(F32)
    return ints[0:1] / jnp.sum(ints, axis=0, keepdims=True)


def dispatch_kernel(near, halves, at_ref, ids_ref, ints_ref, tok_ref, grad_ref, *outs):
    hot = slot_onehot(ids_ref[...], near, halves, at_ref[5])
    pick = hot.astype(BF16)
    rows = dot(pick, tok_ref[...]).astype(BF16)
    scale = jnp.sum(jnp.where(hot, token_weights(ints_ref[...]), 0.0), axis=1, keepdims=True)
    grads = (scale * dot(pick, grad_ref[...])).astype(BF16)
    size = halves * CAP
    for k, out_ref in enumerate(outs):
        out_ref[0] = rows[k * size : (k + 1) * size]
        out_ref[1] = grads[k * size : (k + 1) * size]


def combine_kernel(near, halves, at_ref, ids_ref, ints_ref, *refs):
    blocks, (out_ref, din_ref) = refs[:near], refs[near:]
    hot = slot_onehot(ids_ref[...], near, halves, at_ref[5])
    pick = hot.astype(BF16)
    tokens = pick.shape[1]
    eye = lax.broadcasted_iota(jnp.int32, (tokens, tokens), 0) == lax.broadcasted_iota(
        jnp.int32, (tokens, tokens), 1
    )
    scale = jnp.sum(jnp.where(eye, token_weights(ints_ref[...]), 0.0), axis=1, keepdims=True)
    rows = jnp.concatenate([ref[0] for ref in blocks], axis=0)
    grads = jnp.concatenate([ref[1] for ref in blocks], axis=0)
    out_ref[...] = (scale * dot(pick, rows, 0, 0)).astype(BF16)
    din_ref[...] = dot(pick, grads, 0, 0).astype(BF16)


def pieces_kernel(at_ref, gate_ref, up_ref, down_ref, pair_ref, last_ref):
    rows = gate_ref.shape[0]
    lanes = down_ref.shape[1]
    shift = lax.rem(at_ref[0], lanes // rows) * rows
    pick = (
        lax.broadcasted_iota(jnp.int32, (rows, lanes), 1)
        == lax.broadcasted_iota(jnp.int32, (rows, lanes), 0) + shift
    ).astype(BF16)
    pair_ref[0] = gate_ref[...]
    pair_ref[1] = up_ref[...]
    last_ref[0] = dot(pick, down_ref[...], 1, 1).astype(BF16)


def row_mask(half, count, halves, width):
    at = lax.broadcasted_iota(jnp.int32, (count, width), 0)
    return lax.div(lax.rem(at, halves * CAP), CAP) == half


def activations(gate, up, keep):
    sig = jax.nn.sigmoid(gate)
    silu = gate * sig
    return jnp.where(keep, silu * up, jnp.zeros_like(gate)).astype(BF16), sig, silu


def input_grads(gate, up, sig, silu, dh, keep):
    zero = jnp.zeros_like(gate)
    dgate = jnp.where(keep, dh * up * sig * (1.0 + gate * (1.0 - sig)), zero).astype(BF16)
    dup = jnp.where(keep, dh * silu, zero).astype(BF16)
    return dgate, dup


def columns(start, size):
    return pl.ds(pl.multiple_of(start, 128), size)


def emit_partials(grads_ref, hidden, x, own_ref, sends):
    parts = len(sends) + 1
    size = grads_ref.shape[1] // parts
    for k in range(parts):
        at = lax.rem(x + k, parts) * size
        part = dot(grads_ref[:, columns(at, size)], hidden, 0, 0)
        if k == 0:
            own_ref[...] = part
        else:
            sends[k - 1][...] = part.astype(BF16)


def near_kernel(halves, near, at_ref, wg_ref, wu_ref, wd_ref, *refs):
    blocks, (rows_ref, grads_ref, out_ref, dx_ref, own_ref) = refs[:near], refs[near : near + 5]
    sends = refs[near + 5 :]
    size = blocks[0].shape[1]
    for k, ref in enumerate(blocks):
        rows_ref[k * size : (k + 1) * size] = ref[0]
        grads_ref[k * size : (k + 1) * size] = ref[1]
    rows, grads = rows_ref[...], grads_ref[...]
    keep = row_mask(at_ref[0], rows.shape[0], halves, wg_ref.shape[1])
    gate, up = dot(rows, wg_ref[...]), dot(rows, wu_ref[...])
    hidden, sig, silu = activations(gate, up, keep)
    emit_partials(grads_ref, hidden, at_ref[1], own_ref, sends)
    dgate, dup = input_grads(gate, up, sig, silu, dot(grads, wd_ref[...], 1, 1), keep)
    out_ref[...] = dot(hidden, wd_ref[...]).astype(BF16)
    dx_ref[...] = (dot(dgate, wg_ref[...], 1, 1) + dot(dup, wu_ref[...], 1, 1)).astype(BF16)


def far_blocks(x, parts, size, refs):
    own, left, right, low, high = refs
    half = size // 2
    across = lax.rem(x + 2, parts) * size
    return (
        (x * size, own, size),
        (lax.rem(x + parts - 1, parts) * size, left, size),
        (lax.rem(x + 1, parts) * size, right, size),
        (across, low, half),
        (across + half, high, half),
    )


def far_first_kernel(halves, at_ref, rows_ref, grads_ref, *refs):
    weights, (gate_ref, up_ref, hidden_ref, own_ref), sends = refs[:5], refs[5:9], refs[9:]
    parts = len(sends) + 1
    size = rows_ref.shape[1] // parts
    gate = up = None
    for start, ref, count in far_blocks(at_ref[1], parts, size, weights):
        part = rows_ref[:, columns(start, count)]
        g, u = dot(part, ref[0]), dot(part, ref[1])
        gate, up = (g, u) if gate is None else (gate + g, up + u)
    keep = row_mask(1 - at_ref[0], rows_ref.shape[0], halves, gate.shape[1])
    hidden, _, _ = activations(gate, up, keep)
    gate_ref[...], up_ref[...], hidden_ref[...] = gate, up, hidden
    emit_partials(grads_ref, hidden, at_ref[1], own_ref, sends)


def far_last_kernel(halves, parts, at_ref, grads_ref, gate_ref, up_ref, hidden_ref, o_ref, d_ref, *refs):
    pairs, downs, outs = refs[:5], refs[5:10], refs[10:]
    size = grads_ref.shape[1] // parts
    x = at_ref[1]
    dh = None
    for start, ref, count in far_blocks(x, parts, size, downs):
        part = dot(grads_ref[:, columns(start, count)], ref[0])
        dh = part if dh is None else dh + part
    gate, up = gate_ref[...], up_ref[...]
    keep = row_mask(1 - at_ref[0], gate.shape[0], halves, gate.shape[1])
    _, sig, silu = activations(gate, up, keep)
    dgate, dup = input_grads(gate, up, sig, silu, dh, keep)
    hidden = hidden_ref[...]
    rows = outs[0].shape[1]
    for (start, down, count), (_, pair, _) in zip(
        far_blocks(x, parts, size, downs), far_blocks(x, parts, size, pairs)
    ):
        cols = columns(start, count)
        out = dot(hidden, down[0], 1, 1).astype(BF16) + o_ref[:, cols]
        dx = dot(dgate, pair[0], 1, 1) + dot(dup, pair[1], 1, 1)
        dx = dx.astype(BF16) + d_ref[:, cols]
        for k, out_ref in enumerate(outs):
            out_ref[0, :, cols] = out[k * rows : (k + 1) * rows]
            out_ref[1, :, cols] = dx[k * rows : (k + 1) * rows]


def order_kernel(quads, at_ref, *refs):
    ins, out_ref = refs[:-1], refs[-1]
    a, b = at_ref[2], at_ref[3]
    near = len(ins)
    depth = ins[0].shape[2]
    for j, ref in enumerate(ins):
        for i in range(quads):
            a_from = lax.rem(a + quads - i, quads)
            b_from = lax.rem(b + near - j, near)
            start = pl.multiple_of((a_from * near + b_from) * depth, depth)
            for k in range(out_ref.shape[0]):
                out_ref[k, pl.ds(start, depth), :] = ref[i, k]


def sum_x_kernel(quads, count, at_ref, *refs):
    near_in, far_in = refs[:count], refs[count : 2 * count]
    own_ref, sends = refs[2 * count], refs[2 * count + 1 :]
    near_count = len(sends) + 1
    depth = own_ref.shape[2]
    half, b = at_ref[0], at_ref[3]
    for group, where in ((near_in, half), (far_in, 1 - half)):
        for j in range(near_count):
            for a in range(quads):
                owner = lax.rem(b + j, near_count)
                at = pl.ds(pl.multiple_of((a * near_count + owner) * depth, depth), depth)
                total = group[0][at, :]
                for ref in group[1:]:
                    total = total + ref[at, :].astype(F32)
                if j == 0:
                    own_ref[where, a] = total
                else:
                    sends[j - 1][where, a] = total.astype(BF16)


def sum_b_kernel(at_ref, *refs):
    count = refs[0].shape[0]
    ins = [ref for ref in refs if ref.shape[0] == count and len(ref.shape) == 3]
    own_ref, sends = refs[len(ins)], refs[len(ins) + 1 :]
    me = at_ref[4]
    for k in range(count):
        to = lax.rem(me + k, count)
        total = ins[0][to]
        for ref in ins[1:]:
            total = total + ref[to].astype(F32)
        if k == 0:
            own_ref[...] = total
        else:
            sends[k - 1][...] = total.astype(BF16)


def sum_last_kernel(*refs):
    total = refs[0][...]
    for ref in refs[1:-1]:
        total = total + ref[...].astype(F32)
    refs[-1][...] = total


def call(kernel, outs, *args, scalar=True, flops=0):
    return raw_call(kernel, outs, *args, scalar=scalar, flops=flops)


def raw_call(kernel, outs, *args, scalar=True, flops=0):
    vmem = pl.BlockSpec(memory_space=pltpu.VMEM)
    smem = pl.BlockSpec(memory_space=pltpu.SMEM)
    size = sum(a.size * a.dtype.itemsize for a in (*args, *outs))
    return pl.pallas_call(
        kernel,
        out_shape=outs,
        in_specs=[smem if scalar and k == 0 else vmem for k in range(len(args))],
        out_specs=tuple(vmem for _ in outs),
        compiler_params=pltpu.CompilerParams(vmem_limit_bytes=60 << 20),
        cost_estimate=pl.CostEstimate(flops=flops, bytes_accessed=size, transcendentals=0),
    )(*args)


def shape(*dims, dtype=BF16):
    return jax.ShapeDtypeStruct(dims, dtype)


def step(tokens, out_grad, expert_ids, combine_ints, w_gate, w_up, w_down):
    count, width = tokens.shape
    inner = w_gate.shape[2]
    halves, quads, nb, nx = (lax.axis_size(name) for name in ("zh", "a", "b", "x"))
    near = lax.axis_size("y") * lax.axis_size("c")
    depth = width // (nx * quads * nb)
    slots = near * halves * CAP
    zh, x, a, b = (lax.axis_index(name).astype(jnp.int32) for name in ("zh", "x", "a", "b"))
    owner = lax.axis_index(("y", "c")).astype(jnp.int32)
    at = jnp.stack([zh, x, a, b, zh * quads + a, owner])
    shard = ((x * quads + a) * nb + b).reshape(1)
    w_gate, w_up, w_down = w_gate[0], w_up[0], w_down[0]

    per = 128 // depth
    pair, last = pl.pallas_call(
        pieces_kernel,
        grid_spec=pltpu.PrefetchScalarGridSpec(
            num_scalar_prefetch=1,
            grid=(1,),
            in_specs=[
                pl.BlockSpec((depth, inner), lambda i, s: (s[0], 0)),
                pl.BlockSpec((depth, inner), lambda i, s: (s[0], 0)),
                pl.BlockSpec((inner, 128), lambda i, s: (0, lax.div(s[0], per))),
            ],
            out_specs=[
                pl.BlockSpec((2, depth, inner), lambda i, s: (0, 0, 0)),
                pl.BlockSpec((1, depth, inner), lambda i, s: (0, 0, 0)),
            ],
        ),
        out_shape=(shape(2, depth, inner), shape(1, depth, inner)),
    )(shard, w_gate, w_up, w_down)

    def cross(v):
        pairs = [
            [
                (h * quads + i, (1 - h) * quads + (i + k) % quads)
                for h in range(halves)
                for i in range(quads)
            ]
            for k in range(quads)
        ]
        parts = []
        for p in pairs:
            parts.append(lax.ppermute(v, ("zh", "a"), p))
        return jnp.stack(parts)

    def shift(v, name, size, k):
        return lax.ppermute(v, name, [(i, (i + k) % size) for i in range(size)])

    def spread(v):
        m = v.shape[1]
        ins = [v] + [shift(v, "b", nb, k) for k in range(1, nb)]
        return call(
            functools.partial(order_kernel, quads),
            (shape(m, width // nx, inner),), at, *ins,
        )[0]

    def around(v):
        half = v.shape[1] // 2
        left = shift(v, "x", nx, 1)
        right = shift(v, "x", nx, nx - 1)
        low = shift(left[:, :half], "x", nx, 1)
        high = shift(right[:, half:], "x", nx, nx - 1)
        return v, left, right, low, high

    spread_pair = spread(cross(pair))
    last, spread_pair = lax.optimization_barrier((last, spread_pair))
    pairs = around(spread_pair)
    downs = around(spread(cross(last)))

    ids = expert_ids.reshape(1, count)
    ints = combine_ints.T
    packet = (shape(2, halves * CAP, width),) * near
    sends = call(
        functools.partial(dispatch_kernel, near, halves),
        packet, at, ids, ints, tokens, out_grad, flops=4 * slots * count * width,
    )
    both = ("y", "c")
    blocks = [shift(v, both, near, k) if k else v for k, v in enumerate(sends)]
    work = 2 * slots * width * inner
    block = width // nx
    partial_shapes = (shape(block, inner, dtype=F32),) + (shape(block, inner),) * (nx - 1)

    def over_x(own, *sends):
        return (own,) + tuple(shift(v, "x", nx, k + 1) for k, v in enumerate(sends))

    rows, grads, near_out, near_dx, *near_parts = call(
        functools.partial(near_kernel, halves, near),
        (shape(slots, width),) * 4 + partial_shapes,
        at, w_gate, w_up, w_down, *blocks, flops=7 * work,
    )
    near_sums = over_x(*near_parts)
    gate, up, hidden, *far_parts = call(
        functools.partial(far_first_kernel, halves),
        (shape(slots, inner, dtype=F32),) * 2 + (shape(slots, inner),) + partial_shapes,
        at, rows, grads, *pairs, flops=3 * work,
    )
    far_sums = over_x(*far_parts)
    results = call(
        functools.partial(far_last_kernel, halves, nx),
        packet,
        at, grads, gate, up, hidden, near_out, near_dx, *pairs, *downs, flops=4 * work,
    )

    own, *sends = call(
        functools.partial(sum_x_kernel, quads, nx),
        (shape(halves, quads, depth, inner, dtype=F32),)
        + (shape(halves, quads, depth, inner),) * (nb - 1),
        at, *near_sums, *far_sums,
    )
    far = halves * quads
    received = [shift(v, "b", nb, k + 1) for k, v in enumerate(sends)]
    own, *sends = call(
        sum_b_kernel,
        (shape(depth, inner, dtype=F32),) + (shape(depth, inner),) * (far - 1),
        at, *(v.reshape(far, depth, inner) for v in (own, *received)),
    )
    received = [shift(v, ("zh", "a"), far, k + 1) for k, v in enumerate(sends)]
    grad = call(sum_last_kernel, (shape(depth, inner, dtype=F32),), own, *received, scalar=False)[0]

    returned = [shift(v, both, near, near - k) if k else v for k, v in enumerate(results)]
    combined, dinput = call(
        functools.partial(combine_kernel, near, halves),
        (shape(count, width),) * 2, at, ids, ints, *returned,
        flops=4 * slots * count * width,
    )
    return combined, dinput, grad.T[None]


def build(mesh, split):
    fine = Mesh(mesh.devices.reshape(split), AXES)
    token = P(AXES, None)
    expert = P(("zh", "y", "c"), None, None)
    return jax.shard_map(
        step,
        mesh=fine,
        in_specs=(token, token, token, token, expert, expert, expert),
        out_specs=(token, token, P(("zh", "y", "c"), None, ("x", "a", "b"))),
        check_vma=False,
    )


def solution(mesh):
    return build(mesh, SPLIT)
```

time: 489 us -> 377 us (0.77)
  waiting for transfers between devices: 380 us -> 69.5 us
  starting transfers between devices: 0.21 us -> 259 us
  blocking collectives: 64.4 us -> 0 us
  Pallas kernels: 24.3 us -> 37.9 us
  between operations: 13.8 us -> 1.85 us
    ppermute x0 -> x52, starting transfers between devices: none -> 259 us  [the longest x44 162 us: shift(): return lax.ppermute(v, name, [(i, (i + k) % size) for i in range(size)])]
    reduce_scatter x3 -> x0, waiting for transfers between devices: 213 us -> none  [the longest x2 111 us: over_x(): return lax.psum_scatter(v, 'x', scatter_dimension=0, tiled=True)]
    all_gather x2 -> x0, waiting for transfers between devices: 166 us -> none  [the longest x1 148 us: body(): lax.all_gather(piece.reshape(3 * depth, hidden_width), ('zh', 'zl'), axis...]
    ppermute x0 -> x52, waiting for transfers between devices: none -> 69.5 us  [the longest x8 44.4 us: cross(): parts.append(lax.ppermute(v, ('zh', 'a'), p))]
    all_to_all x4 -> x0, blocking collectives: 64.4 us -> none  [swap(): lax.all_to_all(v, ('y', 'c'), split_axis=0, concat_axis=0, tiled=True)]
    pallas_call x5 -> x11, Pallas kernels: 24.3 us -> 37.9 us  [the longest x10 36.2 us: raw_call(): pl.pallas_call(kernel, out_shape=outs, in_specs=[smem if scalar and k ==...]
  transfers between devices with their start and end apart: 5 -> 52, of which waited for: 5 -> 15; matrix products, arithmetic and copies ran while one was open for 0% -> 0% of each run, Pallas kernels for 5% -> 9%
where the time goes in v2:
time: 377 us; the launch traced here: 373 us
  starting transfers between devices  259 us (69%)
  waiting for transfers between devices  69.5 us (18%)
  Pallas kernels  37.9 us (10%)
  local copies, waits for them, and re-layouts  4.88 us (1%)
    ppermute x44, starting transfers between devices, shift(): return lax.ppermute(v, name, [(i, (i + k) % size) for i in range(size)])  162 us
    ppermute x8, starting transfers between devices, cross(): parts.append(lax.ppermute(v, ('zh', 'a'), p))  96.6 us
    ppermute x8, waiting for transfers between devices, cross(): parts.append(lax.ppermute(v, ('zh', 'a'), p))  44.4 us
    pallas_call x10, Pallas kernels, raw_call(): pl.pallas_call(kernel, out_shape=outs, in_specs=[smem if scalar and k ==...  36.2 us
    ppermute x44, waiting for transfers between devices, shift(): return lax.ppermute(v, name, [(i, (i + k) % size) for i in range(size)])  25.1 us
  transfers between devices with their start and end apart: 52, of which 15 were waited for; matrix products, arithmetic and copies ran while one was open for 0% of the time, Pallas kernels for 9%

profile of v2, /device:TPU:24, one launch (start us, length us, event | category | flops | bytes accessed | tf_op | source)
XLA Modules:
  0.0 373.2 jit_solution(9036333304124181164)
XLA Ops:
  2.3 29.1 %collective-permute-start.7 = (bf16[2,32,384]{2,1,0:T(8,128)(2,1)}, bf16[2,32,384]{2,1,0:T(8,128)(2,1)S(1)}, u32[]{:S(2)}, u32[]{:S(2)}) collective-permute-start(bf16[2,32,384]{2,1,0:T(8,128)(2,1)} %get-tuple-element.63), channel_id=1, source_target_pairs={{0,512},{4,516},{8,520},{12,524},{512,0},{516,4},{520,8},{524,12},... | collective-permute-start | bytes 147464 | tf_op jit(solution)/shard_map/ppermute | solution.py:311
  33.4 13.3 %collective-permute-start.9 = (bf16[2,32,384]{2,1,0:T(8,128)(2,1)}, bf16[2,32,384]{2,1,0:T(8,128)(2,1)S(1)}, u32[]{:S(2)}, u32[]{:S(2)}) collective-permute-start(bf16[2,32,384]{2,1,0:T(8,128)(2,1)} %get-tuple-element.63), channel_id=1, source_target_pairs={{0,520},{4,524},{8,512},{12,516},{512,8},{516,12},{520,0},{524,4},... | collective-permute-start | bytes 147464 | tf_op jit(solution)/shard_map/ppermute | solution.py:311
  48.6 15.6 %collective-permute-done.8 = bf16[2,32,384]{2,1,0:T(8,128)(2,1)S(1)} collective-permute-done((bf16[2,32,384]{2,1,0:T(8,128)(2,1)}, bf16[2,32,384]{2,1,0:T(8,128)(2,1)S(1)}, u32[]{:S(2)}, u32[]{:S(2)}) %collective-permute-start.8) | collective-permute-done | bytes 49184 | tf_op jit(solution)/shard_map/ppermute | solution.py:311
  67.6 2.7 collective-permute-start.11
  70.3 3.8 %collective-permute-start.12 = (bf16[4,2,32,384]{3,2,1,0:T(8,128)(2,1)S(1)}, bf16[4,2,32,384]{3,2,1,0:T(8,128)(2,1)S(1)}, u32[]{:S(2)}, u32[]{:S(2)}) collective-permute-start(bf16[4,2,32,384]{3,2,1,0:T(8,128)(2,1)S(1)} %pad_maximum_fusion.refs_0_), channel_id=1, source_target_pairs={{0,2},{1,3},{2,0},{3,1},{4,6},{5,7},{6,4},{7,5},{8,10},{9,11},{10,... | collective-permute-start | bytes 589832 | tf_op jit(solution)/shard_map/ppermute | solution.py:315
  74.1 3.1 collective-permute-start.13
  79.2 6.1 %collective-permute-done.12.refs_2_ = bf16[4,2,32,384]{3,2,1,0:T(8,128)(2,1)S(1)} collective-permute-done((bf16[4,2,32,384]{3,2,1,0:T(8,128)(2,1)S(1)}, bf16[4,2,32,384]{3,2,1,0:T(8,128)(2,1)S(1)}, u32[]{:S(2)}, u32[]{:S(2)}) %collective-permute-start.12) | collective-permute-done | bytes 196640 | tf_op jit(solution)/shard_map/ppermute | solution.py:315
  89.2 3.4 collective-permute-start.14
  92.5 3.7 collective-permute-start.15
  96.2 12.1 %collective-permute-start.18 = (bf16[1,32,384]{2,1,0:T(8,128)(2,1)S(1)}, bf16[1,32,384]{2,1,0:T(8,128)(2,1)S(1)}, u32[]{:S(2)}, u32[]{:S(2)}) collective-permute-start(bf16[1,32,384]{2,1,0:T(8,128)(2,1)S(1)} %copy-done.47), channel_id=1, source_target_pairs={{0,512},{4,516},{8,520},{12,524},{512,0},{516,4},{520,8},{524,12},... | collective-permute-start | bytes 73736 | tf_op jit(solution)/shard_map/ppermute | solution.py:311
  108.4 3.0 shard_map.94
  113.5 6.7 %collective-permute-done.18 = bf16[1,32,384]{2,1,0:T(8,128)(2,1)S(1)} collective-permute-done((bf16[1,32,384]{2,1,0:T(8,128)(2,1)S(1)}, bf16[1,32,384]{2,1,0:T(8,128)(2,1)S(1)}, u32[]{:S(2)}, u32[]{:S(2)}) %collective-permute-start.18) | collective-permute-done | bytes 24608 | tf_op jit(solution)/shard_map/ppermute | solution.py:311
  120.3 15.8 %collective-permute-start.19 = (bf16[1,32,384]{2,1,0:T(8,128)(2,1)S(1)}, bf16[1,32,384]{2,1,0:T(8,128)(2,1)S(1)}, u32[]{:S(2)}, u32[]{:S(2)}) collective-permute-start(bf16[1,32,384]{2,1,0:T(8,128)(2,1)S(1)} %copy-done.47), channel_id=1, source_target_pairs={{0,516},{4,520},{8,524},{12,512},{512,4},{516,8},{520,12},{524,0},... | collective-permute-start | bytes 73736 | tf_op jit(solution)/shard_map/ppermute | solution.py:311
  137.6 18.5 %collective-permute-start.20 = (bf16[1,32,384]{2,1,0:T(8,128)(2,1)S(1)}, bf16[1,32,384]{2,1,0:T(8,128)(2,1)S(1)}, u32[]{:S(2)}, u32[]{:S(2)}) collective-permute-start(bf16[1,32,384]{2,1,0:T(8,128)(2,1)S(1)} %copy-done.47), channel_id=1, source_target_pairs={{0,520},{4,524},{8,512},{12,516},{512,8},{516,12},{520,0},{524,4},... | collective-permute-start | bytes 73736 | tf_op jit(solution)/shard_map/ppermute | solution.py:311
  158.0 3.9 %collective-permute-start.21 = (bf16[1,32,384]{2,1,0:T(8,128)(2,1)S(1)}, bf16[1,32,384]{2,1,0:T(8,128)(2,1)S(1)}, u32[]{:S(2)}, u32[]{:S(2)}) collective-permute-start(bf16[1,32,384]{2,1,0:T(8,128)(2,1)S(1)} %copy-done.47), channel_id=1, source_target_pairs={{0,524},{4,512},{8,516},{12,520},{512,12},{516,0},{520,4},{524,8},... | collective-permute-start | bytes 73736 | tf_op jit(solution)/shard_map/ppermute | solution.py:311
  161.9 15.3 %collective-permute-done.21 = bf16[1,32,384]{2,1,0:T(8,128)(2,1)S(1)} collective-permute-done((bf16[1,32,384]{2,1,0:T(8,128)(2,1)S(1)}, bf16[1,32,384]{2,1,0:T(8,128)(2,1)S(1)}, u32[]{:S(2)}, u32[]{:S(2)}) %collective-permute-start.21) | collective-permute-done | bytes 24608 | tf_op jit(solution)/shard_map/ppermute | solution.py:311
  177.2 4.7 %collective-permute-start.22 = (bf16[4,1,32,384]{3,2,1,0:T(8,128)(2,1)S(1)}, bf16[4,1,32,384]{3,2,1,0:T(8,128)(2,1)S(1)}, u32[]{:S(2)}, u32[]{:S(2)}) collective-permute-start(bf16[4,1,32,384]{3,2,1,0:T(8,128)(2,1)S(1)} %pad_maximum_fusion.1.refs_0_), channel_id=1, source_target_pairs={{0,1},{1,2},{2,3},{3,0},{4,5},{5,6},{6,7},{7,4},{8,9},{9,10},{10,1... | collective-permute-start | bytes 294920 | tf_op jit(solution)/shard_map/ppermute | solution.py:315
  182.0 2.8 collective-permute-start.23
  184.7 3.9 %collective-permute-start.24 = (bf16[4,1,32,384]{3,2,1,0:T(8,128)(2,1)S(1)}, bf16[4,1,32,384]{3,2,1,0:T(8,128)(2,1)S(1)}, u32[]{:S(2)}, u32[]{:S(2)}) collective-permute-start(bf16[4,1,32,384]{3,2,1,0:T(8,128)(2,1)S(1)} %pad_maximum_fusion.1.refs_0_), channel_id=1, source_target_pairs={{0,3},{1,0},{2,1},{3,2},{4,7},{5,4},{6,5},{7,6},{8,11},{9,8},{10,9... | collective-permute-start | bytes 294920 | tf_op jit(solution)/shard_map/ppermute | solution.py:315
  190.6 3.5 collective-permute-start.3
  194.2 4.9 %collective-permute-start.4 = (bf16[2,24,2048]{2,1,0:T(8,128)(2,1)}, bf16[2,24,2048]{2,1,0:T(8,128)(2,1)}, u32[]{:S(2)}, u32[]{:S(2)}) collective-permute-start(bf16[2,24,2048]{2,1,0:T(8,128)(2,1)} %get-tuple-element.57), channel_id=1, source_target_pairs={{0,320},{64,384},{128,448},{192,0},{256,64},{320,128},{384,192},{4... | collective-permute-start | bytes 589832 | tf_op jit(solution)/shard_map/ppermute | solution.py:315
  206.6 4.9 %collective-permute-start.26 = (bf16[1,512,384]{2,1,0:T(8,128)(2,1)S(1)}, bf16[1,512,384]{2,1,0:T(8,128)(2,1)S(1)}, u32[]{:S(2)}, u32[]{:S(2)}) collective-permute-start(bf16[1,512,384]{2,1,0:T(8,128)(2,1)S(1)} %copy-done.4), channel_id=1, source_target_pairs={{0,48},{16,0},{32,16},{48,32},{1,49},{17,1},{33,17},{49,33},{2,50}... | collective-permute-start | bytes 1179656 | tf_op jit(solution)/shard_map/ppermute | solution.py:315
  213.4 5.1 %collective-permute-start.17 = (bf16[2,256,384]{2,1,0:T(8,128)(2,1)S(1)}, bf16[2,256,384]{2,1,0:T(8,128)(2,1)S(1)}, u32[]{:S(2)}, u32[]{:S(2)}) collective-permute-start(bf16[2,256,384]{2,1,0:T(8,128)(2,1)S(1)} %slice.17), channel_id=1, source_target_pairs={{0,48},{16,0},{32,16},{48,32},{1,49},{17,1},{33,17},{49,33},{2,50}... | collective-permute-start | bytes 1179656 | tf_op jit(solution)/shard_map/ppermute | solution.py:315
  218.6 7.7 %shard_map.95 = (bf16[192,2048]{1,0:T(8,128)(2,1)}, bf16[192,2048]{1,0:T(8,128)(2,1)}, bf16[192,2048]{1,0:T(8,128)(2,1)}, bf16[192,2048]{1,0:T(8,128)(2,1)}, f32...) custom-call(s32[6]{0:T(128)} %stack.57.at_ref, ...), custom_call_target="tpu_custom_call" | custom-call | flops 2113929216 | bytes 11403288 | tf_op jit(solution)/shard_map/pallas_call | solution.py:254
  230.3 5.1 %collective-permute-start.28 = (bf16[1,256,384]{2,1,0:T(8,128)(2,1)S(1)}, bf16[1,256,384]{2,1,0:T(8,128)(2,1)}, u32[]{:S(2)}, u32[]{:S(2)}) collective-permute-start(bf16[1,256,384]{2,1,0:T(8,128)(2,1)S(1)} %slice.19), channel_id=1, source_target_pairs={{0,48},{16,0},{32,16},{48,32},{1,49},{17,1},{33,17},{49,33},{2,50}... | collective-permute-start | bytes 589832 | tf_op jit(solution)/shard_map/ppermute | solution.py:315
  235.4 3.4 collective-permute-start.37
  238.8 2.5 collective-permute-start.38
  241.3 4.9 %shard_map.98 = (f32[192,384]{1,0:T(8,128)}, f32[192,384]{1,0:T(8,128)}, bf16[192,384]{1,0:T(8,128)(2,1)}, f32[512,384]{1,0:T(8,128)}, bf16[512,384]{1,0:T(8,128...) custom-call(s32[6]{0:T(128)} %stack.57.at_ref, bf16[192,2048]{1,0:T(8,128)(2,1)} %get-tuple-element.61.rows_ref, ...), custom_call_target="tpu_custom_call" | custom-call | flops 905969664 | bytes 7421976 | tf_op jit(solution)/shard_map/pallas_call | solution.py:254
  246.3 3.4 collective-permute-start.39
  249.7 4.2 %collective-permute-done.27.refs_8_ = bf16[1,256,384]{2,1,0:T(8,128)(2,1)S(1)} collective-permute-done((bf16[1,256,384]{2,1,0:T(8,128)(2,1)S(1)}, bf16[1,256,384]{2,1,0:T(8,128)(2,1)S(1)}, u32[]{:S(2)}, u32[]{:S(2)}) %collective-permute-start.27) | collective-permute-done | bytes 196640 | tf_op jit(solution)/shard_map/ppermute | solution.py:315
  258.3 6.5 %shard_map.100 = (bf16[2,24,2048]{2,1,0:T(8,128)(2,1)}, bf16[2,24,2048]{2,1,0:T(8,128)(2,1)}, bf16[2,24,2048]{2,1,0:T(8,128)(2,1)}, bf16[2,24,2048]{2,1,0:T(8,12...) custom-call(s32[6]{0:T(128)} %stack.57.at_ref, ...), custom_call_target="tpu_custom_call" | custom-call | flops 1207959552 | bytes 9388056 | tf_op jit(solution)/shard_map/pallas_call | solution.py:254
  264.9 3.7 collective-permute-start.30
  269.3 3.8 %collective-permute-done.41.refs_7_ = bf16[512,384]{1,0:T(8,128)(2,1)S(1)} collective-permute-done((bf16[512,384]{1,0:T(8,128)(2,1)}, bf16[512,384]{1,0:T(8,128)(2,1)S(1)}, u32[]{:S(2)}, u32[]{:S(2)}) %collective-permute-start.41) | collective-permute-done | bytes 393248 | tf_op jit(solution)/shard_map/ppermute | solution.py:315
  273.9 3.4 shard_map.102
  279.2 3.5 collective-permute-start.43
  282.7 4.2 %collective-permute-start.44 = (bf16[2,4,32,384]{3,2,1,0:T(8,128)(2,1)}, bf16[2,4,32,384]{3,2,1,0:T(8,128)(2,1)S(1)}, u32[]{:S(2)}, u32[]{:S(2)}) collective-permute-start(bf16[2,4,32,384]{3,2,1,0:T(8,128)(2,1)} %get-tuple-element.92), channel_id=1, source_target_pairs={{0,3},{1,0},{2,1},{3,2},{4,7},{5,4},{6,5},{7,6},{8,11},{9,8},{10,9... | collective-permute-start | bytes 589832 | tf_op jit(solution)/shard_map/ppermute | solution.py:315
  286.9 3.1 collective-permute-start.31
  290.0 3.7 collective-permute-start.32
  293.7 4.0 %collective-permute-start.33 = (bf16[2,24,2048]{2,1,0:T(8,128)(2,1)S(1)}, bf16[2,24,2048]{2,1,0:T(8,128)(2,1)S(1)}, u32[]{:S(2)}, u32[]{:S(2)}) collective-permute-start(bf16[2,24,2048]{2,1,0:T(8,128)(2,1)S(1)} %copy-done.41), channel_id=1, source_target_pairs={{0,192},{64,256},{128,320},{192,384},{256,448},{320,0},{384,64},{4... | collective-permute-start | bytes 589832 | tf_op jit(solution)/shard_map/ppermute | solution.py:315
  297.8 3.1 collective-permute-start.34
  303.4 2.8 collective-permute-start.45
  306.3 11.5 %collective-permute-start.46 = (bf16[32,384]{1,0:T(8,128)(2,1)}, bf16[32,384]{1,0:T(8,128)(2,1)S(1)}, u32[]{:S(2)}, u32[]{:S(2)}) collective-permute-start(bf16[32,384]{1,0:T(8,128)(2,1)} %get-tuple-element.95), channel_id=1, source_target_pairs={{0,8},{4,12},{8,512},{12,516},{512,520},{516,524},{520,0},{524,4},... | collective-permute-start | bytes 73736 | tf_op jit(solution)/shard_map/ppermute | solution.py:315
  317.8 13.6 %collective-permute-start.47 = (bf16[32,384]{1,0:T(8,128)(2,1)}, bf16[32,384]{1,0:T(8,128)(2,1)S(1)}, u32[]{:S(2)}, u32[]{:S(2)}) collective-permute-start(bf16[32,384]{1,0:T(8,128)(2,1)} %get-tuple-element.96), channel_id=1, source_target_pairs={{0,12},{4,512},{8,516},{12,520},{512,524},{516,0},{520,4},{524,8},... | collective-permute-start | bytes 73736 | tf_op jit(solution)/shard_map/ppermute | solution.py:315
  331.4 11.2 %collective-permute-start.48 = (bf16[32,384]{1,0:T(8,128)(2,1)}, bf16[32,384]{1,0:T(8,128)(2,1)S(1)}, u32[]{:S(2)}, u32[]{:S(2)}) collective-permute-start(bf16[32,384]{1,0:T(8,128)(2,1)} %get-tuple-element.97), channel_id=1, source_target_pairs={{0,512},{4,516},{8,520},{12,524},{512,0},{516,4},{520,8},{524,12},... | collective-permute-start | bytes 73736 | tf_op jit(solution)/shard_map/ppermute | solution.py:315
  342.6 7.7 %collective-permute-start.49 = (bf16[32,384]{1,0:T(8,128)(2,1)}, bf16[32,384]{1,0:T(8,128)(2,1)S(1)}, u32[]{:S(2)}, u32[]{:S(2)}) collective-permute-start(bf16[32,384]{1,0:T(8,128)(2,1)} %get-tuple-element.98), channel_id=1, source_target_pairs={{0,516},{4,520},{8,524},{12,0},{512,4},{516,8},{520,12},{524,512},... | collective-permute-start | bytes 73736 | tf_op jit(solution)/shard_map/ppermute | solution.py:315
  350.3 7.4 %collective-permute-start.50 = (bf16[32,384]{1,0:T(8,128)(2,1)}, bf16[32,384]{1,0:T(8,128)(2,1)S(1)}, u32[]{:S(2)}, u32[]{:S(2)}) collective-permute-start(bf16[32,384]{1,0:T(8,128)(2,1)} %get-tuple-element.99), channel_id=1, source_target_pairs={{0,520},{4,524},{8,0},{12,4},{512,8},{516,12},{520,512},{524,516},... | collective-permute-start | bytes 73736 | tf_op jit(solution)/shard_map/ppermute | solution.py:315
  360.1 2.9 shard_map.101
  363.1 5.7 %collective-permute-done.49.refs_5_ = bf16[32,384]{1,0:T(8,128)(2,1)S(1)} collective-permute-done((bf16[32,384]{1,0:T(8,128)(2,1)}, bf16[32,384]{1,0:T(8,128)(2,1)S(1)}, u32[]{:S(2)}, u32[]{:S(2)}) %collective-permute-start.49) | collective-permute-done | bytes 24608 | tf_op jit(solution)/shard_map/ppermute | solution.py:315
  (170 shorter events, 52.9 us)
Async XLA Ops:
  2.3 46.3 %collective-permute-start.7 = (bf16[2,32,384]{2,1,0:T(8,128)(2,1)}, bf16[2,32,384]{2,1,0:T(8,128)(2,1)S(1)}, u32[]{:S(2)}, u32[]{:S(2)}) collective-permute-start(bf16[2,32,384]{2,1,0:T(8,128)(2,1)} %get-tuple-element.63), channel_id=1, source_target_pairs={{0,512},{4,516},{8,520},{12,524},{512,0},{516,4},{520,8},{524,12},... | collective-permute-start | bytes 147464 | tf_op jit(solution)/shard_map/ppermute | solution.py:311
  31.4 32.7 %collective-permute-start.8 = (bf16[2,32,384]{2,1,0:T(8,128)(2,1)}, bf16[2,32,384]{2,1,0:T(8,128)(2,1)S(1)}, u32[]{:S(2)}, u32[]{:S(2)}) collective-permute-start(bf16[2,32,384]{2,1,0:T(8,128)(2,1)} %get-tuple-element.63), channel_id=1, source_target_pairs={{0,516},{4,520},{8,524},{12,512},{512,4},{516,8},{520,12},{524,0},... | collective-permute-start | bytes 147464 | tf_op jit(solution)/shard_map/ppermute | solution.py:311
  33.4 31.9 %collective-permute-start.9 = (bf16[2,32,384]{2,1,0:T(8,128)(2,1)}, bf16[2,32,384]{2,1,0:T(8,128)(2,1)S(1)}, u32[]{:S(2)}, u32[]{:S(2)}) collective-permute-start(bf16[2,32,384]{2,1,0:T(8,128)(2,1)} %get-tuple-element.63), channel_id=1, source_target_pairs={{0,520},{4,524},{8,512},{12,516},{512,8},{516,12},{520,0},{524,4},... | collective-permute-start | bytes 147464 | tf_op jit(solution)/shard_map/ppermute | solution.py:311
  46.6 20.9 %collective-permute-start.10 = (bf16[2,32,384]{2,1,0:T(8,128)(2,1)}, bf16[2,32,384]{2,1,0:T(8,128)(2,1)S(1)}, u32[]{:S(2)}, u32[]{:S(2)}) collective-permute-start(bf16[2,32,384]{2,1,0:T(8,128)(2,1)} %get-tuple-element.63), channel_id=1, source_target_pairs={{0,524},{4,512},{8,516},{12,520},{512,12},{516,0},{520,4},{524,8},... | collective-permute-start | bytes 147464 | tf_op jit(solution)/shard_map/ppermute | solution.py:311
  70.3 15.0 %collective-permute-start.12 = (bf16[4,2,32,384]{3,2,1,0:T(8,128)(2,1)S(1)}, bf16[4,2,32,384]{3,2,1,0:T(8,128)(2,1)S(1)}, u32[]{:S(2)}, u32[]{:S(2)}) collective-permute-start(bf16[4,2,32,384]{3,2,1,0:T(8,128)(2,1)S(1)} %pad_maximum_fusion.refs_0_), channel_id=1, source_target_pairs={{0,2},{1,3},{2,0},{3,1},{4,6},{5,7},{6,4},{7,5},{8,10},{9,11},{10,... | collective-permute-start | bytes 589832 | tf_op jit(solution)/shard_map/ppermute | solution.py:315
  74.1 12.2 %collective-permute-start.13 = (bf16[4,2,32,384]{3,2,1,0:T(8,128)(2,1)S(1)}, bf16[4,2,32,384]{3,2,1,0:T(8,128)(2,1)S(1)}, u32[]{:S(2)}, u32[]{:S(2)}) collective-permute-start(bf16[4,2,32,384]{3,2,1,0:T(8,128)(2,1)S(1)} %pad_maximum_fusion.refs_0_), channel_id=1, source_target_pairs={{0,3},{1,0},{2,1},{3,2},{4,7},{5,4},{6,5},{7,6},{8,11},{9,8},{10,9... | collective-permute-start | bytes 589832 | tf_op jit(solution)/shard_map/ppermute | solution.py:315
  89.2 109.9 %collective-permute-start.14 = (bf16[2,512,384]{2,1,0:T(8,128)(2,1)}, bf16[2,512,384]{2,1,0:T(8,128)(2,1)S(1)}, u32[]{:S(2)}, u32[]{:S(2)}) collective-permute-start(bf16[2,512,384]{2,1,0:T(8,128)(2,1)} %shard_map.97.refs_0_), channel_id=1, source_target_pairs={{0,16},{16,32},{32,48},{48,0},{1,17},{17,33},{33,49},{49,1},{2,18}... | collective-permute-start | bytes 2359304 | tf_op jit(solution)/shard_map/ppermute | solution.py:315
  92.5 108.5 %collective-permute-start.15 = (bf16[2,512,384]{2,1,0:T(8,128)(2,1)}, bf16[2,512,384]{2,1,0:T(8,128)(2,1)S(1)}, u32[]{:S(2)}, u32[]{:S(2)}) collective-permute-start(bf16[2,512,384]{2,1,0:T(8,128)(2,1)} %shard_map.97.refs_0_), channel_id=1, source_target_pairs={{0,48},{16,0},{32,16},{48,32},{1,49},{17,1},{33,17},{49,33},{2,50}... | collective-permute-start | bytes 2359304 | tf_op jit(solution)/shard_map/ppermute | solution.py:315
  96.2 24.0 %collective-permute-start.18 = (bf16[1,32,384]{2,1,0:T(8,128)(2,1)S(1)}, bf16[1,32,384]{2,1,0:T(8,128)(2,1)S(1)}, u32[]{:S(2)}, u32[]{:S(2)}) collective-permute-start(bf16[1,32,384]{2,1,0:T(8,128)(2,1)S(1)} %copy-done.47), channel_id=1, source_target_pairs={{0,512},{4,516},{8,520},{12,524},{512,0},{516,4},{520,8},{524,12},... | collective-permute-start | bytes 73736 | tf_op jit(solution)/shard_map/ppermute | solution.py:311
  111.4 70.5 %collective-permute-start = (bf16[2,24,2048]{2,1,0:T(8,128)(2,1)}, bf16[2,24,2048]{2,1,0:T(8,128)(2,1)S(1)}, u32[]{:S(2)}, u32[]{:S(2)}) collective-permute-start(bf16[2,24,2048]{2,1,0:T(8,128)(2,1)} %get-tuple-element.53), channel_id=1, source_target_pairs={{0,64},{64,128},{128,192},{192,256},{256,320},{320,384},{384,448},... | collective-permute-start | bytes 589832 | tf_op jit(solution)/shard_map/ppermute | solution.py:315
  111.4 73.3 %collective-permute-start.1 = (bf16[2,24,2048]{2,1,0:T(8,128)(2,1)}, bf16[2,24,2048]{2,1,0:T(8,128)(2,1)}, u32[]{:S(2)}, u32[]{:S(2)}) collective-permute-start(bf16[2,24,2048]{2,1,0:T(8,128)(2,1)} %get-tuple-element.54), channel_id=1, source_target_pairs={{0,128},{64,192},{128,256},{192,320},{256,384},{320,448},{384,0},{... | collective-permute-start | bytes 589832 | tf_op jit(solution)/shard_map/ppermute | solution.py:315
  120.3 17.3 %collective-permute-start.19 = (bf16[1,32,384]{2,1,0:T(8,128)(2,1)S(1)}, bf16[1,32,384]{2,1,0:T(8,128)(2,1)S(1)}, u32[]{:S(2)}, u32[]{:S(2)}) collective-permute-start(bf16[1,32,384]{2,1,0:T(8,128)(2,1)S(1)} %copy-done.47), channel_id=1, source_target_pairs={{0,516},{4,520},{8,524},{12,512},{512,4},{516,8},{520,12},{524,0},... | collective-permute-start | bytes 73736 | tf_op jit(solution)/shard_map/ppermute | solution.py:311
  137.6 20.4 %collective-permute-start.20 = (bf16[1,32,384]{2,1,0:T(8,128)(2,1)S(1)}, bf16[1,32,384]{2,1,0:T(8,128)(2,1)S(1)}, u32[]{:S(2)}, u32[]{:S(2)}) collective-permute-start(bf16[1,32,384]{2,1,0:T(8,128)(2,1)S(1)} %copy-done.47), channel_id=1, source_target_pairs={{0,520},{4,524},{8,512},{12,516},{512,8},{516,12},{520,0},{524,4},... | collective-permute-start | bytes 73736 | tf_op jit(solution)/shard_map/ppermute | solution.py:311
  158.0 19.3 %collective-permute-start.21 = (bf16[1,32,384]{2,1,0:T(8,128)(2,1)S(1)}, bf16[1,32,384]{2,1,0:T(8,128)(2,1)S(1)}, u32[]{:S(2)}, u32[]{:S(2)}) collective-permute-start(bf16[1,32,384]{2,1,0:T(8,128)(2,1)S(1)} %copy-done.47), channel_id=1, source_target_pairs={{0,524},{4,512},{8,516},{12,520},{512,12},{516,0},{520,4},{524,8},... | collective-permute-start | bytes 73736 | tf_op jit(solution)/shard_map/ppermute | solution.py:311
  188.7 15.4 %collective-permute-start.2 = (bf16[2,24,2048]{2,1,0:T(8,128)(2,1)}, bf16[2,24,2048]{2,1,0:T(8,128)(2,1)S(1)}, u32[]{:S(2)}, u32[]{:S(2)}) collective-permute-start(bf16[2,24,2048]{2,1,0:T(8,128)(2,1)} %get-tuple-element.55), channel_id=1, source_target_pairs={{0,192},{64,256},{128,320},{192,384},{256,448},{320,0},{384,64},{4... | collective-permute-start | bytes 589832 | tf_op jit(solution)/shard_map/ppermute | solution.py:315
  190.6 15.9 %collective-permute-start.3 = (bf16[2,24,2048]{2,1,0:T(8,128)(2,1)}, bf16[2,24,2048]{2,1,0:T(8,128)(2,1)S(1)}, u32[]{:S(2)}, u32[]{:S(2)}) collective-permute-start(bf16[2,24,2048]{2,1,0:T(8,128)(2,1)} %get-tuple-element.56), channel_id=1, source_target_pairs={{0,256},{64,320},{128,384},{192,448},{256,0},{320,64},{384,128},{4... | collective-permute-start | bytes 589832 | tf_op jit(solution)/shard_map/ppermute | solution.py:315
  194.2 17.3 %collective-permute-start.4 = (bf16[2,24,2048]{2,1,0:T(8,128)(2,1)}, bf16[2,24,2048]{2,1,0:T(8,128)(2,1)}, u32[]{:S(2)}, u32[]{:S(2)}) collective-permute-start(bf16[2,24,2048]{2,1,0:T(8,128)(2,1)} %get-tuple-element.57), channel_id=1, source_target_pairs={{0,320},{64,384},{128,448},{192,0},{256,64},{320,128},{384,192},{4... | collective-permute-start | bytes 589832 | tf_op jit(solution)/shard_map/ppermute | solution.py:315
  199.1 14.3 %collective-permute-start.5 = (bf16[2,24,2048]{2,1,0:T(8,128)(2,1)}, bf16[2,24,2048]{2,1,0:T(8,128)(2,1)}, u32[]{:S(2)}, u32[]{:S(2)}) collective-permute-start(bf16[2,24,2048]{2,1,0:T(8,128)(2,1)} %get-tuple-element.58), channel_id=1, source_target_pairs={{0,384},{64,448},{128,0},{192,64},{256,128},{320,192},{384,256},{4... | collective-permute-start | bytes 589832 | tf_op jit(solution)/shard_map/ppermute | solution.py:315
  201.1 17.5 %collective-permute-start.6 = (bf16[2,24,2048]{2,1,0:T(8,128)(2,1)}, bf16[2,24,2048]{2,1,0:T(8,128)(2,1)}, u32[]{:S(2)}, u32[]{:S(2)}) collective-permute-start(bf16[2,24,2048]{2,1,0:T(8,128)(2,1)} %get-tuple-element.59), channel_id=1, source_target_pairs={{0,448},{64,0},{128,64},{192,128},{256,192},{320,256},{384,320},{4... | collective-permute-start | bytes 589832 | tf_op jit(solution)/shard_map/ppermute | solution.py:315
  204.4 23.9 %collective-permute-start.25 = (bf16[1,512,384]{2,1,0:T(8,128)(2,1)S(1)}, bf16[1,512,384]{2,1,0:T(8,128)(2,1)S(1)}, u32[]{:S(2)}, u32[]{:S(2)}) collective-permute-start(bf16[1,512,384]{2,1,0:T(8,128)(2,1)S(1)} %copy-done.4), channel_id=1, source_target_pairs={{0,16},{16,32},{32,48},{48,0},{1,17},{17,33},{33,49},{49,1},{2,18}... | collective-permute-start | bytes 1179656 | tf_op jit(solution)/shard_map/ppermute | solution.py:315
  206.6 23.7 %collective-permute-start.26 = (bf16[1,512,384]{2,1,0:T(8,128)(2,1)S(1)}, bf16[1,512,384]{2,1,0:T(8,128)(2,1)S(1)}, u32[]{:S(2)}, u32[]{:S(2)}) collective-permute-start(bf16[1,512,384]{2,1,0:T(8,128)(2,1)S(1)} %copy-done.4), channel_id=1, source_target_pairs={{0,48},{16,0},{32,16},{48,32},{1,49},{17,1},{33,17},{49,33},{2,50}... | collective-permute-start | bytes 1179656 | tf_op jit(solution)/shard_map/ppermute | solution.py:315
  211.4 24.0 %collective-permute-start.16 = (bf16[2,256,384]{2,1,0:T(8,128)(2,1)}, bf16[2,256,384]{2,1,0:T(8,128)(2,1)S(1)}, u32[]{:S(2)}, u32[]{:S(2)}) collective-permute-start(bf16[2,256,384]{2,1,0:T(8,128)(2,1)} %slice.16), channel_id=1, source_target_pairs={{0,16},{16,32},{32,48},{48,0},{1,17},{17,33},{33,49},{49,1},{2,18}... | collective-permute-start | bytes 1179656 | tf_op jit(solution)/shard_map/ppermute | solution.py:315
  213.4 25.4 %collective-permute-start.17 = (bf16[2,256,384]{2,1,0:T(8,128)(2,1)S(1)}, bf16[2,256,384]{2,1,0:T(8,128)(2,1)S(1)}, u32[]{:S(2)}, u32[]{:S(2)}) collective-permute-start(bf16[2,256,384]{2,1,0:T(8,128)(2,1)S(1)} %slice.17), channel_id=1, source_target_pairs={{0,48},{16,0},{32,16},{48,32},{1,49},{17,1},{33,17},{49,33},{2,50}... | collective-permute-start | bytes 1179656 | tf_op jit(solution)/shard_map/ppermute | solution.py:315
  226.3 19.9 %collective-permute-start.36 = (bf16[512,384]{1,0:T(8,128)(2,1)}, bf16[512,384]{1,0:T(8,128)(2,1)S(1)}, u32[]{:S(2)}, u32[]{:S(2)}) collective-permute-start(bf16[512,384]{1,0:T(8,128)(2,1)} %get-tuple-element.82), channel_id=1, source_target_pairs={{0,16},{16,32},{32,48},{48,0},{1,17},{17,33},{33,49},{49,1},{2,18}... | collective-permute-start | bytes 1179656 | tf_op jit(solution)/shard_map/ppermute | solution.py:315
  228.3 25.5 %collective-permute-start.27 = (bf16[1,256,384]{2,1,0:T(8,128)(2,1)S(1)}, bf16[1,256,384]{2,1,0:T(8,128)(2,1)S(1)}, u32[]{:S(2)}, u32[]{:S(2)}) collective-permute-start(bf16[1,256,384]{2,1,0:T(8,128)(2,1)S(1)} %slice.18), channel_id=1, source_target_pairs={{0,16},{16,32},{32,48},{48,0},{1,17},{17,33},{33,49},{49,1},{2,18}... | collective-permute-start | bytes 589832 | tf_op jit(solution)/shard_map/ppermute | solution.py:315
  230.3 26.1 %collective-permute-start.28 = (bf16[1,256,384]{2,1,0:T(8,128)(2,1)S(1)}, bf16[1,256,384]{2,1,0:T(8,128)(2,1)}, u32[]{:S(2)}, u32[]{:S(2)}) collective-permute-start(bf16[1,256,384]{2,1,0:T(8,128)(2,1)S(1)} %slice.19), channel_id=1, source_target_pairs={{0,48},{16,0},{32,16},{48,32},{1,49},{17,1},{33,17},{49,33},{2,50}... | collective-permute-start | bytes 589832 | tf_op jit(solution)/shard_map/ppermute | solution.py:315
  235.4 29.4 %collective-permute-start.37 = (bf16[512,384]{1,0:T(8,128)(2,1)}, bf16[512,384]{1,0:T(8,128)(2,1)S(1)}, u32[]{:S(2)}, u32[]{:S(2)}) collective-permute-start(bf16[512,384]{1,0:T(8,128)(2,1)} %get-tuple-element.83), channel_id=1, source_target_pairs={{0,32},{16,48},{32,0},{48,16},{1,33},{17,49},{33,1},{49,17},{2,34}... | collective-permute-start | bytes 1179656 | tf_op jit(solution)/shard_map/ppermute | solution.py:315
  238.8 26.0 %collective-permute-start.38 = (bf16[512,384]{1,0:T(8,128)(2,1)}, bf16[512,384]{1,0:T(8,128)(2,1)S(1)}, u32[]{:S(2)}, u32[]{:S(2)}) collective-permute-start(bf16[512,384]{1,0:T(8,128)(2,1)} %get-tuple-element.84), channel_id=1, source_target_pairs={{0,48},{16,0},{32,16},{48,32},{1,49},{17,1},{33,17},{49,33},{2,50}... | collective-permute-start | bytes 1179656 | tf_op jit(solution)/shard_map/ppermute | solution.py:315
  246.3 23.0 %collective-permute-start.39 = (bf16[512,384]{1,0:T(8,128)(2,1)}, bf16[512,384]{1,0:T(8,128)(2,1)S(1)}, u32[]{:S(2)}, u32[]{:S(2)}) collective-permute-start(bf16[512,384]{1,0:T(8,128)(2,1)} %get-tuple-element.86), channel_id=1, source_target_pairs={{0,16},{16,32},{32,48},{48,0},{1,17},{17,33},{33,49},{49,1},{2,18}... | collective-permute-start | bytes 1179656 | tf_op jit(solution)/shard_map/ppermute | solution.py:315
  254.5 14.8 %collective-permute-start.40 = (bf16[512,384]{1,0:T(8,128)(2,1)}, bf16[512,384]{1,0:T(8,128)(2,1)S(1)}, u32[]{:S(2)}, u32[]{:S(2)}) collective-permute-start(bf16[512,384]{1,0:T(8,128)(2,1)} %get-tuple-element.87), channel_id=1, source_target_pairs={{0,32},{16,48},{32,0},{48,16},{1,33},{17,49},{33,1},{49,17},{2,34}... | collective-permute-start | bytes 1179656 | tf_op jit(solution)/shard_map/ppermute | solution.py:315
  256.4 16.7 %collective-permute-start.41 = (bf16[512,384]{1,0:T(8,128)(2,1)}, bf16[512,384]{1,0:T(8,128)(2,1)S(1)}, u32[]{:S(2)}, u32[]{:S(2)}) collective-permute-start(bf16[512,384]{1,0:T(8,128)(2,1)} %get-tuple-element.88), channel_id=1, source_target_pairs={{0,48},{16,0},{32,16},{48,32},{1,49},{17,1},{33,17},{49,33},{2,50}... | collective-permute-start | bytes 1179656 | tf_op jit(solution)/shard_map/ppermute | solution.py:315
  264.8 22.0 %collective-permute-start.29 = (bf16[2,24,2048]{2,1,0:T(8,128)(2,1)}, bf16[2,24,2048]{2,1,0:T(8,128)(2,1)S(1)}, u32[]{:S(2)}, u32[]{:S(2)}) collective-permute-start(bf16[2,24,2048]{2,1,0:T(8,128)(2,1)} %get-tuple-element.72), channel_id=1, source_target_pairs={{0,448},{64,0},{128,64},{192,128},{256,192},{320,256},{384,320},{4... | collective-permute-start | bytes 589832 | tf_op jit(solution)/shard_map/ppermute | solution.py:315
  264.9 25.1 %collective-permute-start.30 = (bf16[2,24,2048]{2,1,0:T(8,128)(2,1)}, bf16[2,24,2048]{2,1,0:T(8,128)(2,1)S(1)}, u32[]{:S(2)}, u32[]{:S(2)}) collective-permute-start(bf16[2,24,2048]{2,1,0:T(8,128)(2,1)} %get-tuple-element.73), channel_id=1, source_target_pairs={{0,384},{64,448},{128,0},{192,64},{256,128},{320,192},{384,256},{4... | collective-permute-start | bytes 589832 | tf_op jit(solution)/shard_map/ppermute | solution.py:315
  277.3 16.4 %collective-permute-start.42 = (bf16[2,4,32,384]{3,2,1,0:T(8,128)(2,1)}, bf16[2,4,32,384]{3,2,1,0:T(8,128)(2,1)S(1)}, u32[]{:S(2)}, u32[]{:S(2)}) collective-permute-start(bf16[2,4,32,384]{3,2,1,0:T(8,128)(2,1)} %get-tuple-element.90), channel_id=1, source_target_pairs={{0,1},{1,2},{2,3},{3,0},{4,5},{5,6},{6,7},{7,4},{8,9},{9,10},{10,1... | collective-permute-start | bytes 589832 | tf_op jit(solution)/shard_map/ppermute | solution.py:315
  279.2 18.5 %collective-permute-start.43 = (bf16[2,4,32,384]{3,2,1,0:T(8,128)(2,1)}, bf16[2,4,32,384]{3,2,1,0:T(8,128)(2,1)S(1)}, u32[]{:S(2)}, u32[]{:S(2)}) collective-permute-start(bf16[2,4,32,384]{3,2,1,0:T(8,128)(2,1)} %get-tuple-element.91), channel_id=1, source_target_pairs={{0,2},{1,3},{2,0},{3,1},{4,6},{5,7},{6,4},{7,5},{8,10},{9,11},{10,... | collective-permute-start | bytes 589832 | tf_op jit(solution)/shard_map/ppermute | solution.py:315
  282.7 18.1 %collective-permute-start.44 = (bf16[2,4,32,384]{3,2,1,0:T(8,128)(2,1)}, bf16[2,4,32,384]{3,2,1,0:T(8,128)(2,1)S(1)}, u32[]{:S(2)}, u32[]{:S(2)}) collective-permute-start(bf16[2,4,32,384]{3,2,1,0:T(8,128)(2,1)} %get-tuple-element.92), channel_id=1, source_target_pairs={{0,3},{1,0},{2,1},{3,2},{4,7},{5,4},{6,5},{7,6},{8,11},{9,8},{10,9... | collective-permute-start | bytes 589832 | tf_op jit(solution)/shard_map/ppermute | solution.py:315
  286.9 16.5 %collective-permute-start.31 = (bf16[2,24,2048]{2,1,0:T(8,128)(2,1)S(1)}, bf16[2,24,2048]{2,1,0:T(8,128)(2,1)S(1)}, u32[]{:S(2)}, u32[]{:S(2)}) collective-permute-start(bf16[2,24,2048]{2,1,0:T(8,128)(2,1)S(1)} %copy-done.44), channel_id=1, source_target_pairs={{0,320},{64,384},{128,448},{192,0},{256,64},{320,128},{384,192},{4... | collective-permute-start | bytes 589832 | tf_op jit(solution)/shard_map/ppermute | solution.py:315
  290.0 16.2 %collective-permute-start.32 = (bf16[2,24,2048]{2,1,0:T(8,128)(2,1)S(1)}, bf16[2,24,2048]{2,1,0:T(8,128)(2,1)S(1)}, u32[]{:S(2)}, u32[]{:S(2)}) collective-permute-start(bf16[2,24,2048]{2,1,0:T(8,128)(2,1)S(1)} %copy-done.43), channel_id=1, source_target_pairs={{0,256},{64,320},{128,384},{192,448},{256,0},{320,64},{384,128},{4... | collective-permute-start | bytes 589832 | tf_op jit(solution)/shard_map/ppermute | solution.py:315
  293.7 24.1 %collective-permute-start.33 = (bf16[2,24,2048]{2,1,0:T(8,128)(2,1)S(1)}, bf16[2,24,2048]{2,1,0:T(8,128)(2,1)S(1)}, u32[]{:S(2)}, u32[]{:S(2)}) collective-permute-start(bf16[2,24,2048]{2,1,0:T(8,128)(2,1)S(1)} %copy-done.41), channel_id=1, source_target_pairs={{0,192},{64,256},{128,320},{192,384},{256,448},{320,0},{384,64},{4... | collective-permute-start | bytes 589832 | tf_op jit(solution)/shard_map/ppermute | solution.py:315
  297.8 33.6 %collective-permute-start.34 = (bf16[2,24,2048]{2,1,0:T(8,128)(2,1)S(1)}, bf16[2,24,2048]{2,1,0:T(8,128)(2,1)S(1)}, u32[]{:S(2)}, u32[]{:S(2)}) collective-permute-start(bf16[2,24,2048]{2,1,0:T(8,128)(2,1)S(1)} %copy-done.40), channel_id=1, source_target_pairs={{0,128},{64,192},{128,256},{192,320},{256,384},{320,448},{384,0},{... | collective-permute-start | bytes 589832 | tf_op jit(solution)/shard_map/ppermute | solution.py:315
  300.9 41.7 %collective-permute-start.35 = (bf16[2,24,2048]{2,1,0:T(8,128)(2,1)S(1)}, bf16[2,24,2048]{2,1,0:T(8,128)(2,1)S(1)}, u32[]{:S(2)}, u32[]{:S(2)}) collective-permute-start(bf16[2,24,2048]{2,1,0:T(8,128)(2,1)S(1)} %copy-done.39), channel_id=1, source_target_pairs={{0,64},{64,128},{128,192},{192,256},{256,320},{320,384},{384,448},... | collective-permute-start | bytes 589832 | tf_op jit(solution)/shard_map/ppermute | solution.py:315
  303.4 46.8 %collective-permute-start.45 = (bf16[32,384]{1,0:T(8,128)(2,1)}, bf16[32,384]{1,0:T(8,128)(2,1)S(1)}, u32[]{:S(2)}, u32[]{:S(2)}) collective-permute-start(bf16[32,384]{1,0:T(8,128)(2,1)} %get-tuple-element.94), channel_id=1, source_target_pairs={{0,4},{4,8},{8,12},{12,512},{512,516},{516,520},{520,524},{524,0},... | collective-permute-start | bytes 73736 | tf_op jit(solution)/shard_map/ppermute | solution.py:315
  306.3 51.4 %collective-permute-start.46 = (bf16[32,384]{1,0:T(8,128)(2,1)}, bf16[32,384]{1,0:T(8,128)(2,1)S(1)}, u32[]{:S(2)}, u32[]{:S(2)}) collective-permute-start(bf16[32,384]{1,0:T(8,128)(2,1)} %get-tuple-element.95), channel_id=1, source_target_pairs={{0,8},{4,12},{8,512},{12,516},{512,520},{516,524},{520,0},{524,4},... | collective-permute-start | bytes 73736 | tf_op jit(solution)/shard_map/ppermute | solution.py:315
  317.8 45.3 %collective-permute-start.47 = (bf16[32,384]{1,0:T(8,128)(2,1)}, bf16[32,384]{1,0:T(8,128)(2,1)S(1)}, u32[]{:S(2)}, u32[]{:S(2)}) collective-permute-start(bf16[32,384]{1,0:T(8,128)(2,1)} %get-tuple-element.96), channel_id=1, source_target_pairs={{0,12},{4,512},{8,516},{12,520},{512,524},{516,0},{520,4},{524,8},... | collective-permute-start | bytes 73736 | tf_op jit(solution)/shard_map/ppermute | solution.py:315
  331.4 31.7 %collective-permute-start.48 = (bf16[32,384]{1,0:T(8,128)(2,1)}, bf16[32,384]{1,0:T(8,128)(2,1)S(1)}, u32[]{:S(2)}, u32[]{:S(2)}) collective-permute-start(bf16[32,384]{1,0:T(8,128)(2,1)} %get-tuple-element.97), channel_id=1, source_target_pairs={{0,512},{4,516},{8,520},{12,524},{512,0},{516,4},{520,8},{524,12},... | collective-permute-start | bytes 73736 | tf_op jit(solution)/shard_map/ppermute | solution.py:315
  342.6 26.2 %collective-permute-start.49 = (bf16[32,384]{1,0:T(8,128)(2,1)}, bf16[32,384]{1,0:T(8,128)(2,1)S(1)}, u32[]{:S(2)}, u32[]{:S(2)}) collective-permute-start(bf16[32,384]{1,0:T(8,128)(2,1)} %get-tuple-element.98), channel_id=1, source_target_pairs={{0,516},{4,520},{8,524},{12,0},{512,4},{516,8},{520,12},{524,512},... | collective-permute-start | bytes 73736 | tf_op jit(solution)/shard_map/ppermute | solution.py:315
  350.3 18.5 %collective-permute-start.50 = (bf16[32,384]{1,0:T(8,128)(2,1)}, bf16[32,384]{1,0:T(8,128)(2,1)S(1)}, u32[]{:S(2)}, u32[]{:S(2)}) collective-permute-start(bf16[32,384]{1,0:T(8,128)(2,1)} %get-tuple-element.99), channel_id=1, source_target_pairs={{0,520},{4,524},{8,0},{12,4},{512,8},{516,12},{520,512},{524,516},... | collective-permute-start | bytes 73736 | tf_op jit(solution)/shard_map/ppermute | solution.py:315
  357.7 13.4 %collective-permute-start.51 = (bf16[32,384]{1,0:T(8,128)(2,1)}, bf16[32,384]{1,0:T(8,128)(2,1)S(1)}, u32[]{:S(2)}, u32[]{:S(2)}) collective-permute-start(bf16[32,384]{1,0:T(8,128)(2,1)} %get-tuple-element.100), channel_id=1, source_target_pairs={{0,524},{4,0},{8,4},{12,8},{512,12},{516,512},{520,516},{524,520},... | collective-permute-start | bytes 73736 | tf_op jit(solution)/shard_map/ppermute | solution.py:315
  (52 other events, 918.2 us)

commit v3 on v2

--- a/solution.py
+++ b/solution.py
@@ -68,7 +68,7 @@
     din_ref[...] = dot(pick, grads, 0, 0).astype(BF16)
 
 
-def pieces_kernel(at_ref, gate_ref, up_ref, down_ref, pair_ref, last_ref):
+def pieces_kernel(at_ref, gate_ref, up_ref, down_ref, out_ref):
     rows = gate_ref.shape[0]
     lanes = down_ref.shape[1]
     shift = lax.rem(at_ref[0], lanes // rows) * rows
@@ -76,9 +76,9 @@
         lax.broadcasted_iota(jnp.int32, (rows, lanes), 1)
         == lax.broadcasted_iota(jnp.int32, (rows, lanes), 0) + shift
     ).astype(BF16)
-    pair_ref[0] = gate_ref[...]
-    pair_ref[1] = up_ref[...]
-    last_ref[0] = dot(pick, down_ref[...], 1, 1).astype(BF16)
+    out_ref[0] = gate_ref[...]
+    out_ref[1] = up_ref[...]
+    out_ref[2] = dot(pick, down_ref[...], 1, 1).astype(BF16)
 
 
 def row_mask(half, count, halves, width):
@@ -161,12 +161,12 @@
 
 
 def far_last_kernel(halves, parts, at_ref, grads_ref, gate_ref, up_ref, hidden_ref, o_ref, d_ref, *refs):
-    pairs, downs, outs = refs[:5], refs[5:10], refs[10:]
+    weights, outs = refs[:5], refs[5:]
     size = grads_ref.shape[1] // parts
     x = at_ref[1]
     dh = None
-    for start, ref, count in far_blocks(x, parts, size, downs):
-        part = dot(grads_ref[:, columns(start, count)], ref[0])
+    for start, ref, count in far_blocks(x, parts, size, weights):
+        part = dot(grads_ref[:, columns(start, count)], ref[2])
         dh = part if dh is None else dh + part
     gate, up = gate_ref[...], up_ref[...]
     keep = row_mask(1 - at_ref[0], gate.shape[0], halves, gate.shape[1])
@@ -174,12 +174,10 @@
     dgate, dup = input_grads(gate, up, sig, silu, dh, keep)
     hidden = hidden_ref[...]
     rows = outs[0].shape[1]
-    for (start, down, count), (_, pair, _) in zip(
-        far_blocks(x, parts, size, downs), far_blocks(x, parts, size, pairs)
-    ):
+    for start, ref, count in far_blocks(x, parts, size, weights):
         cols = columns(start, count)
-        out = dot(hidden, down[0], 1, 1).astype(BF16) + o_ref[:, cols]
-        dx = dot(dgate, pair[0], 1, 1) + dot(dup, pair[1], 1, 1)
+        out = dot(hidden, ref[2], 1, 1).astype(BF16) + o_ref[:, cols]
+        dx = dot(dgate, ref[0], 1, 1) + dot(dup, ref[1], 1, 1)
         dx = dx.astype(BF16) + d_ref[:, cols]
         for k, out_ref in enumerate(outs):
             out_ref[0, :, cols] = out[k * rows : (k + 1) * rows]
@@ -220,27 +218,28 @@
                     sends[j - 1][where, a] = total.astype(BF16)
 
 
-def sum_b_kernel(at_ref, *refs):
-    count = refs[0].shape[0]
-    ins = [ref for ref in refs if ref.shape[0] == count and len(ref.shape) == 3]
-    own_ref, sends = refs[len(ins)], refs[len(ins) + 1 :]
+def sum_b_kernel(at_ref, first_ref, *refs):
+    ins, (own_ref, send_ref) = refs[:-2], refs[-2:]
     me = at_ref[4]
-    for k in range(count):
-        to = lax.rem(me + k, count)
-        total = ins[0][to]
-        for ref in ins[1:]:
-            total = total + ref[to].astype(F32)
-        if k == 0:
-            own_ref[...] = total
-        else:
-            sends[k - 1][...] = total.astype(BF16)
-
-
-def sum_last_kernel(*refs):
-    total = refs[0][...]
-    for ref in refs[1:-1]:
-        total = total + ref[...].astype(F32)
-    refs[-1][...] = total
+    for k in range(first_ref.shape[0]):
+        total = first_ref[k]
+        for ref in ins:
+            total = total + ref[k].astype(F32)
+        send_ref[k] = total.astype(BF16)
+
+    total = first_ref[me]
+    for ref in ins:
+        total = total + ref[me].astype(F32)
+    own_ref[...] = total
+
+
+def sum_last_kernel(at_ref, own_ref, in_ref, out_ref):
+    me = at_ref[4]
+    total = own_ref[...]
+    for k in range(in_ref.shape[0]):
+        part = in_ref[k].astype(F32)
+        total = total + jnp.where(me == k, jnp.zeros_like(part), part)
+    out_ref[...] = total
 
 
 def call(kernel, outs, *args, scalar=True, flops=0):
@@ -279,7 +278,7 @@
     w_gate, w_up, w_down = w_gate[0], w_up[0], w_down[0]
 
     per = 128 // depth
-    pair, last = pl.pallas_call(
+    piece = pl.pallas_call(
         pieces_kernel,
         grid_spec=pltpu.PrefetchScalarGridSpec(
             num_scalar_prefetch=1,
@@ -289,12 +288,9 @@
                 pl.BlockSpec((depth, inner), lambda i, s: (s[0], 0)),
                 pl.BlockSpec((inner, 128), lambda i, s: (0, lax.div(s[0], per))),
             ],
-            out_specs=[
-                pl.BlockSpec((2, depth, inner), lambda i, s: (0, 0, 0)),
-                pl.BlockSpec((1, depth, inner), lambda i, s: (0, 0, 0)),
-            ],
+            out_specs=pl.BlockSpec((3, depth, inner), lambda i, s: (0, 0, 0)),
         ),
-        out_shape=(shape(2, depth, inner), shape(1, depth, inner)),
+        out_shape=shape(3, depth, inner),
     )(shard, w_gate, w_up, w_down)
 
     def cross(v):
@@ -330,10 +326,7 @@
         high = shift(right[:, half:], "x", nx, nx - 1)
         return v, left, right, low, high
 
-    spread_pair = spread(cross(pair))
-    last, spread_pair = lax.optimization_barrier((last, spread_pair))
-    pairs = around(spread_pair)
-    downs = around(spread(cross(last)))
+    far_weights = around(spread(cross(piece)))
 
     ids = expert_ids.reshape(1, count)
     ints = combine_ints.T
@@ -360,13 +353,13 @@
     gate, up, hidden, *far_parts = call(
         functools.partial(far_first_kernel, halves),
         (shape(slots, inner, dtype=F32),) * 2 + (shape(slots, inner),) + partial_shapes,
-        at, rows, grads, *pairs, flops=3 * work,
+        at, rows, grads, *far_weights, flops=3 * work,
     )
     far_sums = over_x(*far_parts)
     results = call(
         functools.partial(far_last_kernel, halves, nx),
         packet,
-        at, grads, gate, up, hidden, near_out, near_dx, *pairs, *downs, flops=4 * work,
+        at, grads, gate, up, hidden, near_out, near_dx, *far_weights, flops=4 * work,
     )
 
     own, *sends = call(
@@ -377,13 +370,13 @@
     )
     far = halves * quads
     received = [shift(v, "b", nb, k + 1) for k, v in enumerate(sends)]
-    own, *sends = call(
+    own, send = call(
         sum_b_kernel,
-        (shape(depth, inner, dtype=F32),) + (shape(depth, inner),) * (far - 1),
+        (shape(depth, inner, dtype=F32), shape(far, depth, inner)),
         at, *(v.reshape(far, depth, inner) for v in (own, *received)),
     )
-    received = [shift(v, ("zh", "a"), far, k + 1) for k, v in enumerate(sends)]
-    grad = call(sum_last_kernel, (shape(depth, inner, dtype=F32),), own, *received, scalar=False)[0]
+    received = lax.all_to_all(send, ("zh", "a"), split_axis=0, concat_axis=0, tiled=True)
+    grad = call(sum_last_kernel, (shape(depth, inner, dtype=F32),), at, own, received)[0]
 
     returned = [shift(v, both, near, near - k) if k else v for k, v in enumerate(results)]
     combined, dinput = call(

time: 377 us -> 292 us (0.77)
  the two profiles are of different devices: /device:TPU:24 before, /device:TPU:38 now
where the time goes in v3:
time: 292 us; the launch traced here: 291 us
  starting transfers between devices  148 us (51%)
  waiting for transfers between devices  97.8 us (33%)
  Pallas kernels  36.7 us (13%)
  local copies, waits for them, and re-layouts  7.08 us (2%)
    ppermute x30, starting transfers between devices, shift(): return lax.ppermute(v, name, [(i, (i + k) % size) for i in range(size)])  89.2 us
    ppermute x30, waiting for transfers between devices, shift(): return lax.ppermute(v, name, [(i, (i + k) % size) for i in range(size)])  68.7 us
    ppermute x4, starting transfers between devices, cross(): parts.append(lax.ppermute(v, ('zh', 'a'), p))  45.2 us
    pallas_call x9, Pallas kernels, raw_call(): pl.pallas_call(kernel, out_shape=outs, in_specs=[smem if scalar and k ==...  35 us
    ppermute x4, waiting for transfers between devices, cross(): parts.append(lax.ppermute(v, ('zh', 'a'), p))  29.1 us
    all_to_all x1, starting transfers between devices, step(): lax.all_to_all(send, ('zh', 'a'), split_axis=0, concat_axis=0, tiled=True)  14 us
  transfers between devices with their start and end apart: 35, of which 18 were waited for; matrix products, arithmetic and copies ran while one was open for 1% of the time, Pallas kernels for 9%

profile of v3, /device:TPU:38, one launch (start us, length us, event | category | flops | bytes accessed | tf_op | source)
XLA Modules:
  0.0 291.2 jit_solution(17019037232889055595)
XLA Ops:
  2.4 28.1 %collective-permute-start.7 = (bf16[3,32,384]{2,1,0:T(8,128)(2,1)}, bf16[3,32,384]{2,1,0:T(8,128)(2,1)S(1)}, u32[]{:S(2)}, u32[]{:S(2)}) collective-permute-start(bf16[3,32,384]{2,1,0:T(8,128)(2,1)} %shard_map.96), channel_id=1, source_target_pairs={{0,512},{4,516},{8,520},{12,524},{512,0},{516,4},{520,8},{524,12},... | collective-permute-start | bytes 221192 | tf_op jit(solution)/shard_map/ppermute | solution.py:307
  30.4 1.9 collective-permute-start.8
  32.4 13.3 %collective-permute-start.9 = (bf16[3,32,384]{2,1,0:T(8,128)(2,1)}, bf16[3,32,384]{2,1,0:T(8,128)(2,1)S(1)}, u32[]{:S(2)}, u32[]{:S(2)}) collective-permute-start(bf16[3,32,384]{2,1,0:T(8,128)(2,1)} %shard_map.96), channel_id=1, source_target_pairs={{0,520},{4,524},{8,512},{12,516},{512,8},{516,12},{520,0},{524,4},... | collective-permute-start | bytes 221192 | tf_op jit(solution)/shard_map/ppermute | solution.py:307
  45.7 1.9 collective-permute-start.10
  47.6 24.9 %collective-permute-done.7 = bf16[3,32,384]{2,1,0:T(8,128)(2,1)S(1)} collective-permute-done((bf16[3,32,384]{2,1,0:T(8,128)(2,1)}, bf16[3,32,384]{2,1,0:T(8,128)(2,1)S(1)}, u32[]{:S(2)}, u32[]{:S(2)}) %collective-permute-start.7) | collective-permute-done | bytes 73760 | tf_op jit(solution)/shard_map/ppermute | solution.py:307
  76.7 1.9 collective-permute-start.11
  78.6 10.4 %collective-permute-start.12 = (bf16[4,3,32,384]{3,2,1,0:T(8,128)(2,1)S(1)}, bf16[4,3,32,384]{3,2,1,0:T(8,128)(2,1)S(1)}, u32[]{:S(2)}, u32[]{:S(2)}) collective-permute-start(bf16[4,3,32,384]{3,2,1,0:T(8,128)(2,1)S(1)} %pad_maximum_fusion.refs_0_), channel_id=1, source_target_pairs={{0,2},{1,3},{2,0},{3,1},{4,6},{5,7},{6,4},{7,5},{8,10},{9,11},{10,... | collective-permute-start | bytes 884744 | tf_op jit(solution)/shard_map/ppermute | solution.py:311
  89.1 1.9 collective-permute-start.13
  92.6 15.2 %collective-permute-done.12.refs_2_ = bf16[4,3,32,384]{3,2,1,0:T(8,128)(2,1)S(1)} collective-permute-done((bf16[4,3,32,384]{3,2,1,0:T(8,128)(2,1)S(1)}, bf16[4,3,32,384]{3,2,1,0:T(8,128)(2,1)S(1)}, u32[]{:S(2)}, u32[]{:S(2)}) %collective-permute-start.12) | collective-permute-done | bytes 294944 | tf_op jit(solution)/shard_map/ppermute | solution.py:311
  107.9 5.1 %collective-permute-done.13.refs_3_ = bf16[4,3,32,384]{3,2,1,0:T(8,128)(2,1)S(1)} collective-permute-done((bf16[4,3,32,384]{3,2,1,0:T(8,128)(2,1)S(1)}, bf16[4,3,32,384]{3,2,1,0:T(8,128)(2,1)S(1)}, u32[]{:S(2)}, u32[]{:S(2)}) %collective-permute-start.13) | collective-permute-done | bytes 294944 | tf_op jit(solution)/shard_map/ppermute | solution.py:311
  113.7 2.4 shard_map.97.refs_0_
  116.1 2.4 collective-permute-start.14
  118.5 3.5 %collective-permute-start.15 = (bf16[3,512,384]{2,1,0:T(8,128)(2,1)}, bf16[3,512,384]{2,1,0:T(8,128)(2,1)S(1)}, u32[]{:S(2)}, u32[]{:S(2)}) collective-permute-start(bf16[3,512,384]{2,1,0:T(8,128)(2,1)} %shard_map.97.refs_0_), channel_id=1, source_target_pairs={{0,48},{16,0},{32,16},{48,32},{1,49},{17,1},{33,17},{49,33},{2,50}... | collective-permute-start | bytes 3538952 | tf_op jit(solution)/shard_map/ppermute | solution.py:311
  122.0 3.0 %shard_map.94 = (bf16[2,24,2048]{2,1,0:T(8,128)(2,1)}, bf16[2,24,2048]{2,1,0:T(8,128)(2,1)}, bf16[2,24,2048]{2,1,0:T(8,128)(2,1)}, bf16[2,24,2048]{2,1,0:T(8,128...) custom-call(s32[6]{0:T(128)} %stack.42.at_ref, ...), custom_call_target="tpu_custom_call" | custom-call | flops 201326592 | bytes 2626072 | tf_op jit(solution)/shard_map/pallas_call | solution.py:253
  125.0 3.5 %collective-permute-start.1 = (bf16[2,24,2048]{2,1,0:T(8,128)(2,1)}, bf16[2,24,2048]{2,1,0:T(8,128)(2,1)S(1)}, u32[]{:S(2)}, u32[]{:S(2)}) collective-permute-start(bf16[2,24,2048]{2,1,0:T(8,128)(2,1)} %get-tuple-element.44), channel_id=1, source_target_pairs={{0,128},{64,192},{128,256},{192,320},{256,384},{320,448},{384,0},{... | collective-permute-start | bytes 589832 | tf_op jit(solution)/shard_map/ppermute | solution.py:311
  128.5 4.2 %collective-permute-start.2 = (bf16[2,24,2048]{2,1,0:T(8,128)(2,1)}, bf16[2,24,2048]{2,1,0:T(8,128)(2,1)S(1)}, u32[]{:S(2)}, u32[]{:S(2)}) collective-permute-start(bf16[2,24,2048]{2,1,0:T(8,128)(2,1)} %get-tuple-element.45), channel_id=1, source_target_pairs={{0,192},{64,256},{128,320},{192,384},{256,448},{320,0},{384,64},{4... | collective-permute-start | bytes 589832 | tf_op jit(solution)/shard_map/ppermute | solution.py:311
  132.7 3.7 %collective-permute-start.3 = (bf16[2,24,2048]{2,1,0:T(8,128)(2,1)}, bf16[2,24,2048]{2,1,0:T(8,128)(2,1)}, u32[]{:S(2)}, u32[]{:S(2)}) collective-permute-start(bf16[2,24,2048]{2,1,0:T(8,128)(2,1)} %get-tuple-element.46), channel_id=1, source_target_pairs={{0,256},{64,320},{128,384},{192,448},{256,0},{320,64},{384,128},{4... | collective-permute-start | bytes 589832 | tf_op jit(solution)/shard_map/ppermute | solution.py:311
  136.5 4.1 %collective-permute-start.4 = (bf16[2,24,2048]{2,1,0:T(8,128)(2,1)}, bf16[2,24,2048]{2,1,0:T(8,128)(2,1)}, u32[]{:S(2)}, u32[]{:S(2)}) collective-permute-start(bf16[2,24,2048]{2,1,0:T(8,128)(2,1)} %get-tuple-element.47), channel_id=1, source_target_pairs={{0,320},{64,384},{128,448},{192,0},{256,64},{320,128},{384,192},{4... | collective-permute-start | bytes 589832 | tf_op jit(solution)/shard_map/ppermute | solution.py:311
  140.6 5.5 %collective-permute-done.14.refs_1_ = bf16[3,512,384]{2,1,0:T(8,128)(2,1)S(1)} collective-permute-done((bf16[3,512,384]{2,1,0:T(8,128)(2,1)}, bf16[3,512,384]{2,1,0:T(8,128)(2,1)S(1)}, u32[]{:S(2)}, u32[]{:S(2)}) %collective-permute-start.14) | collective-permute-done | bytes 1179680 | tf_op jit(solution)/shard_map/ppermute | solution.py:311
  146.1 4.9 %collective-permute-start.5 = (bf16[2,24,2048]{2,1,0:T(8,128)(2,1)}, bf16[2,24,2048]{2,1,0:T(8,128)(2,1)}, u32[]{:S(2)}, u32[]{:S(2)}) collective-permute-start(bf16[2,24,2048]{2,1,0:T(8,128)(2,1)} %get-tuple-element.48), channel_id=1, source_target_pairs={{0,384},{64,448},{128,0},{192,64},{256,128},{320,192},{384,256},{4... | collective-permute-start | bytes 589832 | tf_op jit(solution)/shard_map/ppermute | solution.py:311
  153.0 3.6 %collective-permute-start.16 = (bf16[3,256,384]{2,1,0:T(8,128)(2,1)}, bf16[3,256,384]{2,1,0:T(8,128)(2,1)S(1)}, u32[]{:S(2)}, u32[]{:S(2)}) collective-permute-start(bf16[3,256,384]{2,1,0:T(8,128)(2,1)} %slice.8), channel_id=1, source_target_pairs={{0,16},{16,32},{32,48},{48,0},{1,17},{17,33},{33,49},{49,1},{2,18}... | collective-permute-start | bytes 1769480 | tf_op jit(solution)/shard_map/ppermute | solution.py:311
  156.6 2.2 collective-permute-start.17
  159.0 7.7 %shard_map.95 = (bf16[192,2048]{1,0:T(8,128)(2,1)}, bf16[192,2048]{1,0:T(8,128)(2,1)}, bf16[192,2048]{1,0:T(8,128)(2,1)}, bf16[192,2048]{1,0:T(8,128)(2,1)}, f32...) custom-call(s32[6]{0:T(128)} %stack.42.at_ref, ...), custom_call_target="tpu_custom_call" | custom-call | flops 2113929216 | bytes 11403288 | tf_op jit(solution)/shard_map/pallas_call | solution.py:253
  166.7 4.8 %collective-permute-start.25 = (bf16[512,384]{1,0:T(8,128)(2,1)}, bf16[512,384]{1,0:T(8,128)(2,1)S(1)}, u32[]{:S(2)}, u32[]{:S(2)}) collective-permute-start(bf16[512,384]{1,0:T(8,128)(2,1)} %get-tuple-element.68), channel_id=1, source_target_pairs={{0,16},{16,32},{32,48},{48,0},{1,17},{17,33},{33,49},{49,1},{2,18}... | collective-permute-start | bytes 1179656 | tf_op jit(solution)/shard_map/ppermute | solution.py:311
  171.5 1.9 collective-permute-start.26
  173.4 2.8 collective-permute-start.27
  177.2 5.4 %shard_map.98 = (f32[192,384]{1,0:T(8,128)}, f32[192,384]{1,0:T(8,128)}, bf16[192,384]{1,0:T(8,128)(2,1)}, f32[512,384]{1,0:T(8,128)}, bf16[512,384]{1,0:T(8,128...) custom-call(s32[6]{0:T(128)} %stack.42.at_ref, bf16[192,2048]{1,0:T(8,128)(2,1)} %get-tuple-element.51.rows_ref, ...), custom_call_target="tpu_custom_call" | custom-call | flops 905969664 | bytes 8994840 | tf_op jit(solution)/shard_map/pallas_call | solution.py:253
  182.6 4.3 %collective-permute-start.28 = (bf16[512,384]{1,0:T(8,128)(2,1)}, bf16[512,384]{1,0:T(8,128)(2,1)S(1)}, u32[]{:S(2)}, u32[]{:S(2)}) collective-permute-start(bf16[512,384]{1,0:T(8,128)(2,1)} %get-tuple-element.72), channel_id=1, source_target_pairs={{0,16},{16,32},{32,48},{48,0},{1,17},{17,33},{33,49},{49,1},{2,18}... | collective-permute-start | bytes 1179656 | tf_op jit(solution)/shard_map/ppermute | solution.py:311
  186.9 4.2 %collective-permute-start.29 = (bf16[512,384]{1,0:T(8,128)(2,1)}, bf16[512,384]{1,0:T(8,128)(2,1)S(1)}, u32[]{:S(2)}, u32[]{:S(2)}) collective-permute-start(bf16[512,384]{1,0:T(8,128)(2,1)} %get-tuple-element.73), channel_id=1, source_target_pairs={{0,32},{16,48},{32,0},{48,16},{1,33},{17,49},{33,1},{49,17},{2,34}... | collective-permute-start | bytes 1179656 | tf_op jit(solution)/shard_map/ppermute | solution.py:311
  191.1 1.9 collective-permute-start.30
  193.1 2.4 collective-permute-done.27.refs_3_
  195.5 9.9 %collective-permute-done.28.refs_5_ = bf16[512,384]{1,0:T(8,128)(2,1)S(1)} collective-permute-done((bf16[512,384]{1,0:T(8,128)(2,1)}, bf16[512,384]{1,0:T(8,128)(2,1)S(1)}, u32[]{:S(2)}, u32[]{:S(2)}) %collective-permute-start.28) | collective-permute-done | bytes 393248 | tf_op jit(solution)/shard_map/ppermute | solution.py:311
  205.4 5.5 %collective-permute-done.30.refs_7_ = bf16[512,384]{1,0:T(8,128)(2,1)S(1)} collective-permute-done((bf16[512,384]{1,0:T(8,128)(2,1)}, bf16[512,384]{1,0:T(8,128)(2,1)S(1)}, u32[]{:S(2)}, u32[]{:S(2)}) %collective-permute-start.30) | collective-permute-done | bytes 393248 | tf_op jit(solution)/shard_map/ppermute | solution.py:311
  211.7 3.4 %shard_map.101 = (f32[2,4,32,384]{3,2,1,0:T(8,128)}, bf16[2,4,32,384]{3,2,1,0:T(8,128)(2,1)}, bf16[2,4,32,384]{3,2,1,0:T(8,128)(2,1)}, bf16[2,4,32,384]{3,2,1,0:T(8,128)(2,1)}) custom-call(s32[6]{0:T(128)} %stack.42.at_ref, f32[512,384]{1,0:T(8,128)} %get-tuple-element.67.refs_0_, bf16[512,384]{1,0:T(8,128)(2,1)} %copy-done.6, bf16[512,384]{1,0:T(8,128)(2,1)} %copy-done.7, ...), custom_call_target="tpu_custom_call" | custom-call | bytes 4915224 | tf_op jit(solution)/shard_map/pallas_call | solution.py:253
  218.9 3.9 %collective-permute-start.33 = (bf16[2,4,32,384]{3,2,1,0:T(8,128)(2,1)}, bf16[2,4,32,384]{3,2,1,0:T(8,128)(2,1)S(1)}, u32[]{:S(2)}, u32[]{:S(2)}) collective-permute-start(bf16[2,4,32,384]{3,2,1,0:T(8,128)(2,1)} %get-tuple-element.78), channel_id=1, source_target_pairs={{0,3},{1,0},{2,1},{3,2},{4,7},{5,4},{6,5},{7,6},{8,11},{9,8},{10,9... | collective-permute-start | bytes 589832 | tf_op jit(solution)/shard_map/ppermute | solution.py:311
  222.8 2.1 collective-permute-done.31
  224.9 9.6 %collective-permute-done.32 = bf16[2,4,32,384]{3,2,1,0:T(8,128)(2,1)S(1)} collective-permute-done((bf16[2,4,32,384]{3,2,1,0:T(8,128)(2,1)}, bf16[2,4,32,384]{3,2,1,0:T(8,128)(2,1)S(1)}, u32[]{:S(2)}, u32[]{:S(2)}) %collective-permute-start.32) | collective-permute-done | bytes 196640 | tf_op jit(solution)/shard_map/ppermute | solution.py:311
  235.9 2.0 shard_map.102
  237.9 14.0 %all-to-all-start = ((bf16[8,32,384]{2,1,0:T(8,128)(2,1)}), bf16[8,32,384]{2,1,0:T(8,128)(2,1)S(1)}, u32[]{:S(2)}, u32[]{:S(2)}) async-start(bf16[8,32,384]{2,1,0:T(8,128)(2,1)} %get-tuple-element.80), calls=%async_computation | async-start | bytes 393216 | tf_op jit(solution)/shard_map/all_to_all | solution.py:378
  252.0 6.5 %shard_map.99 = (bf16[2,24,2048]{2,1,0:T(8,128)(2,1)}, bf16[2,24,2048]{2,1,0:T(8,128)(2,1)}, bf16[2,24,2048]{2,1,0:T(8,128)(2,1)}, bf16[2,24,2048]{2,1,0:T(8,128...) custom-call(s32[6]{0:T(128)} %stack.42.at_ref, ...), custom_call_target="tpu_custom_call" | custom-call | flops 1207959552 | bytes 9388056 | tf_op jit(solution)/shard_map/pallas_call | solution.py:253
  258.6 2.6 collective-permute-start.19
  261.2 2.0 collective-permute-start.20
  263.2 5.2 %collective-permute-start.21 = (bf16[2,24,2048]{2,1,0:T(8,128)(2,1)}, bf16[2,24,2048]{2,1,0:T(8,128)(2,1)S(1)}, u32[]{:S(2)}, u32[]{:S(2)}) collective-permute-start(bf16[2,24,2048]{2,1,0:T(8,128)(2,1)} %get-tuple-element.61), channel_id=1, source_target_pairs={{0,256},{64,320},{128,384},{192,448},{256,0},{320,64},{384,128},{4... | collective-permute-start | bytes 589832 | tf_op jit(solution)/shard_map/ppermute | solution.py:311
  268.4 2.0 collective-permute-start.22
  270.4 3.0 %collective-permute-start.23 = (bf16[2,24,2048]{2,1,0:T(8,128)(2,1)}, bf16[2,24,2048]{2,1,0:T(8,128)(2,1)S(1)}, u32[]{:S(2)}, u32[]{:S(2)}) collective-permute-start(bf16[2,24,2048]{2,1,0:T(8,128)(2,1)} %get-tuple-element.63), channel_id=1, source_target_pairs={{0,128},{64,192},{128,256},{192,320},{256,384},{320,448},{384,0},{... | collective-permute-start | bytes 589832 | tf_op jit(solution)/shard_map/ppermute | solution.py:311
  274.5 4.7 %collective-permute-done.22.refs_5_ = bf16[2,24,2048]{2,1,0:T(8,128)(2,1)S(1)} collective-permute-done((bf16[2,24,2048]{2,1,0:T(8,128)(2,1)}, bf16[2,24,2048]{2,1,0:T(8,128)(2,1)S(1)}, u32[]{:S(2)}, u32[]{:S(2)}) %collective-permute-start.22) | collective-permute-done | bytes 196640 | tf_op jit(solution)/shard_map/ppermute | solution.py:311
  279.2 4.8 %collective-permute-done.23.refs_6_ = bf16[2,24,2048]{2,1,0:T(8,128)(2,1)S(1)} collective-permute-done((bf16[2,24,2048]{2,1,0:T(8,128)(2,1)}, bf16[2,24,2048]{2,1,0:T(8,128)(2,1)S(1)}, u32[]{:S(2)}, u32[]{:S(2)}) %collective-permute-start.23) | collective-permute-done | bytes 196640 | tf_op jit(solution)/shard_map/ppermute | solution.py:311
  286.0 2.9 %shard_map.100 = (bf16[128,2048]{1,0:T(8,128)(2,1)}, bf16[128,2048]{1,0:T(8,128)(2,1)}) custom-call(s32[6]{0:T(128)} %stack.42.at_ref, s32[1,128]{1,0:T(1,128)} %bitcast.41, s32[8,128]{1,0:T(8,128)} %bitcast.39, bf16[2,24,2048]{2,1,0:T(8,128)(2,1)} %get-tuple-element.57.refs_0_, bf16[2,24,2048]{2,1,0:T(8,128)(2,1)} %copy-done.18, ...), custom_call_target="tpu_custom_call" | custom-call | flops 201326592 | bytes 2626072 | tf_op jit(solution)/shard_map/pallas_call | solution.py:253
  (92 shorter events, 22.9 us)
Async XLA Ops:
  2.4 70.1 %collective-permute-start.7 = (bf16[3,32,384]{2,1,0:T(8,128)(2,1)}, bf16[3,32,384]{2,1,0:T(8,128)(2,1)S(1)}, u32[]{:S(2)}, u32[]{:S(2)}) collective-permute-start(bf16[3,32,384]{2,1,0:T(8,128)(2,1)} %shard_map.96), channel_id=1, source_target_pairs={{0,512},{4,516},{8,520},{12,524},{512,0},{516,4},{520,8},{524,12},... | collective-permute-start | bytes 221192 | tf_op jit(solution)/shard_map/ppermute | solution.py:307
  30.4 43.7 %collective-permute-start.8 = (bf16[3,32,384]{2,1,0:T(8,128)(2,1)}, bf16[3,32,384]{2,1,0:T(8,128)(2,1)S(1)}, u32[]{:S(2)}, u32[]{:S(2)}) collective-permute-start(bf16[3,32,384]{2,1,0:T(8,128)(2,1)} %shard_map.96), channel_id=1, source_target_pairs={{0,516},{4,520},{8,524},{12,512},{512,4},{516,8},{520,12},{524,0},... | collective-permute-start | bytes 221192 | tf_op jit(solution)/shard_map/ppermute | solution.py:307
  32.4 43.4 %collective-permute-start.9 = (bf16[3,32,384]{2,1,0:T(8,128)(2,1)}, bf16[3,32,384]{2,1,0:T(8,128)(2,1)S(1)}, u32[]{:S(2)}, u32[]{:S(2)}) collective-permute-start(bf16[3,32,384]{2,1,0:T(8,128)(2,1)} %shard_map.96), channel_id=1, source_target_pairs={{0,520},{4,524},{8,512},{12,516},{512,8},{516,12},{520,0},{524,4},... | collective-permute-start | bytes 221192 | tf_op jit(solution)/shard_map/ppermute | solution.py:307
  45.7 31.0 %collective-permute-start.10 = (bf16[3,32,384]{2,1,0:T(8,128)(2,1)}, bf16[3,32,384]{2,1,0:T(8,128)(2,1)S(1)}, u32[]{:S(2)}, u32[]{:S(2)}) collective-permute-start(bf16[3,32,384]{2,1,0:T(8,128)(2,1)} %shard_map.96), channel_id=1, source_target_pairs={{0,524},{4,512},{8,516},{12,520},{512,12},{516,0},{520,4},{524,8},... | collective-permute-start | bytes 221192 | tf_op jit(solution)/shard_map/ppermute | solution.py:307
  76.7 36.3 %copy-start.4 = (bf16[4,3,32,384]{3,2,1,0:T(8,128)(2,1)}, bf16[4,3,32,384]{3,2,1,0:T(8,128)(2,1)S(1)}, u32[]{:S(2)}) copy-start(bf16[4,3,32,384]{3,2,1,0:T(8,128)(2,1)S(1)} %pad_maximum_fusion.refs_0_) | copy-start | bytes 884740
  76.7 15.9 %collective-permute-start.11 = (bf16[4,3,32,384]{3,2,1,0:T(8,128)(2,1)S(1)}, bf16[4,3,32,384]{3,2,1,0:T(8,128)(2,1)S(1)}, u32[]{:S(2)}, u32[]{:S(2)}) collective-permute-start(bf16[4,3,32,384]{3,2,1,0:T(8,128)(2,1)S(1)} %pad_maximum_fusion.refs_0_), channel_id=1, source_target_pairs={{0,1},{1,2},{2,3},{3,0},{4,5},{5,6},{6,7},{7,4},{8,9},{9,10},{10,1... | collective-permute-start | bytes 884744 | tf_op jit(solution)/shard_map/ppermute | solution.py:311
  78.6 29.2 %collective-permute-start.12 = (bf16[4,3,32,384]{3,2,1,0:T(8,128)(2,1)S(1)}, bf16[4,3,32,384]{3,2,1,0:T(8,128)(2,1)S(1)}, u32[]{:S(2)}, u32[]{:S(2)}) collective-permute-start(bf16[4,3,32,384]{3,2,1,0:T(8,128)(2,1)S(1)} %pad_maximum_fusion.refs_0_), channel_id=1, source_target_pairs={{0,2},{1,3},{2,0},{3,1},{4,6},{5,7},{6,4},{7,5},{8,10},{9,11},{10,... | collective-permute-start | bytes 884744 | tf_op jit(solution)/shard_map/ppermute | solution.py:311
  89.1 23.9 %collective-permute-start.13 = (bf16[4,3,32,384]{3,2,1,0:T(8,128)(2,1)S(1)}, bf16[4,3,32,384]{3,2,1,0:T(8,128)(2,1)S(1)}, u32[]{:S(2)}, u32[]{:S(2)}) collective-permute-start(bf16[4,3,32,384]{3,2,1,0:T(8,128)(2,1)S(1)} %pad_maximum_fusion.refs_0_), channel_id=1, source_target_pairs={{0,3},{1,0},{2,1},{3,2},{4,7},{5,4},{6,5},{7,6},{8,11},{9,8},{10,9... | collective-permute-start | bytes 884744 | tf_op jit(solution)/shard_map/ppermute | solution.py:311
  92.6 20.4 %copy-start.12 = (bf16[4,3,32,384]{3,2,1,0:T(8,128)(2,1)}, bf16[4,3,32,384]{3,2,1,0:T(8,128)(2,1)S(1)}, u32[]{:S(2)}) copy-start(bf16[4,3,32,384]{3,2,1,0:T(8,128)(2,1)S(1)} %collective-permute-done.11.refs_1_) | copy-start | bytes 884740
  116.1 30.0 %collective-permute-start.14 = (bf16[3,512,384]{2,1,0:T(8,128)(2,1)}, bf16[3,512,384]{2,1,0:T(8,128)(2,1)S(1)}, u32[]{:S(2)}, u32[]{:S(2)}) collective-permute-start(bf16[3,512,384]{2,1,0:T(8,128)(2,1)} %shard_map.97.refs_0_), channel_id=1, source_target_pairs={{0,16},{16,32},{32,48},{48,0},{1,17},{17,33},{33,49},{49,1},{2,18}... | collective-permute-start | bytes 3538952 | tf_op jit(solution)/shard_map/ppermute | solution.py:311
  118.5 32.5 %collective-permute-start.15 = (bf16[3,512,384]{2,1,0:T(8,128)(2,1)}, bf16[3,512,384]{2,1,0:T(8,128)(2,1)S(1)}, u32[]{:S(2)}, u32[]{:S(2)}) collective-permute-start(bf16[3,512,384]{2,1,0:T(8,128)(2,1)} %shard_map.97.refs_0_), channel_id=1, source_target_pairs={{0,48},{16,0},{32,16},{48,32},{1,49},{17,1},{33,17},{49,33},{2,50}... | collective-permute-start | bytes 3538952 | tf_op jit(solution)/shard_map/ppermute | solution.py:311
  125.0 7.7 %collective-permute-start = (bf16[2,24,2048]{2,1,0:T(8,128)(2,1)}, bf16[2,24,2048]{2,1,0:T(8,128)(2,1)S(1)}, u32[]{:S(2)}, u32[]{:S(2)}) collective-permute-start(bf16[2,24,2048]{2,1,0:T(8,128)(2,1)} %get-tuple-element.43), channel_id=1, source_target_pairs={{0,64},{64,128},{128,192},{192,256},{256,320},{320,384},{384,448},... | collective-permute-start | bytes 589832 | tf_op jit(solution)/shard_map/ppermute | solution.py:311
  125.0 11.5 %collective-permute-start.1 = (bf16[2,24,2048]{2,1,0:T(8,128)(2,1)}, bf16[2,24,2048]{2,1,0:T(8,128)(2,1)S(1)}, u32[]{:S(2)}, u32[]{:S(2)}) collective-permute-start(bf16[2,24,2048]{2,1,0:T(8,128)(2,1)} %get-tuple-element.44), channel_id=1, source_target_pairs={{0,128},{64,192},{128,256},{192,320},{256,384},{320,448},{384,0},{... | collective-permute-start | bytes 589832 | tf_op jit(solution)/shard_map/ppermute | solution.py:311
  128.5 24.5 %collective-permute-start.2 = (bf16[2,24,2048]{2,1,0:T(8,128)(2,1)}, bf16[2,24,2048]{2,1,0:T(8,128)(2,1)S(1)}, u32[]{:S(2)}, u32[]{:S(2)}) collective-permute-start(bf16[2,24,2048]{2,1,0:T(8,128)(2,1)} %get-tuple-element.45), channel_id=1, source_target_pairs={{0,192},{64,256},{128,320},{192,384},{256,448},{320,0},{384,64},{4... | collective-permute-start | bytes 589832 | tf_op jit(solution)/shard_map/ppermute | solution.py:311
  132.7 26.2 %copy-start.25 = (bf16[2,24,2048]{2,1,0:T(8,128)(2,1)}, bf16[2,24,2048]{2,1,0:T(8,128)(2,1)S(1)}, u32[]{:S(2)}) copy-start(bf16[2,24,2048]{2,1,0:T(8,128)(2,1)S(1)} %collective-permute-done.refs_1_) | copy-start | bytes 589828
  132.7 23.9 %collective-permute-start.3 = (bf16[2,24,2048]{2,1,0:T(8,128)(2,1)}, bf16[2,24,2048]{2,1,0:T(8,128)(2,1)}, u32[]{:S(2)}, u32[]{:S(2)}) collective-permute-start(bf16[2,24,2048]{2,1,0:T(8,128)(2,1)} %get-tuple-element.46), channel_id=1, source_target_pairs={{0,256},{64,320},{128,384},{192,448},{256,0},{320,64},{384,128},{4... | collective-permute-start | bytes 589832 | tf_op jit(solution)/shard_map/ppermute | solution.py:311
  136.5 22.4 %copy-start.26 = (bf16[2,24,2048]{2,1,0:T(8,128)(2,1)}, bf16[2,24,2048]{2,1,0:T(8,128)(2,1)S(1)}, u32[]{:S(2)}) copy-start(bf16[2,24,2048]{2,1,0:T(8,128)(2,1)S(1)} %collective-permute-done.1.refs_2_) | copy-start | bytes 589828
  136.5 22.4 %collective-permute-start.4 = (bf16[2,24,2048]{2,1,0:T(8,128)(2,1)}, bf16[2,24,2048]{2,1,0:T(8,128)(2,1)}, u32[]{:S(2)}, u32[]{:S(2)}) collective-permute-start(bf16[2,24,2048]{2,1,0:T(8,128)(2,1)} %get-tuple-element.47), channel_id=1, source_target_pairs={{0,320},{64,384},{128,448},{192,0},{256,64},{320,128},{384,192},{4... | collective-permute-start | bytes 589832 | tf_op jit(solution)/shard_map/ppermute | solution.py:311
  146.1 20.5 %copy-start = (bf16[3,512,384]{2,1,0:T(8,128)(2,1)}, bf16[3,512,384]{2,1,0:T(8,128)(2,1)S(1)}, u32[]{:S(2)}) copy-start(bf16[3,512,384]{2,1,0:T(8,128)(2,1)S(1)} %collective-permute-done.14.refs_1_) | copy-start | bytes 3538948
  146.1 12.8 %collective-permute-start.5 = (bf16[2,24,2048]{2,1,0:T(8,128)(2,1)}, bf16[2,24,2048]{2,1,0:T(8,128)(2,1)}, u32[]{:S(2)}, u32[]{:S(2)}) collective-permute-start(bf16[2,24,2048]{2,1,0:T(8,128)(2,1)} %get-tuple-element.48), channel_id=1, source_target_pairs={{0,384},{64,448},{128,0},{192,64},{256,128},{320,192},{384,256},{4... | collective-permute-start | bytes 589832 | tf_op jit(solution)/shard_map/ppermute | solution.py:311
  151.0 15.6 %copy-start.1 = (bf16[3,512,384]{2,1,0:T(8,128)(2,1)}, bf16[3,512,384]{2,1,0:T(8,128)(2,1)S(1)}, u32[]{:S(2)}) copy-start(bf16[3,512,384]{2,1,0:T(8,128)(2,1)S(1)} %collective-permute-done.15.refs_2_) | copy-start | bytes 3538948
  151.1 7.9 %collective-permute-start.6 = (bf16[2,24,2048]{2,1,0:T(8,128)(2,1)}, bf16[2,24,2048]{2,1,0:T(8,128)(2,1)}, u32[]{:S(2)}, u32[]{:S(2)}) collective-permute-start(bf16[2,24,2048]{2,1,0:T(8,128)(2,1)} %get-tuple-element.49), channel_id=1, source_target_pairs={{0,448},{64,0},{128,64},{192,128},{256,192},{320,256},{384,320},{4... | collective-permute-start | bytes 589832 | tf_op jit(solution)/shard_map/ppermute | solution.py:311
  153.0 23.2 %collective-permute-start.16 = (bf16[3,256,384]{2,1,0:T(8,128)(2,1)}, bf16[3,256,384]{2,1,0:T(8,128)(2,1)S(1)}, u32[]{:S(2)}, u32[]{:S(2)}) collective-permute-start(bf16[3,256,384]{2,1,0:T(8,128)(2,1)} %slice.8), channel_id=1, source_target_pairs={{0,16},{16,32},{32,48},{48,0},{1,17},{17,33},{33,49},{49,1},{2,18}... | collective-permute-start | bytes 1769480 | tf_op jit(solution)/shard_map/ppermute | solution.py:311
  156.6 19.6 %collective-permute-start.17 = (bf16[3,256,384]{2,1,0:T(8,128)(2,1)}, bf16[3,256,384]{2,1,0:T(8,128)(2,1)S(1)}, u32[]{:S(2)}, u32[]{:S(2)}) collective-permute-start(bf16[3,256,384]{2,1,0:T(8,128)(2,1)} %slice.9), channel_id=1, source_target_pairs={{0,48},{16,0},{32,16},{48,32},{1,49},{17,1},{33,17},{49,33},{2,50}... | collective-permute-start | bytes 1769480 | tf_op jit(solution)/shard_map/ppermute | solution.py:311
  166.7 24.4 %collective-permute-start.25 = (bf16[512,384]{1,0:T(8,128)(2,1)}, bf16[512,384]{1,0:T(8,128)(2,1)S(1)}, u32[]{:S(2)}, u32[]{:S(2)}) collective-permute-start(bf16[512,384]{1,0:T(8,128)(2,1)} %get-tuple-element.68), channel_id=1, source_target_pairs={{0,16},{16,32},{32,48},{48,0},{1,17},{17,33},{33,49},{49,1},{2,18}... | collective-permute-start | bytes 1179656 | tf_op jit(solution)/shard_map/ppermute | solution.py:311
  171.5 21.6 %collective-permute-start.26 = (bf16[512,384]{1,0:T(8,128)(2,1)}, bf16[512,384]{1,0:T(8,128)(2,1)S(1)}, u32[]{:S(2)}, u32[]{:S(2)}) collective-permute-start(bf16[512,384]{1,0:T(8,128)(2,1)} %get-tuple-element.69), channel_id=1, source_target_pairs={{0,32},{16,48},{32,0},{48,16},{1,33},{17,49},{33,1},{49,17},{2,34}... | collective-permute-start | bytes 1179656 | tf_op jit(solution)/shard_map/ppermute | solution.py:311
  173.4 22.1 %collective-permute-start.27 = (bf16[512,384]{1,0:T(8,128)(2,1)}, bf16[512,384]{1,0:T(8,128)(2,1)S(1)}, u32[]{:S(2)}, u32[]{:S(2)}) collective-permute-start(bf16[512,384]{1,0:T(8,128)(2,1)} %get-tuple-element.70), channel_id=1, source_target_pairs={{0,48},{16,0},{32,16},{48,32},{1,49},{17,1},{33,17},{49,33},{2,50}... | collective-permute-start | bytes 1179656 | tf_op jit(solution)/shard_map/ppermute | solution.py:311
  182.6 22.8 %collective-permute-start.28 = (bf16[512,384]{1,0:T(8,128)(2,1)}, bf16[512,384]{1,0:T(8,128)(2,1)S(1)}, u32[]{:S(2)}, u32[]{:S(2)}) collective-permute-start(bf16[512,384]{1,0:T(8,128)(2,1)} %get-tuple-element.72), channel_id=1, source_target_pairs={{0,16},{16,32},{32,48},{48,0},{1,17},{17,33},{33,49},{49,1},{2,18}... | collective-permute-start | bytes 1179656 | tf_op jit(solution)/shard_map/ppermute | solution.py:311
  186.9 18.5 %collective-permute-start.29 = (bf16[512,384]{1,0:T(8,128)(2,1)}, bf16[512,384]{1,0:T(8,128)(2,1)S(1)}, u32[]{:S(2)}, u32[]{:S(2)}) collective-permute-start(bf16[512,384]{1,0:T(8,128)(2,1)} %get-tuple-element.73), channel_id=1, source_target_pairs={{0,32},{16,48},{32,0},{48,16},{1,33},{17,49},{33,1},{49,17},{2,34}... | collective-permute-start | bytes 1179656 | tf_op jit(solution)/shard_map/ppermute | solution.py:311
  191.1 19.8 %copy-start.6 = (bf16[512,384]{1,0:T(8,128)(2,1)}, bf16[512,384]{1,0:T(8,128)(2,1)S(1)}, u32[]{:S(2)}) copy-start(bf16[512,384]{1,0:T(8,128)(2,1)S(1)} %collective-permute-done.25.refs_1_) | copy-start | bytes 1179652
  191.1 19.8 %collective-permute-start.30 = (bf16[512,384]{1,0:T(8,128)(2,1)}, bf16[512,384]{1,0:T(8,128)(2,1)S(1)}, u32[]{:S(2)}, u32[]{:S(2)}) collective-permute-start(bf16[512,384]{1,0:T(8,128)(2,1)} %get-tuple-element.74), channel_id=1, source_target_pairs={{0,48},{16,0},{32,16},{48,32},{1,49},{17,1},{33,17},{49,33},{2,50}... | collective-permute-start | bytes 1179656 | tf_op jit(solution)/shard_map/ppermute | solution.py:311
  193.1 17.9 %copy-start.7 = (bf16[512,384]{1,0:T(8,128)(2,1)}, bf16[512,384]{1,0:T(8,128)(2,1)S(1)}, u32[]{:S(2)}) copy-start(bf16[512,384]{1,0:T(8,128)(2,1)S(1)} %collective-permute-done.26.refs_2_) | copy-start | bytes 1179652
  195.5 15.4 %copy-start.8 = (bf16[512,384]{1,0:T(8,128)(2,1)}, bf16[512,384]{1,0:T(8,128)(2,1)S(1)}, u32[]{:S(2)}) copy-start(bf16[512,384]{1,0:T(8,128)(2,1)S(1)} %collective-permute-done.27.refs_3_) | copy-start | bytes 1179652
  215.1 9.9 %collective-permute-start.31 = (bf16[2,4,32,384]{3,2,1,0:T(8,128)(2,1)}, bf16[2,4,32,384]{3,2,1,0:T(8,128)(2,1)S(1)}, u32[]{:S(2)}, u32[]{:S(2)}) collective-permute-start(bf16[2,4,32,384]{3,2,1,0:T(8,128)(2,1)} %get-tuple-element.76), channel_id=1, source_target_pairs={{0,1},{1,2},{2,3},{3,0},{4,5},{5,6},{6,7},{7,4},{8,9},{9,10},{10,1... | collective-permute-start | bytes 589832 | tf_op jit(solution)/shard_map/ppermute | solution.py:311
  217.0 17.5 %collective-permute-start.32 = (bf16[2,4,32,384]{3,2,1,0:T(8,128)(2,1)}, bf16[2,4,32,384]{3,2,1,0:T(8,128)(2,1)S(1)}, u32[]{:S(2)}, u32[]{:S(2)}) collective-permute-start(bf16[2,4,32,384]{3,2,1,0:T(8,128)(2,1)} %get-tuple-element.77), channel_id=1, source_target_pairs={{0,2},{1,3},{2,0},{3,1},{4,6},{5,7},{6,4},{7,5},{8,10},{9,11},{10,... | collective-permute-start | bytes 589832 | tf_op jit(solution)/shard_map/ppermute | solution.py:311
  218.9 16.3 %collective-permute-start.33 = (bf16[2,4,32,384]{3,2,1,0:T(8,128)(2,1)}, bf16[2,4,32,384]{3,2,1,0:T(8,128)(2,1)S(1)}, u32[]{:S(2)}, u32[]{:S(2)}) collective-permute-start(bf16[2,4,32,384]{3,2,1,0:T(8,128)(2,1)} %get-tuple-element.78), channel_id=1, source_target_pairs={{0,3},{1,0},{2,1},{3,2},{4,7},{5,4},{6,5},{7,6},{8,11},{9,8},{10,9... | collective-permute-start | bytes 589832 | tf_op jit(solution)/shard_map/ppermute | solution.py:311
  237.9 51.0 %all-to-all-start = ((bf16[8,32,384]{2,1,0:T(8,128)(2,1)}), bf16[8,32,384]{2,1,0:T(8,128)(2,1)S(1)}, u32[]{:S(2)}, u32[]{:S(2)}) async-start(bf16[8,32,384]{2,1,0:T(8,128)(2,1)} %get-tuple-element.80), calls=%async_computation | async-start | bytes 393216 | tf_op jit(solution)/shard_map/all_to_all | solution.py:378
  258.4 11.9 %collective-permute-start.18 = (bf16[2,24,2048]{2,1,0:T(8,128)(2,1)}, bf16[2,24,2048]{2,1,0:T(8,128)(2,1)S(1)}, u32[]{:S(2)}, u32[]{:S(2)}) collective-permute-start(bf16[2,24,2048]{2,1,0:T(8,128)(2,1)} %get-tuple-element.58), channel_id=1, source_target_pairs={{0,448},{64,0},{128,64},{192,128},{256,192},{320,256},{384,320},{4... | collective-permute-start | bytes 589832 | tf_op jit(solution)/shard_map/ppermute | solution.py:311
  258.6 14.8 %collective-permute-start.19 = (bf16[2,24,2048]{2,1,0:T(8,128)(2,1)}, bf16[2,24,2048]{2,1,0:T(8,128)(2,1)S(1)}, u32[]{:S(2)}, u32[]{:S(2)}) collective-permute-start(bf16[2,24,2048]{2,1,0:T(8,128)(2,1)} %get-tuple-element.59), channel_id=1, source_target_pairs={{0,384},{64,448},{128,0},{192,64},{256,128},{320,192},{384,256},{4... | collective-permute-start | bytes 589832 | tf_op jit(solution)/shard_map/ppermute | solution.py:311
  261.2 12.5 %collective-permute-start.20 = (bf16[2,24,2048]{2,1,0:T(8,128)(2,1)}, bf16[2,24,2048]{2,1,0:T(8,128)(2,1)S(1)}, u32[]{:S(2)}, u32[]{:S(2)}) collective-permute-start(bf16[2,24,2048]{2,1,0:T(8,128)(2,1)} %get-tuple-element.60), channel_id=1, source_target_pairs={{0,320},{64,384},{128,448},{192,0},{256,64},{320,128},{384,192},{4... | collective-permute-start | bytes 589832 | tf_op jit(solution)/shard_map/ppermute | solution.py:311
  263.2 11.3 %collective-permute-start.21 = (bf16[2,24,2048]{2,1,0:T(8,128)(2,1)}, bf16[2,24,2048]{2,1,0:T(8,128)(2,1)S(1)}, u32[]{:S(2)}, u32[]{:S(2)}) collective-permute-start(bf16[2,24,2048]{2,1,0:T(8,128)(2,1)} %get-tuple-element.61), channel_id=1, source_target_pairs={{0,256},{64,320},{128,384},{192,448},{256,0},{320,64},{384,128},{4... | collective-permute-start | bytes 589832 | tf_op jit(solution)/shard_map/ppermute | solution.py:311
  268.4 10.8 %collective-permute-start.22 = (bf16[2,24,2048]{2,1,0:T(8,128)(2,1)}, bf16[2,24,2048]{2,1,0:T(8,128)(2,1)S(1)}, u32[]{:S(2)}, u32[]{:S(2)}) collective-permute-start(bf16[2,24,2048]{2,1,0:T(8,128)(2,1)} %get-tuple-element.62), channel_id=1, source_target_pairs={{0,192},{64,256},{128,320},{192,384},{256,448},{320,0},{384,64},{4... | collective-permute-start | bytes 589832 | tf_op jit(solution)/shard_map/ppermute | solution.py:311
  270.4 14.9 %copy-start.18 = (bf16[2,24,2048]{2,1,0:T(8,128)(2,1)}, bf16[2,24,2048]{2,1,0:T(8,128)(2,1)S(1)}, u32[]{:S(2)}) copy-start(bf16[2,24,2048]{2,1,0:T(8,128)(2,1)S(1)} %collective-permute-done.18.refs_1_) | copy-start | bytes 589828
  270.4 13.5 %collective-permute-start.23 = (bf16[2,24,2048]{2,1,0:T(8,128)(2,1)}, bf16[2,24,2048]{2,1,0:T(8,128)(2,1)S(1)}, u32[]{:S(2)}, u32[]{:S(2)}) collective-permute-start(bf16[2,24,2048]{2,1,0:T(8,128)(2,1)} %get-tuple-element.63), channel_id=1, source_target_pairs={{0,128},{64,192},{128,256},{192,320},{256,384},{320,448},{384,0},{... | collective-permute-start | bytes 589832 | tf_op jit(solution)/shard_map/ppermute | solution.py:311
  273.4 11.9 %copy-start.19 = (bf16[2,24,2048]{2,1,0:T(8,128)(2,1)}, bf16[2,24,2048]{2,1,0:T(8,128)(2,1)S(1)}, u32[]{:S(2)}) copy-start(bf16[2,24,2048]{2,1,0:T(8,128)(2,1)S(1)} %collective-permute-done.19.refs_2_) | copy-start | bytes 589828
  273.5 11.8 %collective-permute-start.24 = (bf16[2,24,2048]{2,1,0:T(8,128)(2,1)}, bf16[2,24,2048]{2,1,0:T(8,128)(2,1)S(1)}, u32[]{:S(2)}, u32[]{:S(2)}) collective-permute-start(bf16[2,24,2048]{2,1,0:T(8,128)(2,1)} %get-tuple-element.64), channel_id=1, source_target_pairs={{0,64},{64,128},{128,192},{192,256},{256,320},{320,384},{384,448},... | collective-permute-start | bytes 589832 | tf_op jit(solution)/shard_map/ppermute | solution.py:311
  273.6 11.7 %copy-start.20 = (bf16[2,24,2048]{2,1,0:T(8,128)(2,1)}, bf16[2,24,2048]{2,1,0:T(8,128)(2,1)S(1)}, u32[]{:S(2)}) copy-start(bf16[2,24,2048]{2,1,0:T(8,128)(2,1)S(1)} %collective-permute-done.20.refs_3_) | copy-start | bytes 589828
  274.5 10.8 %copy-start.21 = (bf16[2,24,2048]{2,1,0:T(8,128)(2,1)}, bf16[2,24,2048]{2,1,0:T(8,128)(2,1)S(1)}, u32[]{:S(2)}) copy-start(bf16[2,24,2048]{2,1,0:T(8,128)(2,1)S(1)} %collective-permute-done.21.refs_4_) | copy-start | bytes 589828
  (15 other events, 46.0 us)

commit v4 on v3

--- a/solution.py
+++ b/solution.py
@@ -161,12 +161,12 @@
 
 
 def far_last_kernel(halves, parts, at_ref, grads_ref, gate_ref, up_ref, hidden_ref, o_ref, d_ref, *refs):
-    weights, outs = refs[:5], refs[5:]
+    pairs, downs, outs = refs[:5], refs[5:10], refs[10:]
     size = grads_ref.shape[1] // parts
     x = at_ref[1]
     dh = None
-    for start, ref, count in far_blocks(x, parts, size, weights):
-        part = dot(grads_ref[:, columns(start, count)], ref[2])
+    for start, ref, count in far_blocks(x, parts, size, downs):
+        part = dot(grads_ref[:, columns(start, count)], ref[0])
         dh = part if dh is None else dh + part
     gate, up = gate_ref[...], up_ref[...]
     keep = row_mask(1 - at_ref[0], gate.shape[0], halves, gate.shape[1])
@@ -174,9 +174,11 @@
     dgate, dup = input_grads(gate, up, sig, silu, dh, keep)
     hidden = hidden_ref[...]
     rows = outs[0].shape[1]
-    for start, ref, count in far_blocks(x, parts, size, weights):
+    for (start, down, count), (_, ref, _) in zip(
+        far_blocks(x, parts, size, downs), far_blocks(x, parts, size, pairs)
+    ):
         cols = columns(start, count)
-        out = dot(hidden, ref[2], 1, 1).astype(BF16) + o_ref[:, cols]
+        out = dot(hidden, down[0], 1, 1).astype(BF16) + o_ref[:, cols]
         dx = dot(dgate, ref[0], 1, 1) + dot(dup, ref[1], 1, 1)
         dx = dx.astype(BF16) + d_ref[:, cols]
         for k, out_ref in enumerate(outs):
@@ -305,7 +307,7 @@
         parts = []
         for p in pairs:
             parts.append(lax.ppermute(v, ("zh", "a"), p))
-        return jnp.stack(parts)
+        return parts
 
     def shift(v, name, size, k):
         return lax.ppermute(v, name, [(i, (i + k) % size) for i in range(size)])
@@ -326,7 +328,9 @@
         high = shift(right[:, half:], "x", nx, nx - 1)
         return v, left, right, low, high
 
-    far_weights = around(spread(cross(piece)))
+    crossed = lax.optimization_barrier(jnp.stack(cross(piece)))
+    pairs = around(spread(crossed[:, :2]))
+    downs = around(spread(crossed[:, 2:]))
 
     ids = expert_ids.reshape(1, count)
     ints = combine_ints.T
@@ -353,13 +357,13 @@
     gate, up, hidden, *far_parts = call(
         functools.partial(far_first_kernel, halves),
         (shape(slots, inner, dtype=F32),) * 2 + (shape(slots, inner),) + partial_shapes,
-        at, rows, grads, *far_weights, flops=3 * work,
+        at, rows, grads, *pairs, flops=3 * work,
     )
     far_sums = over_x(*far_parts)
     results = call(
         functools.partial(far_last_kernel, halves, nx),
         packet,
-        at, grads, gate, up, hidden, near_out, near_dx, *far_weights, flops=4 * work,
+        at, grads, gate, up, hidden, near_out, near_dx, *pairs, *downs, flops=4 * work,
     )
 
     own, *sends = call(

time: 292 us -> 332 us (1.14)
  the two profiles are of different devices: /device:TPU:38 before, /device:TPU:24 now
where the time goes in v4:
time: 332 us; the launch traced here: 327 us
  starting transfers between devices  174 us (52%)
  waiting for transfers between devices  106 us (32%)
  Pallas kernels  38 us (11%)
  local copies, waits for them, and re-layouts  7.56 us (2%)
    ppermute x37, starting transfers between devices, shift(): return lax.ppermute(v, name, [(i, (i + k) % size) for i in range(size)])  114 us
    ppermute x37, waiting for transfers between devices, shift(): return lax.ppermute(v, name, [(i, (i + k) % size) for i in range(size)])  71.4 us
    ppermute x4, starting transfers between devices, cross(): parts.append(lax.ppermute(v, ('zh', 'a'), p))  46.1 us
    pallas_call x10, Pallas kernels, raw_call(): pl.pallas_call(kernel, out_shape=outs, in_specs=[smem if scalar and k ==...  36.2 us
    ppermute x4, waiting for transfers between devices, cross(): parts.append(lax.ppermute(v, ('zh', 'a'), p))  34.2 us
    all_to_all x1, starting transfers between devices, step(): lax.all_to_all(send, ('zh', 'a'), split_axis=0, concat_axis=0, tiled=True)  14 us
    unnamed x72, local copies, waits for them, and re-layouts  6.73 us
  transfers between devices with their start and end apart: 42, of which 20 were waited for; matrix products, arithmetic and copies ran while one was open for 0% of the time, Pallas kernels for 8%

profile of v4, /device:TPU:24, one launch (start us, length us, event | category | flops | bytes accessed | tf_op | source)
XLA Modules:
  0.0 326.7 jit_solution(15123679062688398931)
XLA Ops:
  2.4 29.0 %collective-permute-start.7 = (bf16[3,32,384]{2,1,0:T(8,128)(2,1)}, bf16[3,32,384]{2,1,0:T(8,128)(2,1)S(1)}, u32[]{:S(2)}, u32[]{:S(2)}) collective-permute-start(bf16[3,32,384]{2,1,0:T(8,128)(2,1)} %shard_map.96), channel_id=1, source_target_pairs={{0,512},{4,516},{8,520},{12,524},{512,0},{516,4},{520,8},{524,12},... | collective-permute-start | bytes 221192 | tf_op jit(solution)/shard_map/ppermute | solution.py:309
  33.3 13.3 %collective-permute-start.9 = (bf16[3,32,384]{2,1,0:T(8,128)(2,1)}, bf16[3,32,384]{2,1,0:T(8,128)(2,1)S(1)}, u32[]{:S(2)}, u32[]{:S(2)}) collective-permute-start(bf16[3,32,384]{2,1,0:T(8,128)(2,1)} %shard_map.96), channel_id=1, source_target_pairs={{0,520},{4,524},{8,512},{12,516},{512,8},{516,12},{520,0},{524,4},... | collective-permute-start | bytes 221192 | tf_op jit(solution)/shard_map/ppermute | solution.py:309
  48.5 31.1 %collective-permute-done.8 = bf16[3,32,384]{2,1,0:T(8,128)(2,1)S(1)} collective-permute-done((bf16[3,32,384]{2,1,0:T(8,128)(2,1)}, bf16[3,32,384]{2,1,0:T(8,128)(2,1)S(1)}, u32[]{:S(2)}, u32[]{:S(2)}) %collective-permute-start.8) | collective-permute-done | bytes 73760 | tf_op jit(solution)/shard_map/ppermute | solution.py:309
  86.7 5.7 %collective-permute-start.13 = (bf16[4,2,32,384]{3,2,1,0:T(8,128)(2,1)S(1)}, bf16[4,2,32,384]{3,2,1,0:T(8,128)(2,1)S(1)}, u32[]{:S(2)}, u32[]{:S(2)}) collective-permute-start(bf16[4,2,32,384]{3,2,1,0:T(8,128)(2,1)S(1)} %slice.24.refs_0_), channel_id=1, source_target_pairs={{0,3},{1,0},{2,1},{3,2},{4,7},{5,4},{6,5},{7,6},{8,11},{9,8},{10,9... | collective-permute-start | bytes 589832 | tf_op jit(solution)/shard_map/ppermute | solution.py:313
  94.4 7.5 %collective-permute-done.12.refs_2_ = bf16[4,2,32,384]{3,2,1,0:T(8,128)(2,1)S(1)} collective-permute-done((bf16[4,2,32,384]{3,2,1,0:T(8,128)(2,1)S(1)}, bf16[4,2,32,384]{3,2,1,0:T(8,128)(2,1)S(1)}, u32[]{:S(2)}, u32[]{:S(2)}) %collective-permute-start.12) | collective-permute-done | bytes 196640 | tf_op jit(solution)/shard_map/ppermute | solution.py:313
  103.2 2.2 shard_map.97.refs_0_
  105.5 3.4 %collective-permute-start.14 = (bf16[2,512,384]{2,1,0:T(8,128)(2,1)}, bf16[2,512,384]{2,1,0:T(8,128)(2,1)S(1)}, u32[]{:S(2)}, u32[]{:S(2)}) collective-permute-start(bf16[2,512,384]{2,1,0:T(8,128)(2,1)} %shard_map.97.refs_0_), channel_id=1, source_target_pairs={{0,16},{16,32},{32,48},{48,0},{1,17},{17,33},{33,49},{49,1},{2,18}... | collective-permute-start | bytes 2359304 | tf_op jit(solution)/shard_map/ppermute | solution.py:313
  108.9 3.7 %collective-permute-start.15 = (bf16[2,512,384]{2,1,0:T(8,128)(2,1)}, bf16[2,512,384]{2,1,0:T(8,128)(2,1)S(1)}, u32[]{:S(2)}, u32[]{:S(2)}) collective-permute-start(bf16[2,512,384]{2,1,0:T(8,128)(2,1)} %shard_map.97.refs_0_), channel_id=1, source_target_pairs={{0,48},{16,0},{32,16},{48,32},{1,49},{17,1},{33,17},{49,33},{2,50}... | collective-permute-start | bytes 2359304 | tf_op jit(solution)/shard_map/ppermute | solution.py:313
  112.5 3.0 shard_map.94
  115.6 2.1 collective-permute-start.1
  117.7 4.5 %collective-permute-start.2 = (bf16[2,24,2048]{2,1,0:T(8,128)(2,1)}, bf16[2,24,2048]{2,1,0:T(8,128)(2,1)S(1)}, u32[]{:S(2)}, u32[]{:S(2)}) collective-permute-start(bf16[2,24,2048]{2,1,0:T(8,128)(2,1)} %get-tuple-element.45), channel_id=1, source_target_pairs={{0,192},{64,256},{128,320},{192,384},{256,448},{320,0},{384,64},{4... | collective-permute-start | bytes 589832 | tf_op jit(solution)/shard_map/ppermute | solution.py:313
  122.2 2.9 collective-permute-start.3
  125.4 3.6 %collective-permute-start.4 = (bf16[2,24,2048]{2,1,0:T(8,128)(2,1)}, bf16[2,24,2048]{2,1,0:T(8,128)(2,1)}, u32[]{:S(2)}, u32[]{:S(2)}) collective-permute-start(bf16[2,24,2048]{2,1,0:T(8,128)(2,1)} %get-tuple-element.47), channel_id=1, source_target_pairs={{0,320},{64,384},{128,448},{192,0},{256,64},{320,128},{384,192},{4... | collective-permute-start | bytes 589832 | tf_op jit(solution)/shard_map/ppermute | solution.py:313
  129.1 2.2 collective-permute-start.5
  132.1 2.2 collective-permute-start.16
  134.3 4.9 %collective-permute-start.17 = (bf16[2,256,384]{2,1,0:T(8,128)(2,1)S(1)}, bf16[2,256,384]{2,1,0:T(8,128)(2,1)S(1)}, u32[]{:S(2)}, u32[]{:S(2)}) collective-permute-start(bf16[2,256,384]{2,1,0:T(8,128)(2,1)S(1)} %slice.26), channel_id=1, source_target_pairs={{0,48},{16,0},{32,16},{48,32},{1,49},{17,1},{33,17},{49,33},{2,50}... | collective-permute-start | bytes 1179656 | tf_op jit(solution)/shard_map/ppermute | solution.py:313
  141.2 7.8 %shard_map.95 = (bf16[192,2048]{1,0:T(8,128)(2,1)}, bf16[192,2048]{1,0:T(8,128)(2,1)}, bf16[192,2048]{1,0:T(8,128)(2,1)}, bf16[192,2048]{1,0:T(8,128)(2,1)}, f32...) custom-call(s32[6]{0:T(128)} %stack.42.at_ref, ...), custom_call_target="tpu_custom_call" | custom-call | flops 2113929216 | bytes 11403288 | tf_op jit(solution)/shard_map/pallas_call | solution.py:255
  149.0 2.2 collective-permute-start.32
  151.2 4.7 %collective-permute-start.33 = (bf16[512,384]{1,0:T(8,128)(2,1)}, bf16[512,384]{1,0:T(8,128)(2,1)S(1)}, u32[]{:S(2)}, u32[]{:S(2)}) collective-permute-start(bf16[512,384]{1,0:T(8,128)(2,1)} %get-tuple-element.69), channel_id=1, source_target_pairs={{0,32},{16,48},{32,0},{48,16},{1,33},{17,49},{33,1},{49,17},{2,34}... | collective-permute-start | bytes 1179656 | tf_op jit(solution)/shard_map/ppermute | solution.py:313
  155.8 3.3 %collective-permute-start.34 = (bf16[512,384]{1,0:T(8,128)(2,1)}, bf16[512,384]{1,0:T(8,128)(2,1)S(1)}, u32[]{:S(2)}, u32[]{:S(2)}) collective-permute-start(bf16[512,384]{1,0:T(8,128)(2,1)} %get-tuple-element.70), channel_id=1, source_target_pairs={{0,48},{16,0},{32,16},{48,32},{1,49},{17,1},{33,17},{49,33},{2,50}... | collective-permute-start | bytes 1179656 | tf_op jit(solution)/shard_map/ppermute | solution.py:313
  160.1 4.9 %shard_map.98 = (f32[192,384]{1,0:T(8,128)}, f32[192,384]{1,0:T(8,128)}, bf16[192,384]{1,0:T(8,128)(2,1)}, f32[512,384]{1,0:T(8,128)}, bf16[512,384]{1,0:T(8,128...) custom-call(s32[6]{0:T(128)} %stack.42.at_ref, bf16[192,2048]{1,0:T(8,128)(2,1)} %get-tuple-element.51.rows_ref, ...), custom_call_target="tpu_custom_call" | custom-call | flops 905969664 | bytes 7421976 | tf_op jit(solution)/shard_map/pallas_call | solution.py:255
  165.1 2.5 collective-permute-start.35
  167.6 3.0 collective-permute-start.36
  170.6 4.5 %collective-permute-start.37 = (bf16[512,384]{1,0:T(8,128)(2,1)}, bf16[512,384]{1,0:T(8,128)(2,1)S(1)}, u32[]{:S(2)}, u32[]{:S(2)}) collective-permute-start(bf16[512,384]{1,0:T(8,128)(2,1)} %get-tuple-element.74), channel_id=1, source_target_pairs={{0,48},{16,0},{32,16},{48,32},{1,49},{17,1},{33,17},{49,33},{2,50}... | collective-permute-start | bytes 1179656 | tf_op jit(solution)/shard_map/ppermute | solution.py:313
  175.2 14.4 %collective-permute-done.35.refs_5_ = bf16[512,384]{1,0:T(8,128)(2,1)S(1)} collective-permute-done((bf16[512,384]{1,0:T(8,128)(2,1)}, bf16[512,384]{1,0:T(8,128)(2,1)S(1)}, u32[]{:S(2)}, u32[]{:S(2)}) %collective-permute-start.35) | collective-permute-done | bytes 393248 | tf_op jit(solution)/shard_map/ppermute | solution.py:313
  192.3 3.4 %shard_map.102 = (f32[2,4,32,384]{3,2,1,0:T(8,128)}, bf16[2,4,32,384]{3,2,1,0:T(8,128)(2,1)}, bf16[2,4,32,384]{3,2,1,0:T(8,128)(2,1)}, bf16[2,4,32,384]{3,2,1,0:T(8,128)(2,1)}) custom-call(s32[6]{0:T(128)} %stack.42.at_ref, f32[512,384]{1,0:T(8,128)} %get-tuple-element.67.refs_0_, bf16[512,384]{1,0:T(8,128)(2,1)} %copy-done.8, bf16[512,384]{1,0:T(8,128)(2,1)} %copy-done.9, ...), custom_call_target="tpu_custom_call" | custom-call | bytes 4915224 | tf_op jit(solution)/shard_map/pallas_call | solution.py:255
  195.7 5.9 %collective-permute-start.38 = (bf16[2,4,32,384]{3,2,1,0:T(8,128)(2,1)}, bf16[2,4,32,384]{3,2,1,0:T(8,128)(2,1)S(1)}, u32[]{:S(2)}, u32[]{:S(2)}) collective-permute-start(bf16[2,4,32,384]{3,2,1,0:T(8,128)(2,1)} %get-tuple-element.76), channel_id=1, source_target_pairs={{0,1},{1,2},{2,3},{3,0},{4,5},{5,6},{6,7},{7,4},{8,9},{9,10},{10,1... | collective-permute-start | bytes 589832 | tf_op jit(solution)/shard_map/ppermute | solution.py:313
  201.6 2.5 collective-permute-start.39
  204.2 3.7 %collective-permute-start.40 = (bf16[2,4,32,384]{3,2,1,0:T(8,128)(2,1)}, bf16[2,4,32,384]{3,2,1,0:T(8,128)(2,1)S(1)}, u32[]{:S(2)}, u32[]{:S(2)}) collective-permute-start(bf16[2,4,32,384]{3,2,1,0:T(8,128)(2,1)} %get-tuple-element.78), channel_id=1, source_target_pairs={{0,3},{1,0},{2,1},{3,2},{4,7},{5,4},{6,5},{7,6},{8,11},{9,8},{10,9... | collective-permute-start | bytes 589832 | tf_op jit(solution)/shard_map/ppermute | solution.py:313
  207.9 8.3 %collective-permute-done.39 = bf16[2,4,32,384]{3,2,1,0:T(8,128)(2,1)S(1)} collective-permute-done((bf16[2,4,32,384]{3,2,1,0:T(8,128)(2,1)}, bf16[2,4,32,384]{3,2,1,0:T(8,128)(2,1)S(1)}, u32[]{:S(2)}, u32[]{:S(2)}) %collective-permute-start.39) | collective-permute-done | bytes 196640 | tf_op jit(solution)/shard_map/ppermute | solution.py:313
  220.0 14.0 %all-to-all-start = ((bf16[8,32,384]{2,1,0:T(8,128)(2,1)}), bf16[8,32,384]{2,1,0:T(8,128)(2,1)S(1)}, u32[]{:S(2)}, u32[]{:S(2)}) async-start(bf16[8,32,384]{2,1,0:T(8,128)(2,1)} %get-tuple-element.80), calls=%async_computation | async-start | bytes 393216 | tf_op jit(solution)/shard_map/all_to_all | solution.py:382
  234.0 5.5 %collective-permute-start.18 = (bf16[4,1,32,384]{3,2,1,0:T(8,128)(2,1)S(1)}, bf16[4,1,32,384]{3,2,1,0:T(8,128)(2,1)S(1)}, u32[]{:S(2)}, u32[]{:S(2)}) collective-permute-start(bf16[4,1,32,384]{3,2,1,0:T(8,128)(2,1)S(1)} %slice.27.refs_0_), channel_id=1, source_target_pairs={{0,1},{1,2},{2,3},{3,0},{4,5},{5,6},{6,7},{7,4},{8,9},{9,10},{10,1... | collective-permute-start | bytes 294920 | tf_op jit(solution)/shard_map/ppermute | solution.py:313
  239.5 4.3 %collective-permute-start.19 = (bf16[4,1,32,384]{3,2,1,0:T(8,128)(2,1)S(1)}, bf16[4,1,32,384]{3,2,1,0:T(8,128)(2,1)S(1)}, u32[]{:S(2)}, u32[]{:S(2)}) collective-permute-start(bf16[4,1,32,384]{3,2,1,0:T(8,128)(2,1)S(1)} %slice.27.refs_0_), channel_id=1, source_target_pairs={{0,2},{1,3},{2,0},{3,1},{4,6},{5,7},{6,4},{7,5},{8,10},{9,11},{10,... | collective-permute-start | bytes 294920 | tf_op jit(solution)/shard_map/ppermute | solution.py:313
  245.7 9.4 %collective-permute-done.18.refs_1_ = bf16[4,1,32,384]{3,2,1,0:T(8,128)(2,1)S(1)} collective-permute-done((bf16[4,1,32,384]{3,2,1,0:T(8,128)(2,1)S(1)}, bf16[4,1,32,384]{3,2,1,0:T(8,128)(2,1)S(1)}, u32[]{:S(2)}, u32[]{:S(2)}) %collective-permute-start.18) | collective-permute-done | bytes 98336 | tf_op jit(solution)/shard_map/ppermute | solution.py:313
  255.1 4.5 %collective-permute-done.19.refs_2_ = bf16[4,1,32,384]{3,2,1,0:T(8,128)(2,1)S(1)} collective-permute-done((bf16[4,1,32,384]{3,2,1,0:T(8,128)(2,1)S(1)}, bf16[4,1,32,384]{3,2,1,0:T(8,128)(2,1)S(1)}, u32[]{:S(2)}, u32[]{:S(2)}) %collective-permute-start.19) | collective-permute-done | bytes 98336 | tf_op jit(solution)/shard_map/ppermute | solution.py:313
  262.7 2.3 collective-permute-start.21
  265.0 4.7 %collective-permute-start.22 = (bf16[1,512,384]{2,1,0:T(8,128)(2,1)}, bf16[1,512,384]{2,1,0:T(8,128)(2,1)S(1)}, u32[]{:S(2)}, u32[]{:S(2)}) collective-permute-start(bf16[1,512,384]{2,1,0:T(8,128)(2,1)} %shard_map.99.refs_5_), channel_id=1, source_target_pairs={{0,48},{16,0},{32,16},{48,32},{1,49},{17,1},{33,17},{49,33},{2,50}... | collective-permute-start | bytes 1179656 | tf_op jit(solution)/shard_map/ppermute | solution.py:313
  269.8 7.2 %collective-permute-done.21.refs_6_ = bf16[1,512,384]{2,1,0:T(8,128)(2,1)S(1)} collective-permute-done((bf16[1,512,384]{2,1,0:T(8,128)(2,1)}, bf16[1,512,384]{2,1,0:T(8,128)(2,1)S(1)}, u32[]{:S(2)}, u32[]{:S(2)}) %collective-permute-start.21) | collective-permute-done | bytes 393248 | tf_op jit(solution)/shard_map/ppermute | solution.py:313
  279.0 5.1 %collective-permute-start.24 = (bf16[1,256,384]{2,1,0:T(8,128)(2,1)S(1)}, bf16[1,256,384]{2,1,0:T(8,128)(2,1)S(1)}, u32[]{:S(2)}, u32[]{:S(2)}) collective-permute-start(bf16[1,256,384]{2,1,0:T(8,128)(2,1)S(1)} %slice.29), channel_id=1, source_target_pairs={{0,48},{16,0},{32,16},{48,32},{1,49},{17,1},{33,17},{49,33},{2,50}... | collective-permute-start | bytes 589832 | tf_op jit(solution)/shard_map/ppermute | solution.py:313
  288.0 6.4 %shard_map.100 = (bf16[2,24,2048]{2,1,0:T(8,128)(2,1)}, bf16[2,24,2048]{2,1,0:T(8,128)(2,1)}, bf16[2,24,2048]{2,1,0:T(8,128)(2,1)}, bf16[2,24,2048]{2,1,0:T(8,12...) custom-call(s32[6]{0:T(128)} %stack.42.at_ref, ...), custom_call_target="tpu_custom_call" | custom-call | flops 1207959552 | bytes 9388056 | tf_op jit(solution)/shard_map/pallas_call | solution.py:255
  296.3 3.4 %collective-permute-start.27 = (bf16[2,24,2048]{2,1,0:T(8,128)(2,1)}, bf16[2,24,2048]{2,1,0:T(8,128)(2,1)S(1)}, u32[]{:S(2)}, u32[]{:S(2)}) collective-permute-start(bf16[2,24,2048]{2,1,0:T(8,128)(2,1)} %get-tuple-element.60), channel_id=1, source_target_pairs={{0,320},{64,384},{128,448},{192,0},{256,64},{320,128},{384,192},{4... | collective-permute-start | bytes 589832 | tf_op jit(solution)/shard_map/ppermute | solution.py:313
  299.8 4.0 %collective-permute-start.28 = (bf16[2,24,2048]{2,1,0:T(8,128)(2,1)}, bf16[2,24,2048]{2,1,0:T(8,128)(2,1)S(1)}, u32[]{:S(2)}, u32[]{:S(2)}) collective-permute-start(bf16[2,24,2048]{2,1,0:T(8,128)(2,1)} %get-tuple-element.61), channel_id=1, source_target_pairs={{0,256},{64,320},{128,384},{192,448},{256,0},{320,64},{384,128},{4... | collective-permute-start | bytes 589832 | tf_op jit(solution)/shard_map/ppermute | solution.py:313
  303.8 2.6 collective-permute-start.29
  306.4 4.2 %collective-permute-start.30 = (bf16[2,24,2048]{2,1,0:T(8,128)(2,1)}, bf16[2,24,2048]{2,1,0:T(8,128)(2,1)S(1)}, u32[]{:S(2)}, u32[]{:S(2)}) collective-permute-start(bf16[2,24,2048]{2,1,0:T(8,128)(2,1)} %get-tuple-element.63), channel_id=1, source_target_pairs={{0,128},{64,192},{128,256},{192,320},{256,384},{320,448},{384,0},{... | collective-permute-start | bytes 589832 | tf_op jit(solution)/shard_map/ppermute | solution.py:313
  310.7 4.9 %collective-permute-done.27.refs_3_ = bf16[2,24,2048]{2,1,0:T(8,128)(2,1)S(1)} collective-permute-done((bf16[2,24,2048]{2,1,0:T(8,128)(2,1)}, bf16[2,24,2048]{2,1,0:T(8,128)(2,1)S(1)}, u32[]{:S(2)}, u32[]{:S(2)}) %collective-permute-start.27) | collective-permute-done | bytes 196640 | tf_op jit(solution)/shard_map/ppermute | solution.py:313
  315.6 3.0 collective-permute-done.30.refs_6_
  318.6 2.2 collective-permute-done.31.refs_7_
  321.4 2.9 shard_map.101
  (127 shorter events, 42.2 us)
Async XLA Ops:
  2.4 46.1 %collective-permute-start.7 = (bf16[3,32,384]{2,1,0:T(8,128)(2,1)}, bf16[3,32,384]{2,1,0:T(8,128)(2,1)S(1)}, u32[]{:S(2)}, u32[]{:S(2)}) collective-permute-start(bf16[3,32,384]{2,1,0:T(8,128)(2,1)} %shard_map.96), channel_id=1, source_target_pairs={{0,512},{4,516},{8,520},{12,524},{512,0},{516,4},{520,8},{524,12},... | collective-permute-start | bytes 221192 | tf_op jit(solution)/shard_map/ppermute | solution.py:309
  31.3 48.3 %collective-permute-start.8 = (bf16[3,32,384]{2,1,0:T(8,128)(2,1)}, bf16[3,32,384]{2,1,0:T(8,128)(2,1)S(1)}, u32[]{:S(2)}, u32[]{:S(2)}) collective-permute-start(bf16[3,32,384]{2,1,0:T(8,128)(2,1)} %shard_map.96), channel_id=1, source_target_pairs={{0,516},{4,520},{8,524},{12,512},{512,4},{516,8},{520,12},{524,0},... | collective-permute-start | bytes 221192 | tf_op jit(solution)/shard_map/ppermute | solution.py:309
  33.3 48.0 %collective-permute-start.9 = (bf16[3,32,384]{2,1,0:T(8,128)(2,1)}, bf16[3,32,384]{2,1,0:T(8,128)(2,1)S(1)}, u32[]{:S(2)}, u32[]{:S(2)}) collective-permute-start(bf16[3,32,384]{2,1,0:T(8,128)(2,1)} %shard_map.96), channel_id=1, source_target_pairs={{0,520},{4,524},{8,512},{12,516},{512,8},{516,12},{520,0},{524,4},... | collective-permute-start | bytes 221192 | tf_op jit(solution)/shard_map/ppermute | solution.py:309
  46.5 36.2 %collective-permute-start.10 = (bf16[3,32,384]{2,1,0:T(8,128)(2,1)}, bf16[3,32,384]{2,1,0:T(8,128)(2,1)S(1)}, u32[]{:S(2)}, u32[]{:S(2)}) collective-permute-start(bf16[3,32,384]{2,1,0:T(8,128)(2,1)} %shard_map.96), channel_id=1, source_target_pairs={{0,524},{4,512},{8,516},{12,520},{512,12},{516,0},{520,4},{524,8},... | collective-permute-start | bytes 221192 | tf_op jit(solution)/shard_map/ppermute | solution.py:309
  82.8 19.3 %copy-start.7 = (bf16[4,2,32,384]{3,2,1,0:T(8,128)(2,1)}, bf16[4,2,32,384]{3,2,1,0:T(8,128)(2,1)S(1)}, u32[]{:S(2)}) copy-start(bf16[4,2,32,384]{3,2,1,0:T(8,128)(2,1)S(1)} %slice.24.refs_0_) | copy-start | bytes 589828
  82.8 11.6 %collective-permute-start.11 = (bf16[4,2,32,384]{3,2,1,0:T(8,128)(2,1)S(1)}, bf16[4,2,32,384]{3,2,1,0:T(8,128)(2,1)S(1)}, u32[]{:S(2)}, u32[]{:S(2)}) collective-permute-start(bf16[4,2,32,384]{3,2,1,0:T(8,128)(2,1)S(1)} %slice.24.refs_0_), channel_id=1, source_target_pairs={{0,1},{1,2},{2,3},{3,0},{4,5},{5,6},{6,7},{7,4},{8,9},{9,10},{10,1... | collective-permute-start | bytes 589832 | tf_op jit(solution)/shard_map/ppermute | solution.py:313
  84.7 17.1 %collective-permute-start.12 = (bf16[4,2,32,384]{3,2,1,0:T(8,128)(2,1)S(1)}, bf16[4,2,32,384]{3,2,1,0:T(8,128)(2,1)S(1)}, u32[]{:S(2)}, u32[]{:S(2)}) collective-permute-start(bf16[4,2,32,384]{3,2,1,0:T(8,128)(2,1)S(1)} %slice.24.refs_0_), channel_id=1, source_target_pairs={{0,2},{1,3},{2,0},{3,1},{4,6},{5,7},{6,4},{7,5},{8,10},{9,11},{10,... | collective-permute-start | bytes 589832 | tf_op jit(solution)/shard_map/ppermute | solution.py:313
  86.7 15.5 %collective-permute-start.13 = (bf16[4,2,32,384]{3,2,1,0:T(8,128)(2,1)S(1)}, bf16[4,2,32,384]{3,2,1,0:T(8,128)(2,1)S(1)}, u32[]{:S(2)}, u32[]{:S(2)}) collective-permute-start(bf16[4,2,32,384]{3,2,1,0:T(8,128)(2,1)S(1)} %slice.24.refs_0_), channel_id=1, source_target_pairs={{0,3},{1,0},{2,1},{3,2},{4,7},{5,4},{6,5},{7,6},{8,11},{9,8},{10,9... | collective-permute-start | bytes 589832 | tf_op jit(solution)/shard_map/ppermute | solution.py:313
  105.5 23.6 %collective-permute-start.14 = (bf16[2,512,384]{2,1,0:T(8,128)(2,1)}, bf16[2,512,384]{2,1,0:T(8,128)(2,1)S(1)}, u32[]{:S(2)}, u32[]{:S(2)}) collective-permute-start(bf16[2,512,384]{2,1,0:T(8,128)(2,1)} %shard_map.97.refs_0_), channel_id=1, source_target_pairs={{0,16},{16,32},{32,48},{48,0},{1,17},{17,33},{33,49},{49,1},{2,18}... | collective-permute-start | bytes 2359304 | tf_op jit(solution)/shard_map/ppermute | solution.py:313
  108.9 22.4 %collective-permute-start.15 = (bf16[2,512,384]{2,1,0:T(8,128)(2,1)}, bf16[2,512,384]{2,1,0:T(8,128)(2,1)S(1)}, u32[]{:S(2)}, u32[]{:S(2)}) collective-permute-start(bf16[2,512,384]{2,1,0:T(8,128)(2,1)} %shard_map.97.refs_0_), channel_id=1, source_target_pairs={{0,48},{16,0},{32,16},{48,32},{1,49},{17,1},{33,17},{49,33},{2,50}... | collective-permute-start | bytes 2359304 | tf_op jit(solution)/shard_map/ppermute | solution.py:313
  115.6 6.6 %collective-permute-start = (bf16[2,24,2048]{2,1,0:T(8,128)(2,1)}, bf16[2,24,2048]{2,1,0:T(8,128)(2,1)S(1)}, u32[]{:S(2)}, u32[]{:S(2)}) collective-permute-start(bf16[2,24,2048]{2,1,0:T(8,128)(2,1)} %get-tuple-element.43), channel_id=1, source_target_pairs={{0,64},{64,128},{128,192},{192,256},{256,320},{320,384},{384,448},... | collective-permute-start | bytes 589832 | tf_op jit(solution)/shard_map/ppermute | solution.py:313
  115.6 9.9 %collective-permute-start.1 = (bf16[2,24,2048]{2,1,0:T(8,128)(2,1)}, bf16[2,24,2048]{2,1,0:T(8,128)(2,1)S(1)}, u32[]{:S(2)}, u32[]{:S(2)}) collective-permute-start(bf16[2,24,2048]{2,1,0:T(8,128)(2,1)} %get-tuple-element.44), channel_id=1, source_target_pairs={{0,128},{64,192},{128,256},{192,320},{256,384},{320,448},{384,0},{... | collective-permute-start | bytes 589832 | tf_op jit(solution)/shard_map/ppermute | solution.py:313
  117.7 14.4 %collective-permute-start.2 = (bf16[2,24,2048]{2,1,0:T(8,128)(2,1)}, bf16[2,24,2048]{2,1,0:T(8,128)(2,1)S(1)}, u32[]{:S(2)}, u32[]{:S(2)}) collective-permute-start(bf16[2,24,2048]{2,1,0:T(8,128)(2,1)} %get-tuple-element.45), channel_id=1, source_target_pairs={{0,192},{64,256},{128,320},{192,384},{256,448},{320,0},{384,64},{4... | collective-permute-start | bytes 589832 | tf_op jit(solution)/shard_map/ppermute | solution.py:313
  122.2 19.0 %copy-start.33 = (bf16[2,24,2048]{2,1,0:T(8,128)(2,1)}, bf16[2,24,2048]{2,1,0:T(8,128)(2,1)S(1)}, u32[]{:S(2)}) copy-start(bf16[2,24,2048]{2,1,0:T(8,128)(2,1)S(1)} %collective-permute-done.refs_1_) | copy-start | bytes 589828
  122.2 12.1 %collective-permute-start.3 = (bf16[2,24,2048]{2,1,0:T(8,128)(2,1)}, bf16[2,24,2048]{2,1,0:T(8,128)(2,1)}, u32[]{:S(2)}, u32[]{:S(2)}) collective-permute-start(bf16[2,24,2048]{2,1,0:T(8,128)(2,1)} %get-tuple-element.46), channel_id=1, source_target_pairs={{0,256},{64,320},{128,384},{192,448},{256,0},{320,64},{384,128},{4... | collective-permute-start | bytes 589832 | tf_op jit(solution)/shard_map/ppermute | solution.py:313
  125.4 13.8 %collective-permute-start.4 = (bf16[2,24,2048]{2,1,0:T(8,128)(2,1)}, bf16[2,24,2048]{2,1,0:T(8,128)(2,1)}, u32[]{:S(2)}, u32[]{:S(2)}) collective-permute-start(bf16[2,24,2048]{2,1,0:T(8,128)(2,1)} %get-tuple-element.47), channel_id=1, source_target_pairs={{0,320},{64,384},{128,448},{192,0},{256,64},{320,128},{384,192},{4... | collective-permute-start | bytes 589832 | tf_op jit(solution)/shard_map/ppermute | solution.py:313
  129.0 19.9 %copy-start = (bf16[2,512,384]{2,1,0:T(8,128)(2,1)}, bf16[2,512,384]{2,1,0:T(8,128)(2,1)S(1)}, u32[]{:S(2)}) copy-start(bf16[2,512,384]{2,1,0:T(8,128)(2,1)S(1)} %collective-permute-done.14.refs_1_) | copy-start | bytes 2359300
  129.1 12.1 %collective-permute-start.5 = (bf16[2,24,2048]{2,1,0:T(8,128)(2,1)}, bf16[2,24,2048]{2,1,0:T(8,128)(2,1)}, u32[]{:S(2)}, u32[]{:S(2)}) collective-permute-start(bf16[2,24,2048]{2,1,0:T(8,128)(2,1)} %get-tuple-element.48), channel_id=1, source_target_pairs={{0,384},{64,448},{128,0},{192,64},{256,128},{320,192},{384,256},{4... | collective-permute-start | bytes 589832 | tf_op jit(solution)/shard_map/ppermute | solution.py:313
  131.3 17.7 %copy-start.1 = (bf16[2,512,384]{2,1,0:T(8,128)(2,1)}, bf16[2,512,384]{2,1,0:T(8,128)(2,1)S(1)}, u32[]{:S(2)}) copy-start(bf16[2,512,384]{2,1,0:T(8,128)(2,1)S(1)} %collective-permute-done.15.refs_2_) | copy-start | bytes 2359300
  131.3 9.9 %collective-permute-start.6 = (bf16[2,24,2048]{2,1,0:T(8,128)(2,1)}, bf16[2,24,2048]{2,1,0:T(8,128)(2,1)}, u32[]{:S(2)}, u32[]{:S(2)}) collective-permute-start(bf16[2,24,2048]{2,1,0:T(8,128)(2,1)} %get-tuple-element.49), channel_id=1, source_target_pairs={{0,448},{64,0},{128,64},{192,128},{256,192},{320,256},{384,320},{4... | collective-permute-start | bytes 589832 | tf_op jit(solution)/shard_map/ppermute | solution.py:313
  132.1 27.0 %collective-permute-start.16 = (bf16[2,256,384]{2,1,0:T(8,128)(2,1)S(1)}, bf16[2,256,384]{2,1,0:T(8,128)(2,1)S(1)}, u32[]{:S(2)}, u32[]{:S(2)}) collective-permute-start(bf16[2,256,384]{2,1,0:T(8,128)(2,1)S(1)} %slice.25), channel_id=1, source_target_pairs={{0,16},{16,32},{32,48},{48,0},{1,17},{17,33},{33,49},{49,1},{2,18}... | collective-permute-start | bytes 1179656 | tf_op jit(solution)/shard_map/ppermute | solution.py:313
  134.3 24.9 %collective-permute-start.17 = (bf16[2,256,384]{2,1,0:T(8,128)(2,1)S(1)}, bf16[2,256,384]{2,1,0:T(8,128)(2,1)S(1)}, u32[]{:S(2)}, u32[]{:S(2)}) collective-permute-start(bf16[2,256,384]{2,1,0:T(8,128)(2,1)S(1)} %slice.26), channel_id=1, source_target_pairs={{0,48},{16,0},{32,16},{48,32},{1,49},{17,1},{33,17},{49,33},{2,50}... | collective-permute-start | bytes 1179656 | tf_op jit(solution)/shard_map/ppermute | solution.py:313
  149.0 21.6 %collective-permute-start.32 = (bf16[512,384]{1,0:T(8,128)(2,1)}, bf16[512,384]{1,0:T(8,128)(2,1)S(1)}, u32[]{:S(2)}, u32[]{:S(2)}) collective-permute-start(bf16[512,384]{1,0:T(8,128)(2,1)} %get-tuple-element.68), channel_id=1, source_target_pairs={{0,16},{16,32},{32,48},{48,0},{1,17},{17,33},{33,49},{49,1},{2,18}... | collective-permute-start | bytes 1179656 | tf_op jit(solution)/shard_map/ppermute | solution.py:313
  151.2 24.0 %collective-permute-start.33 = (bf16[512,384]{1,0:T(8,128)(2,1)}, bf16[512,384]{1,0:T(8,128)(2,1)S(1)}, u32[]{:S(2)}, u32[]{:S(2)}) collective-permute-start(bf16[512,384]{1,0:T(8,128)(2,1)} %get-tuple-element.69), channel_id=1, source_target_pairs={{0,32},{16,48},{32,0},{48,16},{1,33},{17,49},{33,1},{49,17},{2,34}... | collective-permute-start | bytes 1179656 | tf_op jit(solution)/shard_map/ppermute | solution.py:313
  155.8 19.4 %collective-permute-start.34 = (bf16[512,384]{1,0:T(8,128)(2,1)}, bf16[512,384]{1,0:T(8,128)(2,1)S(1)}, u32[]{:S(2)}, u32[]{:S(2)}) collective-permute-start(bf16[512,384]{1,0:T(8,128)(2,1)} %get-tuple-element.70), channel_id=1, source_target_pairs={{0,48},{16,0},{32,16},{48,32},{1,49},{17,1},{33,17},{49,33},{2,50}... | collective-permute-start | bytes 1179656 | tf_op jit(solution)/shard_map/ppermute | solution.py:313
  165.1 24.5 %collective-permute-start.35 = (bf16[512,384]{1,0:T(8,128)(2,1)}, bf16[512,384]{1,0:T(8,128)(2,1)S(1)}, u32[]{:S(2)}, u32[]{:S(2)}) collective-permute-start(bf16[512,384]{1,0:T(8,128)(2,1)} %get-tuple-element.72), channel_id=1, source_target_pairs={{0,16},{16,32},{32,48},{48,0},{1,17},{17,33},{33,49},{49,1},{2,18}... | collective-permute-start | bytes 1179656 | tf_op jit(solution)/shard_map/ppermute | solution.py:313
  167.6 22.0 %collective-permute-start.36 = (bf16[512,384]{1,0:T(8,128)(2,1)}, bf16[512,384]{1,0:T(8,128)(2,1)S(1)}, u32[]{:S(2)}, u32[]{:S(2)}) collective-permute-start(bf16[512,384]{1,0:T(8,128)(2,1)} %get-tuple-element.73), channel_id=1, source_target_pairs={{0,32},{16,48},{32,0},{48,16},{1,33},{17,49},{33,1},{49,17},{2,34}... | collective-permute-start | bytes 1179656 | tf_op jit(solution)/shard_map/ppermute | solution.py:313
  170.6 21.0 %copy-start.8 = (bf16[512,384]{1,0:T(8,128)(2,1)}, bf16[512,384]{1,0:T(8,128)(2,1)S(1)}, u32[]{:S(2)}) copy-start(bf16[512,384]{1,0:T(8,128)(2,1)S(1)} %collective-permute-done.32.refs_1_) | copy-start | bytes 1179652
  170.6 21.0 %collective-permute-start.37 = (bf16[512,384]{1,0:T(8,128)(2,1)}, bf16[512,384]{1,0:T(8,128)(2,1)S(1)}, u32[]{:S(2)}, u32[]{:S(2)}) collective-permute-start(bf16[512,384]{1,0:T(8,128)(2,1)} %get-tuple-element.74), channel_id=1, source_target_pairs={{0,48},{16,0},{32,16},{48,32},{1,49},{17,1},{33,17},{49,33},{2,50}... | collective-permute-start | bytes 1179656 | tf_op jit(solution)/shard_map/ppermute | solution.py:313
  195.7 12.1 %collective-permute-start.38 = (bf16[2,4,32,384]{3,2,1,0:T(8,128)(2,1)}, bf16[2,4,32,384]{3,2,1,0:T(8,128)(2,1)S(1)}, u32[]{:S(2)}, u32[]{:S(2)}) collective-permute-start(bf16[2,4,32,384]{3,2,1,0:T(8,128)(2,1)} %get-tuple-element.76), channel_id=1, source_target_pairs={{0,1},{1,2},{2,3},{3,0},{4,5},{5,6},{6,7},{7,4},{8,9},{9,10},{10,1... | collective-permute-start | bytes 589832 | tf_op jit(solution)/shard_map/ppermute | solution.py:313
  201.6 14.5 %collective-permute-start.39 = (bf16[2,4,32,384]{3,2,1,0:T(8,128)(2,1)}, bf16[2,4,32,384]{3,2,1,0:T(8,128)(2,1)S(1)}, u32[]{:S(2)}, u32[]{:S(2)}) collective-permute-start(bf16[2,4,32,384]{3,2,1,0:T(8,128)(2,1)} %get-tuple-element.77), channel_id=1, source_target_pairs={{0,2},{1,3},{2,0},{3,1},{4,6},{5,7},{6,4},{7,5},{8,10},{9,11},{10,... | collective-permute-start | bytes 589832 | tf_op jit(solution)/shard_map/ppermute | solution.py:313
  204.2 13.1 %collective-permute-start.40 = (bf16[2,4,32,384]{3,2,1,0:T(8,128)(2,1)}, bf16[2,4,32,384]{3,2,1,0:T(8,128)(2,1)S(1)}, u32[]{:S(2)}, u32[]{:S(2)}) collective-permute-start(bf16[2,4,32,384]{3,2,1,0:T(8,128)(2,1)} %get-tuple-element.78), channel_id=1, source_target_pairs={{0,3},{1,0},{2,1},{3,2},{4,7},{5,4},{6,5},{7,6},{8,11},{9,8},{10,9... | collective-permute-start | bytes 589832 | tf_op jit(solution)/shard_map/ppermute | solution.py:313
  220.0 104.4 %all-to-all-start = ((bf16[8,32,384]{2,1,0:T(8,128)(2,1)}), bf16[8,32,384]{2,1,0:T(8,128)(2,1)S(1)}, u32[]{:S(2)}, u32[]{:S(2)}) async-start(bf16[8,32,384]{2,1,0:T(8,128)(2,1)} %get-tuple-element.80), calls=%async_computation | async-start | bytes 393216 | tf_op jit(solution)/shard_map/all_to_all | solution.py:382
  234.0 25.6 %copy-start.14 = (bf16[4,1,32,384]{3,2,1,0:T(8,128)(2,1)}, bf16[4,1,32,384]{3,2,1,0:T(8,128)(2,1)S(1)}, u32[]{:S(2)}) copy-start(bf16[4,1,32,384]{3,2,1,0:T(8,128)(2,1)S(1)} %slice.27.refs_0_) | copy-start | bytes 294916
  234.0 21.1 %collective-permute-start.18 = (bf16[4,1,32,384]{3,2,1,0:T(8,128)(2,1)S(1)}, bf16[4,1,32,384]{3,2,1,0:T(8,128)(2,1)S(1)}, u32[]{:S(2)}, u32[]{:S(2)}) collective-permute-start(bf16[4,1,32,384]{3,2,1,0:T(8,128)(2,1)S(1)} %slice.27.refs_0_), channel_id=1, source_target_pairs={{0,1},{1,2},{2,3},{3,0},{4,5},{5,6},{6,7},{7,4},{8,9},{9,10},{10,1... | collective-permute-start | bytes 294920 | tf_op jit(solution)/shard_map/ppermute | solution.py:313
  239.5 20.1 %collective-permute-start.19 = (bf16[4,1,32,384]{3,2,1,0:T(8,128)(2,1)S(1)}, bf16[4,1,32,384]{3,2,1,0:T(8,128)(2,1)S(1)}, u32[]{:S(2)}, u32[]{:S(2)}) collective-permute-start(bf16[4,1,32,384]{3,2,1,0:T(8,128)(2,1)S(1)} %slice.27.refs_0_), channel_id=1, source_target_pairs={{0,2},{1,3},{2,0},{3,1},{4,6},{5,7},{6,4},{7,5},{8,10},{9,11},{10,... | collective-permute-start | bytes 294920 | tf_op jit(solution)/shard_map/ppermute | solution.py:313
  243.8 15.8 %collective-permute-start.20 = (bf16[4,1,32,384]{3,2,1,0:T(8,128)(2,1)S(1)}, bf16[4,1,32,384]{3,2,1,0:T(8,128)(2,1)S(1)}, u32[]{:S(2)}, u32[]{:S(2)}) collective-permute-start(bf16[4,1,32,384]{3,2,1,0:T(8,128)(2,1)S(1)} %slice.27.refs_0_), channel_id=1, source_target_pairs={{0,3},{1,0},{2,1},{3,2},{4,7},{5,4},{6,5},{7,6},{8,11},{9,8},{10,9... | collective-permute-start | bytes 294920 | tf_op jit(solution)/shard_map/ppermute | solution.py:313
  262.7 14.2 %collective-permute-start.21 = (bf16[1,512,384]{2,1,0:T(8,128)(2,1)}, bf16[1,512,384]{2,1,0:T(8,128)(2,1)S(1)}, u32[]{:S(2)}, u32[]{:S(2)}) collective-permute-start(bf16[1,512,384]{2,1,0:T(8,128)(2,1)} %shard_map.99.refs_5_), channel_id=1, source_target_pairs={{0,16},{16,32},{32,48},{48,0},{1,17},{17,33},{33,49},{49,1},{2,18}... | collective-permute-start | bytes 1179656 | tf_op jit(solution)/shard_map/ppermute | solution.py:313
  265.0 13.9 %collective-permute-start.22 = (bf16[1,512,384]{2,1,0:T(8,128)(2,1)}, bf16[1,512,384]{2,1,0:T(8,128)(2,1)S(1)}, u32[]{:S(2)}, u32[]{:S(2)}) collective-permute-start(bf16[1,512,384]{2,1,0:T(8,128)(2,1)} %shard_map.99.refs_5_), channel_id=1, source_target_pairs={{0,48},{16,0},{32,16},{48,32},{1,49},{17,1},{33,17},{49,33},{2,50}... | collective-permute-start | bytes 1179656 | tf_op jit(solution)/shard_map/ppermute | solution.py:313
  277.0 9.0 %collective-permute-start.23 = (bf16[1,256,384]{2,1,0:T(8,128)(2,1)S(1)}, bf16[1,256,384]{2,1,0:T(8,128)(2,1)S(1)}, u32[]{:S(2)}, u32[]{:S(2)}) collective-permute-start(bf16[1,256,384]{2,1,0:T(8,128)(2,1)S(1)} %slice.28), channel_id=1, source_target_pairs={{0,16},{16,32},{32,48},{48,0},{1,17},{17,33},{33,49},{49,1},{2,18}... | collective-permute-start | bytes 589832 | tf_op jit(solution)/shard_map/ppermute | solution.py:313
  279.0 8.3 %collective-permute-start.24 = (bf16[1,256,384]{2,1,0:T(8,128)(2,1)S(1)}, bf16[1,256,384]{2,1,0:T(8,128)(2,1)S(1)}, u32[]{:S(2)}, u32[]{:S(2)}) collective-permute-start(bf16[1,256,384]{2,1,0:T(8,128)(2,1)S(1)} %slice.29), channel_id=1, source_target_pairs={{0,48},{16,0},{32,16},{48,32},{1,49},{17,1},{33,17},{49,33},{2,50}... | collective-permute-start | bytes 589832 | tf_op jit(solution)/shard_map/ppermute | solution.py:313
  294.4 12.0 %collective-permute-start.25 = (bf16[2,24,2048]{2,1,0:T(8,128)(2,1)}, bf16[2,24,2048]{2,1,0:T(8,128)(2,1)S(1)}, u32[]{:S(2)}, u32[]{:S(2)}) collective-permute-start(bf16[2,24,2048]{2,1,0:T(8,128)(2,1)} %get-tuple-element.58), channel_id=1, source_target_pairs={{0,448},{64,0},{128,64},{192,128},{256,192},{320,256},{384,320},{4... | collective-permute-start | bytes 589832 | tf_op jit(solution)/shard_map/ppermute | solution.py:313
  294.4 16.2 %collective-permute-start.26 = (bf16[2,24,2048]{2,1,0:T(8,128)(2,1)}, bf16[2,24,2048]{2,1,0:T(8,128)(2,1)S(1)}, u32[]{:S(2)}, u32[]{:S(2)}) collective-permute-start(bf16[2,24,2048]{2,1,0:T(8,128)(2,1)} %get-tuple-element.59), channel_id=1, source_target_pairs={{0,384},{64,448},{128,0},{192,64},{256,128},{320,192},{384,256},{4... | collective-permute-start | bytes 589832 | tf_op jit(solution)/shard_map/ppermute | solution.py:313
  296.3 19.2 %collective-permute-start.27 = (bf16[2,24,2048]{2,1,0:T(8,128)(2,1)}, bf16[2,24,2048]{2,1,0:T(8,128)(2,1)S(1)}, u32[]{:S(2)}, u32[]{:S(2)}) collective-permute-start(bf16[2,24,2048]{2,1,0:T(8,128)(2,1)} %get-tuple-element.60), channel_id=1, source_target_pairs={{0,320},{64,384},{128,448},{192,0},{256,64},{320,128},{384,192},{4... | collective-permute-start | bytes 589832 | tf_op jit(solution)/shard_map/ppermute | solution.py:313
  299.8 15.8 %collective-permute-start.28 = (bf16[2,24,2048]{2,1,0:T(8,128)(2,1)}, bf16[2,24,2048]{2,1,0:T(8,128)(2,1)S(1)}, u32[]{:S(2)}, u32[]{:S(2)}) collective-permute-start(bf16[2,24,2048]{2,1,0:T(8,128)(2,1)} %get-tuple-element.61), channel_id=1, source_target_pairs={{0,256},{64,320},{128,384},{192,448},{256,0},{320,64},{384,128},{4... | collective-permute-start | bytes 589832 | tf_op jit(solution)/shard_map/ppermute | solution.py:313
  303.8 11.8 %collective-permute-start.29 = (bf16[2,24,2048]{2,1,0:T(8,128)(2,1)}, bf16[2,24,2048]{2,1,0:T(8,128)(2,1)S(1)}, u32[]{:S(2)}, u32[]{:S(2)}) collective-permute-start(bf16[2,24,2048]{2,1,0:T(8,128)(2,1)} %get-tuple-element.62), channel_id=1, source_target_pairs={{0,192},{64,256},{128,320},{192,384},{256,448},{320,0},{384,64},{4... | collective-permute-start | bytes 589832 | tf_op jit(solution)/shard_map/ppermute | solution.py:313
  306.4 12.2 %collective-permute-start.30 = (bf16[2,24,2048]{2,1,0:T(8,128)(2,1)}, bf16[2,24,2048]{2,1,0:T(8,128)(2,1)S(1)}, u32[]{:S(2)}, u32[]{:S(2)}) collective-permute-start(bf16[2,24,2048]{2,1,0:T(8,128)(2,1)} %get-tuple-element.63), channel_id=1, source_target_pairs={{0,128},{64,192},{128,256},{192,320},{256,384},{320,448},{384,0},{... | collective-permute-start | bytes 589832 | tf_op jit(solution)/shard_map/ppermute | solution.py:313
  310.6 10.1 %collective-permute-start.31 = (bf16[2,24,2048]{2,1,0:T(8,128)(2,1)}, bf16[2,24,2048]{2,1,0:T(8,128)(2,1)S(1)}, u32[]{:S(2)}, u32[]{:S(2)}) collective-permute-start(bf16[2,24,2048]{2,1,0:T(8,128)(2,1)} %get-tuple-element.64), channel_id=1, source_target_pairs={{0,64},{64,128},{128,192},{192,256},{256,320},{320,384},{384,448},... | collective-permute-start | bytes 589832 | tf_op jit(solution)/shard_map/ppermute | solution.py:313
  (30 other events, 154.6 us)

commit v5 on v4

--- a/solution.py
+++ b/solution.py
@@ -68,17 +68,21 @@
     din_ref[...] = dot(pick, grads, 0, 0).astype(BF16)
 
 
-def pieces_kernel(at_ref, gate_ref, up_ref, down_ref, out_ref):
-    rows = gate_ref.shape[0]
-    lanes = down_ref.shape[1]
-    shift = lax.rem(at_ref[0], lanes // rows) * rows
-    pick = (
-        lax.broadcasted_iota(jnp.int32, (rows, lanes), 1)
-        == lax.broadcasted_iota(jnp.int32, (rows, lanes), 0) + shift
-    ).astype(BF16)
-    out_ref[0] = gate_ref[...]
-    out_ref[1] = up_ref[...]
-    out_ref[2] = dot(pick, down_ref[...], 1, 1).astype(BF16)
+def pieces_kernel(at_ref, *refs):
+    ins, (own_ref, out_ref) = refs[:-2], refs[-2:]
+    for k in range(2):
+        gate_ref, up_ref, down_ref = ins[3 * k : 3 * k + 3]
+        rows = gate_ref.shape[0]
+        lanes = down_ref.shape[1]
+        shift = lax.rem(at_ref[k], lanes // rows) * rows
+        pick = (
+            lax.broadcasted_iota(jnp.int32, (rows, lanes), 1)
+            == lax.broadcasted_iota(jnp.int32, (rows, lanes), 0) + shift
+        ).astype(BF16)
+        out_ref[k, 0] = gate_ref[...]
+        out_ref[k, 1] = up_ref[...]
+        out_ref[k, 2] = dot(pick, down_ref[...], 1, 1).astype(BF16)
+    own_ref[...] = out_ref[0]
 
 
 def row_mask(half, count, halves, width):
@@ -276,38 +280,44 @@
     zh, x, a, b = (lax.axis_index(name).astype(jnp.int32) for name in ("zh", "x", "a", "b"))
     owner = lax.axis_index(("y", "c")).astype(jnp.int32)
     at = jnp.stack([zh, x, a, b, zh * quads + a, owner])
-    shard = ((x * quads + a) * nb + b).reshape(1)
+    away = jnp.where(a >= quads // 2, a - quads // 2, a + quads // 2)
+    shard = jnp.stack([(x * quads + quad) * nb + b for quad in (a, away)])
     w_gate, w_up, w_down = w_gate[0], w_up[0], w_down[0]
 
     per = 128 // depth
-    piece = pl.pallas_call(
+    piece, pieces = pl.pallas_call(
         pieces_kernel,
         grid_spec=pltpu.PrefetchScalarGridSpec(
             num_scalar_prefetch=1,
             grid=(1,),
             in_specs=[
-                pl.BlockSpec((depth, inner), lambda i, s: (s[0], 0)),
-                pl.BlockSpec((depth, inner), lambda i, s: (s[0], 0)),
-                pl.BlockSpec((inner, 128), lambda i, s: (0, lax.div(s[0], per))),
+                spec
+                for k in range(2)
+                for spec in (
+                    pl.BlockSpec((depth, inner), lambda i, s, k=k: (s[k], 0)),
+                    pl.BlockSpec((depth, inner), lambda i, s, k=k: (s[k], 0)),
+                    pl.BlockSpec((inner, 128), lambda i, s, k=k: (0, lax.div(s[k], per))),
+                )
             ],
-            out_specs=pl.BlockSpec((3, depth, inner), lambda i, s: (0, 0, 0)),
+            out_specs=[
+                pl.BlockSpec((3, depth, inner), lambda i, s: (0, 0, 0)),
+                pl.BlockSpec((2, 3, depth, inner), lambda i, s: (0, 0, 0, 0)),
+            ],
         ),
-        out_shape=shape(3, depth, inner),
-    )(shard, w_gate, w_up, w_down)
-
-    def cross(v):
-        pairs = [
-            [
+        out_shape=(shape(3, depth, inner), shape(2, 3, depth, inner)),
+    )(shard, *((w_gate, w_up, w_down) * 2))
+
+    def cross(own, two):
+        def hop(u, k):
+            pairs = [
                 (h * quads + i, (1 - h) * quads + (i + k) % quads)
                 for h in range(halves)
                 for i in range(quads)
             ]
-            for k in range(quads)
-        ]
-        parts = []
-        for p in pairs:
-            parts.append(lax.ppermute(v, ("zh", "a"), p))
-        return parts
+            return lax.ppermute(u, ("zh", "a"), pairs)
+
+        one, both, three = hop(own, 1), hop(two, 2), hop(own, 3)
+        return jnp.stack([both[1], one, both[0], three])
 
     def shift(v, name, size, k):
         return lax.ppermute(v, name, [(i, (i + k) % size) for i in range(size)])
@@ -328,7 +338,7 @@
         high = shift(right[:, half:], "x", nx, nx - 1)
         return v, left, right, low, high
 
-    crossed = lax.optimization_barrier(jnp.stack(cross(piece)))
+    crossed = lax.optimization_barrier(cross(piece, pieces))
     pairs = around(spread(crossed[:, :2]))
     downs = around(spread(crossed[:, 2:]))
 

time: 332 us -> 328 us (0.988)
  starting transfers between devices: 174 us -> 163 us
  waiting for transfers between devices: 106 us -> 112 us
    ppermute x4 -> x3, starting transfers between devices: 46.1 us -> 32.7 us  [hop(): return lax.ppermute(u, ('zh', 'a'), pairs)]
    ppermute x4 -> x3, waiting for transfers between devices: 34.2 us -> 41 us  [hop(): return lax.ppermute(u, ('zh', 'a'), pairs)]
  transfers between devices with their start and end apart: 42 -> 41, of which waited for: 20 -> 20; matrix products, arithmetic and copies ran while one was open for 0% -> 0% of each run, Pallas kernels for 8% -> 8%
where the time goes in v5:
time: 328 us; the launch traced here: 323 us
  starting transfers between devices  163 us (50%)
  waiting for transfers between devices  112 us (34%)
  Pallas kernels  38.8 us (12%)
  local copies, waits for them, and re-layouts  7.39 us (2%)
    ppermute x37, starting transfers between devices, shift(): return lax.ppermute(v, name, [(i, (i + k) % size) for i in range(size)])  114 us
    ppermute x37, waiting for transfers between devices, shift(): return lax.ppermute(v, name, [(i, (i + k) % size) for i in range(size)])  71.1 us
    ppermute x3, waiting for transfers between devices, hop(): return lax.ppermute(u, ('zh', 'a'), pairs)  41 us
    pallas_call x10, Pallas kernels, raw_call(): pl.pallas_call(kernel, out_shape=outs, in_specs=[smem if scalar and k ==...  36.3 us
    ppermute x3, starting transfers between devices, hop(): return lax.ppermute(u, ('zh', 'a'), pairs)  32.7 us
    all_to_all x1, starting transfers between devices, step(): lax.all_to_all(send, ('zh', 'a'), split_axis=0, concat_axis=0, tiled=True)  15.5 us
  transfers between devices with their start and end apart: 41, of which 20 were waited for; matrix products, arithmetic and copies ran while one was open for 0% of the time, Pallas kernels for 8%

profile of v5, /device:TPU:24, one launch (start us, length us, event | category | flops | bytes accessed | tf_op | source)
XLA Modules:
  0.0 323.1 jit_solution(3011280924713820166)
XLA Ops:
  1.2 2.5 shard_map.96
  3.8 23.0 %collective-permute-start.7 = (bf16[2,3,32,384]{3,2,1,0:T(8,128)(2,1)}, bf16[2,3,32,384]{3,2,1,0:T(8,128)(2,1)S(1)}, u32[]{:S(2)}, u32[]{:S(2)}) collective-permute-start(bf16[2,3,32,384]{3,2,1,0:T(8,128)(2,1)} %get-tuple-element.54), channel_id=1, source_target_pairs={{0,520},{4,524},{8,512},{12,516},{512,8},{516,12},{520,0},{524,4},... | collective-permute-start | bytes 442376 | tf_op jit(solution)/shard_map/ppermute | solution.py:317
  26.8 6.6 %collective-permute-start.8 = (bf16[3,32,384]{2,1,0:T(8,128)(2,1)}, bf16[3,32,384]{2,1,0:T(8,128)(2,1)S(1)}, u32[]{:S(2)}, u32[]{:S(2)}) collective-permute-start(bf16[3,32,384]{2,1,0:T(8,128)(2,1)} %get-tuple-element.55), channel_id=1, source_target_pairs={{0,516},{4,520},{8,524},{12,512},{512,4},{516,8},{520,12},{524,0},... | collective-permute-start | bytes 221192 | tf_op jit(solution)/shard_map/ppermute | solution.py:317
  33.4 3.1 collective-permute-start.9
  36.5 38.4 %collective-permute-done.7 = bf16[2,3,32,384]{3,2,1,0:T(8,128)(2,1)S(1)} collective-permute-done((bf16[2,3,32,384]{3,2,1,0:T(8,128)(2,1)}, bf16[2,3,32,384]{3,2,1,0:T(8,128)(2,1)S(1)}, u32[]{:S(2)}, u32[]{:S(2)}) %collective-permute-start.7) | collective-permute-done | bytes 147488 | tf_op jit(solution)/shard_map/ppermute | solution.py:317
  81.5 5.7 %collective-permute-start.12 = (bf16[4,2,32,384]{3,2,1,0:T(8,128)(2,1)S(1)}, bf16[4,2,32,384]{3,2,1,0:T(8,128)(2,1)S(1)}, u32[]{:S(2)}, u32[]{:S(2)}) collective-permute-start(bf16[4,2,32,384]{3,2,1,0:T(8,128)(2,1)S(1)} %slice.34.refs_0_), channel_id=1, source_target_pairs={{0,3},{1,0},{2,1},{3,2},{4,7},{5,4},{6,5},{7,6},{8,11},{9,8},{10,9... | collective-permute-start | bytes 589832 | tf_op jit(solution)/shard_map/ppermute | solution.py:323
  89.2 7.1 %collective-permute-done.11.refs_2_ = bf16[4,2,32,384]{3,2,1,0:T(8,128)(2,1)S(1)} collective-permute-done((bf16[4,2,32,384]{3,2,1,0:T(8,128)(2,1)S(1)}, bf16[4,2,32,384]{3,2,1,0:T(8,128)(2,1)S(1)}, u32[]{:S(2)}, u32[]{:S(2)}) %collective-permute-start.11) | collective-permute-done | bytes 196640 | tf_op jit(solution)/shard_map/ppermute | solution.py:323
  97.6 2.2 shard_map.97.refs_0_
  99.9 3.4 %collective-permute-start.13 = (bf16[2,512,384]{2,1,0:T(8,128)(2,1)}, bf16[2,512,384]{2,1,0:T(8,128)(2,1)S(1)}, u32[]{:S(2)}, u32[]{:S(2)}) collective-permute-start(bf16[2,512,384]{2,1,0:T(8,128)(2,1)} %shard_map.97.refs_0_), channel_id=1, source_target_pairs={{0,16},{16,32},{32,48},{48,0},{1,17},{17,33},{33,49},{49,1},{2,18}... | collective-permute-start | bytes 2359304 | tf_op jit(solution)/shard_map/ppermute | solution.py:323
  103.3 3.7 %collective-permute-start.14 = (bf16[2,512,384]{2,1,0:T(8,128)(2,1)}, bf16[2,512,384]{2,1,0:T(8,128)(2,1)S(1)}, u32[]{:S(2)}, u32[]{:S(2)}) collective-permute-start(bf16[2,512,384]{2,1,0:T(8,128)(2,1)} %shard_map.97.refs_0_), channel_id=1, source_target_pairs={{0,48},{16,0},{32,16},{48,32},{1,49},{17,1},{33,17},{49,33},{2,50}... | collective-permute-start | bytes 2359304 | tf_op jit(solution)/shard_map/ppermute | solution.py:323
  106.9 3.0 shard_map.94
  112.1 4.5 %collective-permute-start.2 = (bf16[2,24,2048]{2,1,0:T(8,128)(2,1)}, bf16[2,24,2048]{2,1,0:T(8,128)(2,1)S(1)}, u32[]{:S(2)}, u32[]{:S(2)}) collective-permute-start(bf16[2,24,2048]{2,1,0:T(8,128)(2,1)} %get-tuple-element.47), channel_id=1, source_target_pairs={{0,192},{64,256},{128,320},{192,384},{256,448},{320,0},{384,64},{4... | collective-permute-start | bytes 589832 | tf_op jit(solution)/shard_map/ppermute | solution.py:323
  116.6 2.9 collective-permute-start.3
  119.8 3.6 %collective-permute-start.4 = (bf16[2,24,2048]{2,1,0:T(8,128)(2,1)}, bf16[2,24,2048]{2,1,0:T(8,128)(2,1)}, u32[]{:S(2)}, u32[]{:S(2)}) collective-permute-start(bf16[2,24,2048]{2,1,0:T(8,128)(2,1)} %get-tuple-element.49), channel_id=1, source_target_pairs={{0,320},{64,384},{128,448},{192,0},{256,64},{320,128},{384,192},{4... | collective-permute-start | bytes 589832 | tf_op jit(solution)/shard_map/ppermute | solution.py:323
  123.5 2.2 collective-permute-start.5
  126.5 2.2 collective-permute-start.15
  128.8 4.9 %collective-permute-start.16 = (bf16[2,256,384]{2,1,0:T(8,128)(2,1)S(1)}, bf16[2,256,384]{2,1,0:T(8,128)(2,1)S(1)}, u32[]{:S(2)}, u32[]{:S(2)}) collective-permute-start(bf16[2,256,384]{2,1,0:T(8,128)(2,1)S(1)} %slice.36), channel_id=1, source_target_pairs={{0,48},{16,0},{32,16},{48,32},{1,49},{17,1},{33,17},{49,33},{2,50}... | collective-permute-start | bytes 1179656 | tf_op jit(solution)/shard_map/ppermute | solution.py:323
  135.6 7.8 %shard_map.95 = (bf16[192,2048]{1,0:T(8,128)(2,1)}, bf16[192,2048]{1,0:T(8,128)(2,1)}, bf16[192,2048]{1,0:T(8,128)(2,1)}, bf16[192,2048]{1,0:T(8,128)(2,1)}, f32...) custom-call(s32[6]{0:T(128)} %stack.45.at_ref, ...), custom_call_target="tpu_custom_call" | custom-call | flops 2113929216 | bytes 11403288 | tf_op jit(solution)/shard_map/pallas_call | solution.py:259
  143.4 2.2 collective-permute-start.31
  145.6 4.6 %collective-permute-start.32 = (bf16[512,384]{1,0:T(8,128)(2,1)}, bf16[512,384]{1,0:T(8,128)(2,1)S(1)}, u32[]{:S(2)}, u32[]{:S(2)}) collective-permute-start(bf16[512,384]{1,0:T(8,128)(2,1)} %get-tuple-element.73), channel_id=1, source_target_pairs={{0,32},{16,48},{32,0},{48,16},{1,33},{17,49},{33,1},{49,17},{2,34}... | collective-permute-start | bytes 1179656 | tf_op jit(solution)/shard_map/ppermute | solution.py:323
  150.2 3.4 %collective-permute-start.33 = (bf16[512,384]{1,0:T(8,128)(2,1)}, bf16[512,384]{1,0:T(8,128)(2,1)S(1)}, u32[]{:S(2)}, u32[]{:S(2)}) collective-permute-start(bf16[512,384]{1,0:T(8,128)(2,1)} %get-tuple-element.74), channel_id=1, source_target_pairs={{0,48},{16,0},{32,16},{48,32},{1,49},{17,1},{33,17},{49,33},{2,50}... | collective-permute-start | bytes 1179656 | tf_op jit(solution)/shard_map/ppermute | solution.py:323
  154.5 4.9 %shard_map.98 = (f32[192,384]{1,0:T(8,128)}, f32[192,384]{1,0:T(8,128)}, bf16[192,384]{1,0:T(8,128)(2,1)}, f32[512,384]{1,0:T(8,128)}, bf16[512,384]{1,0:T(8,128...) custom-call(s32[6]{0:T(128)} %stack.45.at_ref, bf16[192,2048]{1,0:T(8,128)(2,1)} %get-tuple-element.53.rows_ref, ...), custom_call_target="tpu_custom_call" | custom-call | flops 905969664 | bytes 7421976 | tf_op jit(solution)/shard_map/pallas_call | solution.py:259
  159.5 2.5 collective-permute-start.34
  162.0 3.0 collective-permute-start.35
  165.0 4.5 %collective-permute-start.36 = (bf16[512,384]{1,0:T(8,128)(2,1)}, bf16[512,384]{1,0:T(8,128)(2,1)S(1)}, u32[]{:S(2)}, u32[]{:S(2)}) collective-permute-start(bf16[512,384]{1,0:T(8,128)(2,1)} %get-tuple-element.78), channel_id=1, source_target_pairs={{0,48},{16,0},{32,16},{48,32},{1,49},{17,1},{33,17},{49,33},{2,50}... | collective-permute-start | bytes 1179656 | tf_op jit(solution)/shard_map/ppermute | solution.py:323
  169.6 14.4 %collective-permute-done.34.refs_5_ = bf16[512,384]{1,0:T(8,128)(2,1)S(1)} collective-permute-done((bf16[512,384]{1,0:T(8,128)(2,1)}, bf16[512,384]{1,0:T(8,128)(2,1)S(1)}, u32[]{:S(2)}, u32[]{:S(2)}) %collective-permute-start.34) | collective-permute-done | bytes 393248 | tf_op jit(solution)/shard_map/ppermute | solution.py:323
  186.8 3.4 %shard_map.102 = (f32[2,4,32,384]{3,2,1,0:T(8,128)}, bf16[2,4,32,384]{3,2,1,0:T(8,128)(2,1)}, bf16[2,4,32,384]{3,2,1,0:T(8,128)(2,1)}, bf16[2,4,32,384]{3,2,1,0:T(8,128)(2,1)}) custom-call(s32[6]{0:T(128)} %stack.45.at_ref, f32[512,384]{1,0:T(8,128)} %get-tuple-element.71.refs_0_, bf16[512,384]{1,0:T(8,128)(2,1)} %copy-done.8, bf16[512,384]{1,0:T(8,128)(2,1)} %copy-done.9, ...), custom_call_target="tpu_custom_call" | custom-call | bytes 4915224 | tf_op jit(solution)/shard_map/pallas_call | solution.py:259
  190.2 5.9 %collective-permute-start.37 = (bf16[2,4,32,384]{3,2,1,0:T(8,128)(2,1)}, bf16[2,4,32,384]{3,2,1,0:T(8,128)(2,1)S(1)}, u32[]{:S(2)}, u32[]{:S(2)}) collective-permute-start(bf16[2,4,32,384]{3,2,1,0:T(8,128)(2,1)} %get-tuple-element.80), channel_id=1, source_target_pairs={{0,1},{1,2},{2,3},{3,0},{4,5},{5,6},{6,7},{7,4},{8,9},{9,10},{10,1... | collective-permute-start | bytes 589832 | tf_op jit(solution)/shard_map/ppermute | solution.py:323
  196.1 2.3 collective-permute-start.38
  198.4 3.9 %collective-permute-start.39 = (bf16[2,4,32,384]{3,2,1,0:T(8,128)(2,1)}, bf16[2,4,32,384]{3,2,1,0:T(8,128)(2,1)S(1)}, u32[]{:S(2)}, u32[]{:S(2)}) collective-permute-start(bf16[2,4,32,384]{3,2,1,0:T(8,128)(2,1)} %get-tuple-element.82), channel_id=1, source_target_pairs={{0,3},{1,0},{2,1},{3,2},{4,7},{5,4},{6,5},{7,6},{8,11},{9,8},{10,9... | collective-permute-start | bytes 589832 | tf_op jit(solution)/shard_map/ppermute | solution.py:323
  202.3 8.0 %collective-permute-done.38 = bf16[2,4,32,384]{3,2,1,0:T(8,128)(2,1)S(1)} collective-permute-done((bf16[2,4,32,384]{3,2,1,0:T(8,128)(2,1)}, bf16[2,4,32,384]{3,2,1,0:T(8,128)(2,1)S(1)}, u32[]{:S(2)}, u32[]{:S(2)}) %collective-permute-start.38) | collective-permute-done | bytes 196640 | tf_op jit(solution)/shard_map/ppermute | solution.py:323
  214.2 15.5 %all-to-all-start = ((bf16[8,32,384]{2,1,0:T(8,128)(2,1)}), bf16[8,32,384]{2,1,0:T(8,128)(2,1)S(1)}, u32[]{:S(2)}, u32[]{:S(2)}) async-start(bf16[8,32,384]{2,1,0:T(8,128)(2,1)} %get-tuple-element.84), calls=%async_computation | async-start | bytes 393216 | tf_op jit(solution)/shard_map/all_to_all | solution.py:392
  229.8 5.5 %collective-permute-start.17 = (bf16[4,1,32,384]{3,2,1,0:T(8,128)(2,1)S(1)}, bf16[4,1,32,384]{3,2,1,0:T(8,128)(2,1)S(1)}, u32[]{:S(2)}, u32[]{:S(2)}) collective-permute-start(bf16[4,1,32,384]{3,2,1,0:T(8,128)(2,1)S(1)} %slice.37.refs_0_), channel_id=1, source_target_pairs={{0,1},{1,2},{2,3},{3,0},{4,5},{5,6},{6,7},{7,4},{8,9},{9,10},{10,1... | collective-permute-start | bytes 294920 | tf_op jit(solution)/shard_map/ppermute | solution.py:323
  235.3 4.5 %collective-permute-start.18 = (bf16[4,1,32,384]{3,2,1,0:T(8,128)(2,1)S(1)}, bf16[4,1,32,384]{3,2,1,0:T(8,128)(2,1)S(1)}, u32[]{:S(2)}, u32[]{:S(2)}) collective-permute-start(bf16[4,1,32,384]{3,2,1,0:T(8,128)(2,1)S(1)} %slice.37.refs_0_), channel_id=1, source_target_pairs={{0,2},{1,3},{2,0},{3,1},{4,6},{5,7},{6,4},{7,5},{8,10},{9,11},{10,... | collective-permute-start | bytes 294920 | tf_op jit(solution)/shard_map/ppermute | solution.py:323
  241.7 9.7 %collective-permute-done.17.refs_1_ = bf16[4,1,32,384]{3,2,1,0:T(8,128)(2,1)S(1)} collective-permute-done((bf16[4,1,32,384]{3,2,1,0:T(8,128)(2,1)S(1)}, bf16[4,1,32,384]{3,2,1,0:T(8,128)(2,1)S(1)}, u32[]{:S(2)}, u32[]{:S(2)}) %collective-permute-start.17) | collective-permute-done | bytes 98336 | tf_op jit(solution)/shard_map/ppermute | solution.py:323
  251.4 4.5 %collective-permute-done.18.refs_2_ = bf16[4,1,32,384]{3,2,1,0:T(8,128)(2,1)S(1)} collective-permute-done((bf16[4,1,32,384]{3,2,1,0:T(8,128)(2,1)S(1)}, bf16[4,1,32,384]{3,2,1,0:T(8,128)(2,1)S(1)}, u32[]{:S(2)}, u32[]{:S(2)}) %collective-permute-start.18) | collective-permute-done | bytes 98336 | tf_op jit(solution)/shard_map/ppermute | solution.py:323
  261.2 4.9 %collective-permute-start.21 = (bf16[1,512,384]{2,1,0:T(8,128)(2,1)}, bf16[1,512,384]{2,1,0:T(8,128)(2,1)S(1)}, u32[]{:S(2)}, u32[]{:S(2)}) collective-permute-start(bf16[1,512,384]{2,1,0:T(8,128)(2,1)} %shard_map.99.refs_5_), channel_id=1, source_target_pairs={{0,48},{16,0},{32,16},{48,32},{1,49},{17,1},{33,17},{49,33},{2,50}... | collective-permute-start | bytes 1179656 | tf_op jit(solution)/shard_map/ppermute | solution.py:323
  266.1 7.2 %collective-permute-done.20.refs_6_ = bf16[1,512,384]{2,1,0:T(8,128)(2,1)S(1)} collective-permute-done((bf16[1,512,384]{2,1,0:T(8,128)(2,1)}, bf16[1,512,384]{2,1,0:T(8,128)(2,1)S(1)}, u32[]{:S(2)}, u32[]{:S(2)}) %collective-permute-start.20) | collective-permute-done | bytes 393248 | tf_op jit(solution)/shard_map/ppermute | solution.py:323
  275.3 5.3 %collective-permute-start.23 = (bf16[1,256,384]{2,1,0:T(8,128)(2,1)S(1)}, bf16[1,256,384]{2,1,0:T(8,128)(2,1)S(1)}, u32[]{:S(2)}, u32[]{:S(2)}) collective-permute-start(bf16[1,256,384]{2,1,0:T(8,128)(2,1)S(1)} %slice.39), channel_id=1, source_target_pairs={{0,48},{16,0},{32,16},{48,32},{1,49},{17,1},{33,17},{49,33},{2,50}... | collective-permute-start | bytes 589832 | tf_op jit(solution)/shard_map/ppermute | solution.py:323
  284.3 6.5 %shard_map.100 = (bf16[2,24,2048]{2,1,0:T(8,128)(2,1)}, bf16[2,24,2048]{2,1,0:T(8,128)(2,1)}, bf16[2,24,2048]{2,1,0:T(8,128)(2,1)}, bf16[2,24,2048]{2,1,0:T(8,12...) custom-call(s32[6]{0:T(128)} %stack.45.at_ref, ...), custom_call_target="tpu_custom_call" | custom-call | flops 1207959552 | bytes 9388056 | tf_op jit(solution)/shard_map/pallas_call | solution.py:259
  292.7 3.2 %collective-permute-start.26 = (bf16[2,24,2048]{2,1,0:T(8,128)(2,1)}, bf16[2,24,2048]{2,1,0:T(8,128)(2,1)S(1)}, u32[]{:S(2)}, u32[]{:S(2)}) collective-permute-start(bf16[2,24,2048]{2,1,0:T(8,128)(2,1)} %get-tuple-element.64), channel_id=1, source_target_pairs={{0,320},{64,384},{128,448},{192,0},{256,64},{320,128},{384,192},{4... | collective-permute-start | bytes 589832 | tf_op jit(solution)/shard_map/ppermute | solution.py:323
  296.0 4.2 %collective-permute-start.27 = (bf16[2,24,2048]{2,1,0:T(8,128)(2,1)}, bf16[2,24,2048]{2,1,0:T(8,128)(2,1)S(1)}, u32[]{:S(2)}, u32[]{:S(2)}) collective-permute-start(bf16[2,24,2048]{2,1,0:T(8,128)(2,1)} %get-tuple-element.65), channel_id=1, source_target_pairs={{0,256},{64,320},{128,384},{192,448},{256,0},{320,64},{384,128},{4... | collective-permute-start | bytes 589832 | tf_op jit(solution)/shard_map/ppermute | solution.py:323
  300.2 2.5 collective-permute-start.28
  302.7 4.2 %collective-permute-start.29 = (bf16[2,24,2048]{2,1,0:T(8,128)(2,1)}, bf16[2,24,2048]{2,1,0:T(8,128)(2,1)S(1)}, u32[]{:S(2)}, u32[]{:S(2)}) collective-permute-start(bf16[2,24,2048]{2,1,0:T(8,128)(2,1)} %get-tuple-element.67), channel_id=1, source_target_pairs={{0,128},{64,192},{128,256},{192,320},{256,384},{320,448},{384,0},{... | collective-permute-start | bytes 589832 | tf_op jit(solution)/shard_map/ppermute | solution.py:323
  307.0 4.9 %collective-permute-done.26.refs_3_ = bf16[2,24,2048]{2,1,0:T(8,128)(2,1)S(1)} collective-permute-done((bf16[2,24,2048]{2,1,0:T(8,128)(2,1)}, bf16[2,24,2048]{2,1,0:T(8,128)(2,1)S(1)}, u32[]{:S(2)}, u32[]{:S(2)}) %collective-permute-start.26) | collective-permute-done | bytes 196640 | tf_op jit(solution)/shard_map/ppermute | solution.py:323
  312.0 3.0 collective-permute-done.29.refs_6_
  315.0 2.2 collective-permute-done.30.refs_7_
  317.8 2.9 shard_map.101
  (127 shorter events, 41.0 us)
Async XLA Ops:
  3.8 71.2 %collective-permute-start.7 = (bf16[2,3,32,384]{3,2,1,0:T(8,128)(2,1)}, bf16[2,3,32,384]{3,2,1,0:T(8,128)(2,1)S(1)}, u32[]{:S(2)}, u32[]{:S(2)}) collective-permute-start(bf16[2,3,32,384]{3,2,1,0:T(8,128)(2,1)} %get-tuple-element.54), channel_id=1, source_target_pairs={{0,520},{4,524},{8,512},{12,516},{512,8},{516,12},{520,0},{524,4},... | collective-permute-start | bytes 442376 | tf_op jit(solution)/shard_map/ppermute | solution.py:317
  26.8 49.8 %collective-permute-start.8 = (bf16[3,32,384]{2,1,0:T(8,128)(2,1)}, bf16[3,32,384]{2,1,0:T(8,128)(2,1)S(1)}, u32[]{:S(2)}, u32[]{:S(2)}) collective-permute-start(bf16[3,32,384]{2,1,0:T(8,128)(2,1)} %get-tuple-element.55), channel_id=1, source_target_pairs={{0,516},{4,520},{8,524},{12,512},{512,4},{516,8},{520,12},{524,0},... | collective-permute-start | bytes 221192 | tf_op jit(solution)/shard_map/ppermute | solution.py:317
  33.4 44.2 %collective-permute-start.9 = (bf16[3,32,384]{2,1,0:T(8,128)(2,1)}, bf16[3,32,384]{2,1,0:T(8,128)(2,1)S(1)}, u32[]{:S(2)}, u32[]{:S(2)}) collective-permute-start(bf16[3,32,384]{2,1,0:T(8,128)(2,1)} %get-tuple-element.55), channel_id=1, source_target_pairs={{0,524},{4,512},{8,516},{12,520},{512,12},{516,0},{520,4},{524,8},... | collective-permute-start | bytes 221192 | tf_op jit(solution)/shard_map/ppermute | solution.py:317
  77.7 19.1 %copy-start.7 = (bf16[4,2,32,384]{3,2,1,0:T(8,128)(2,1)}, bf16[4,2,32,384]{3,2,1,0:T(8,128)(2,1)S(1)}, u32[]{:S(2)}) copy-start(bf16[4,2,32,384]{3,2,1,0:T(8,128)(2,1)S(1)} %slice.34.refs_0_) | copy-start | bytes 589828
  77.7 11.6 %collective-permute-start.10 = (bf16[4,2,32,384]{3,2,1,0:T(8,128)(2,1)S(1)}, bf16[4,2,32,384]{3,2,1,0:T(8,128)(2,1)S(1)}, u32[]{:S(2)}, u32[]{:S(2)}) collective-permute-start(bf16[4,2,32,384]{3,2,1,0:T(8,128)(2,1)S(1)} %slice.34.refs_0_), channel_id=1, source_target_pairs={{0,1},{1,2},{2,3},{3,0},{4,5},{5,6},{6,7},{7,4},{8,9},{9,10},{10,1... | collective-permute-start | bytes 589832 | tf_op jit(solution)/shard_map/ppermute | solution.py:323
  79.6 16.7 %collective-permute-start.11 = (bf16[4,2,32,384]{3,2,1,0:T(8,128)(2,1)S(1)}, bf16[4,2,32,384]{3,2,1,0:T(8,128)(2,1)S(1)}, u32[]{:S(2)}, u32[]{:S(2)}) collective-permute-start(bf16[4,2,32,384]{3,2,1,0:T(8,128)(2,1)S(1)} %slice.34.refs_0_), channel_id=1, source_target_pairs={{0,2},{1,3},{2,0},{3,1},{4,6},{5,7},{6,4},{7,5},{8,10},{9,11},{10,... | collective-permute-start | bytes 589832 | tf_op jit(solution)/shard_map/ppermute | solution.py:323
  81.5 15.2 %collective-permute-start.12 = (bf16[4,2,32,384]{3,2,1,0:T(8,128)(2,1)S(1)}, bf16[4,2,32,384]{3,2,1,0:T(8,128)(2,1)S(1)}, u32[]{:S(2)}, u32[]{:S(2)}) collective-permute-start(bf16[4,2,32,384]{3,2,1,0:T(8,128)(2,1)S(1)} %slice.34.refs_0_), channel_id=1, source_target_pairs={{0,3},{1,0},{2,1},{3,2},{4,7},{5,4},{6,5},{7,6},{8,11},{9,8},{10,9... | collective-permute-start | bytes 589832 | tf_op jit(solution)/shard_map/ppermute | solution.py:323
  99.9 23.6 %collective-permute-start.13 = (bf16[2,512,384]{2,1,0:T(8,128)(2,1)}, bf16[2,512,384]{2,1,0:T(8,128)(2,1)S(1)}, u32[]{:S(2)}, u32[]{:S(2)}) collective-permute-start(bf16[2,512,384]{2,1,0:T(8,128)(2,1)} %shard_map.97.refs_0_), channel_id=1, source_target_pairs={{0,16},{16,32},{32,48},{48,0},{1,17},{17,33},{33,49},{49,1},{2,18}... | collective-permute-start | bytes 2359304 | tf_op jit(solution)/shard_map/ppermute | solution.py:323
  103.3 22.4 %collective-permute-start.14 = (bf16[2,512,384]{2,1,0:T(8,128)(2,1)}, bf16[2,512,384]{2,1,0:T(8,128)(2,1)S(1)}, u32[]{:S(2)}, u32[]{:S(2)}) collective-permute-start(bf16[2,512,384]{2,1,0:T(8,128)(2,1)} %shard_map.97.refs_0_), channel_id=1, source_target_pairs={{0,48},{16,0},{32,16},{48,32},{1,49},{17,1},{33,17},{49,33},{2,50}... | collective-permute-start | bytes 2359304 | tf_op jit(solution)/shard_map/ppermute | solution.py:323
  110.0 6.6 %collective-permute-start = (bf16[2,24,2048]{2,1,0:T(8,128)(2,1)}, bf16[2,24,2048]{2,1,0:T(8,128)(2,1)S(1)}, u32[]{:S(2)}, u32[]{:S(2)}) collective-permute-start(bf16[2,24,2048]{2,1,0:T(8,128)(2,1)} %get-tuple-element.45), channel_id=1, source_target_pairs={{0,64},{64,128},{128,192},{192,256},{256,320},{320,384},{384,448},... | collective-permute-start | bytes 589832 | tf_op jit(solution)/shard_map/ppermute | solution.py:323
  110.0 9.9 %collective-permute-start.1 = (bf16[2,24,2048]{2,1,0:T(8,128)(2,1)}, bf16[2,24,2048]{2,1,0:T(8,128)(2,1)S(1)}, u32[]{:S(2)}, u32[]{:S(2)}) collective-permute-start(bf16[2,24,2048]{2,1,0:T(8,128)(2,1)} %get-tuple-element.46), channel_id=1, source_target_pairs={{0,128},{64,192},{128,256},{192,320},{256,384},{320,448},{384,0},{... | collective-permute-start | bytes 589832 | tf_op jit(solution)/shard_map/ppermute | solution.py:323
  112.1 14.4 %collective-permute-start.2 = (bf16[2,24,2048]{2,1,0:T(8,128)(2,1)}, bf16[2,24,2048]{2,1,0:T(8,128)(2,1)S(1)}, u32[]{:S(2)}, u32[]{:S(2)}) collective-permute-start(bf16[2,24,2048]{2,1,0:T(8,128)(2,1)} %get-tuple-element.47), channel_id=1, source_target_pairs={{0,192},{64,256},{128,320},{192,384},{256,448},{320,0},{384,64},{4... | collective-permute-start | bytes 589832 | tf_op jit(solution)/shard_map/ppermute | solution.py:323
  116.6 19.0 %copy-start.33 = (bf16[2,24,2048]{2,1,0:T(8,128)(2,1)}, bf16[2,24,2048]{2,1,0:T(8,128)(2,1)S(1)}, u32[]{:S(2)}) copy-start(bf16[2,24,2048]{2,1,0:T(8,128)(2,1)S(1)} %collective-permute-done.refs_1_) | copy-start | bytes 589828
  116.6 12.1 %collective-permute-start.3 = (bf16[2,24,2048]{2,1,0:T(8,128)(2,1)}, bf16[2,24,2048]{2,1,0:T(8,128)(2,1)}, u32[]{:S(2)}, u32[]{:S(2)}) collective-permute-start(bf16[2,24,2048]{2,1,0:T(8,128)(2,1)} %get-tuple-element.48), channel_id=1, source_target_pairs={{0,256},{64,320},{128,384},{192,448},{256,0},{320,64},{384,128},{4... | collective-permute-start | bytes 589832 | tf_op jit(solution)/shard_map/ppermute | solution.py:323
  119.8 13.8 %collective-permute-start.4 = (bf16[2,24,2048]{2,1,0:T(8,128)(2,1)}, bf16[2,24,2048]{2,1,0:T(8,128)(2,1)}, u32[]{:S(2)}, u32[]{:S(2)}) collective-permute-start(bf16[2,24,2048]{2,1,0:T(8,128)(2,1)} %get-tuple-element.49), channel_id=1, source_target_pairs={{0,320},{64,384},{128,448},{192,0},{256,64},{320,128},{384,192},{4... | collective-permute-start | bytes 589832 | tf_op jit(solution)/shard_map/ppermute | solution.py:323
  123.5 19.9 %copy-start = (bf16[2,512,384]{2,1,0:T(8,128)(2,1)}, bf16[2,512,384]{2,1,0:T(8,128)(2,1)S(1)}, u32[]{:S(2)}) copy-start(bf16[2,512,384]{2,1,0:T(8,128)(2,1)S(1)} %collective-permute-done.13.refs_1_) | copy-start | bytes 2359300
  123.5 12.1 %collective-permute-start.5 = (bf16[2,24,2048]{2,1,0:T(8,128)(2,1)}, bf16[2,24,2048]{2,1,0:T(8,128)(2,1)}, u32[]{:S(2)}, u32[]{:S(2)}) collective-permute-start(bf16[2,24,2048]{2,1,0:T(8,128)(2,1)} %get-tuple-element.50), channel_id=1, source_target_pairs={{0,384},{64,448},{128,0},{192,64},{256,128},{320,192},{384,256},{4... | collective-permute-start | bytes 589832 | tf_op jit(solution)/shard_map/ppermute | solution.py:323
  125.7 17.7 %copy-start.1 = (bf16[2,512,384]{2,1,0:T(8,128)(2,1)}, bf16[2,512,384]{2,1,0:T(8,128)(2,1)S(1)}, u32[]{:S(2)}) copy-start(bf16[2,512,384]{2,1,0:T(8,128)(2,1)S(1)} %collective-permute-done.14.refs_2_) | copy-start | bytes 2359300
  125.7 9.9 %collective-permute-start.6 = (bf16[2,24,2048]{2,1,0:T(8,128)(2,1)}, bf16[2,24,2048]{2,1,0:T(8,128)(2,1)}, u32[]{:S(2)}, u32[]{:S(2)}) collective-permute-start(bf16[2,24,2048]{2,1,0:T(8,128)(2,1)} %get-tuple-element.51), channel_id=1, source_target_pairs={{0,448},{64,0},{128,64},{192,128},{256,192},{320,256},{384,320},{4... | collective-permute-start | bytes 589832 | tf_op jit(solution)/shard_map/ppermute | solution.py:323
  126.5 27.0 %collective-permute-start.15 = (bf16[2,256,384]{2,1,0:T(8,128)(2,1)S(1)}, bf16[2,256,384]{2,1,0:T(8,128)(2,1)S(1)}, u32[]{:S(2)}, u32[]{:S(2)}) collective-permute-start(bf16[2,256,384]{2,1,0:T(8,128)(2,1)S(1)} %slice.35), channel_id=1, source_target_pairs={{0,16},{16,32},{32,48},{48,0},{1,17},{17,33},{33,49},{49,1},{2,18}... | collective-permute-start | bytes 1179656 | tf_op jit(solution)/shard_map/ppermute | solution.py:323
  128.8 24.9 %collective-permute-start.16 = (bf16[2,256,384]{2,1,0:T(8,128)(2,1)S(1)}, bf16[2,256,384]{2,1,0:T(8,128)(2,1)S(1)}, u32[]{:S(2)}, u32[]{:S(2)}) collective-permute-start(bf16[2,256,384]{2,1,0:T(8,128)(2,1)S(1)} %slice.36), channel_id=1, source_target_pairs={{0,48},{16,0},{32,16},{48,32},{1,49},{17,1},{33,17},{49,33},{2,50}... | collective-permute-start | bytes 1179656 | tf_op jit(solution)/shard_map/ppermute | solution.py:323
  143.4 21.6 %collective-permute-start.31 = (bf16[512,384]{1,0:T(8,128)(2,1)}, bf16[512,384]{1,0:T(8,128)(2,1)S(1)}, u32[]{:S(2)}, u32[]{:S(2)}) collective-permute-start(bf16[512,384]{1,0:T(8,128)(2,1)} %get-tuple-element.72), channel_id=1, source_target_pairs={{0,16},{16,32},{32,48},{48,0},{1,17},{17,33},{33,49},{49,1},{2,18}... | collective-permute-start | bytes 1179656 | tf_op jit(solution)/shard_map/ppermute | solution.py:323
  145.6 24.0 %collective-permute-start.32 = (bf16[512,384]{1,0:T(8,128)(2,1)}, bf16[512,384]{1,0:T(8,128)(2,1)S(1)}, u32[]{:S(2)}, u32[]{:S(2)}) collective-permute-start(bf16[512,384]{1,0:T(8,128)(2,1)} %get-tuple-element.73), channel_id=1, source_target_pairs={{0,32},{16,48},{32,0},{48,16},{1,33},{17,49},{33,1},{49,17},{2,34}... | collective-permute-start | bytes 1179656 | tf_op jit(solution)/shard_map/ppermute | solution.py:323
  150.2 19.4 %collective-permute-start.33 = (bf16[512,384]{1,0:T(8,128)(2,1)}, bf16[512,384]{1,0:T(8,128)(2,1)S(1)}, u32[]{:S(2)}, u32[]{:S(2)}) collective-permute-start(bf16[512,384]{1,0:T(8,128)(2,1)} %get-tuple-element.74), channel_id=1, source_target_pairs={{0,48},{16,0},{32,16},{48,32},{1,49},{17,1},{33,17},{49,33},{2,50}... | collective-permute-start | bytes 1179656 | tf_op jit(solution)/shard_map/ppermute | solution.py:323
  159.5 24.5 %collective-permute-start.34 = (bf16[512,384]{1,0:T(8,128)(2,1)}, bf16[512,384]{1,0:T(8,128)(2,1)S(1)}, u32[]{:S(2)}, u32[]{:S(2)}) collective-permute-start(bf16[512,384]{1,0:T(8,128)(2,1)} %get-tuple-element.76), channel_id=1, source_target_pairs={{0,16},{16,32},{32,48},{48,0},{1,17},{17,33},{33,49},{49,1},{2,18}... | collective-permute-start | bytes 1179656 | tf_op jit(solution)/shard_map/ppermute | solution.py:323
  162.0 22.0 %collective-permute-start.35 = (bf16[512,384]{1,0:T(8,128)(2,1)}, bf16[512,384]{1,0:T(8,128)(2,1)S(1)}, u32[]{:S(2)}, u32[]{:S(2)}) collective-permute-start(bf16[512,384]{1,0:T(8,128)(2,1)} %get-tuple-element.77), channel_id=1, source_target_pairs={{0,32},{16,48},{32,0},{48,16},{1,33},{17,49},{33,1},{49,17},{2,34}... | collective-permute-start | bytes 1179656 | tf_op jit(solution)/shard_map/ppermute | solution.py:323
  165.0 21.0 %copy-start.8 = (bf16[512,384]{1,0:T(8,128)(2,1)}, bf16[512,384]{1,0:T(8,128)(2,1)S(1)}, u32[]{:S(2)}) copy-start(bf16[512,384]{1,0:T(8,128)(2,1)S(1)} %collective-permute-done.31.refs_1_) | copy-start | bytes 1179652
  165.0 21.0 %collective-permute-start.36 = (bf16[512,384]{1,0:T(8,128)(2,1)}, bf16[512,384]{1,0:T(8,128)(2,1)S(1)}, u32[]{:S(2)}, u32[]{:S(2)}) collective-permute-start(bf16[512,384]{1,0:T(8,128)(2,1)} %get-tuple-element.78), channel_id=1, source_target_pairs={{0,48},{16,0},{32,16},{48,32},{1,49},{17,1},{33,17},{49,33},{2,50}... | collective-permute-start | bytes 1179656 | tf_op jit(solution)/shard_map/ppermute | solution.py:323
  169.6 16.4 %copy-start.9 = (bf16[512,384]{1,0:T(8,128)(2,1)}, bf16[512,384]{1,0:T(8,128)(2,1)S(1)}, u32[]{:S(2)}) copy-start(bf16[512,384]{1,0:T(8,128)(2,1)S(1)} %collective-permute-done.32.refs_2_) | copy-start | bytes 1179652
  190.2 12.2 %collective-permute-start.37 = (bf16[2,4,32,384]{3,2,1,0:T(8,128)(2,1)}, bf16[2,4,32,384]{3,2,1,0:T(8,128)(2,1)S(1)}, u32[]{:S(2)}, u32[]{:S(2)}) collective-permute-start(bf16[2,4,32,384]{3,2,1,0:T(8,128)(2,1)} %get-tuple-element.80), channel_id=1, source_target_pairs={{0,1},{1,2},{2,3},{3,0},{4,5},{5,6},{6,7},{7,4},{8,9},{9,10},{10,1... | collective-permute-start | bytes 589832 | tf_op jit(solution)/shard_map/ppermute | solution.py:323
  196.1 14.2 %collective-permute-start.38 = (bf16[2,4,32,384]{3,2,1,0:T(8,128)(2,1)}, bf16[2,4,32,384]{3,2,1,0:T(8,128)(2,1)S(1)}, u32[]{:S(2)}, u32[]{:S(2)}) collective-permute-start(bf16[2,4,32,384]{3,2,1,0:T(8,128)(2,1)} %get-tuple-element.81), channel_id=1, source_target_pairs={{0,2},{1,3},{2,0},{3,1},{4,6},{5,7},{6,4},{7,5},{8,10},{9,11},{10,... | collective-permute-start | bytes 589832 | tf_op jit(solution)/shard_map/ppermute | solution.py:323
  198.4 13.1 %collective-permute-start.39 = (bf16[2,4,32,384]{3,2,1,0:T(8,128)(2,1)}, bf16[2,4,32,384]{3,2,1,0:T(8,128)(2,1)S(1)}, u32[]{:S(2)}, u32[]{:S(2)}) collective-permute-start(bf16[2,4,32,384]{3,2,1,0:T(8,128)(2,1)} %get-tuple-element.82), channel_id=1, source_target_pairs={{0,3},{1,0},{2,1},{3,2},{4,7},{5,4},{6,5},{7,6},{8,11},{9,8},{10,9... | collective-permute-start | bytes 589832 | tf_op jit(solution)/shard_map/ppermute | solution.py:323
  214.2 106.5 %all-to-all-start = ((bf16[8,32,384]{2,1,0:T(8,128)(2,1)}), bf16[8,32,384]{2,1,0:T(8,128)(2,1)S(1)}, u32[]{:S(2)}, u32[]{:S(2)}) async-start(bf16[8,32,384]{2,1,0:T(8,128)(2,1)} %get-tuple-element.84), calls=%async_computation | async-start | bytes 393216 | tf_op jit(solution)/shard_map/all_to_all | solution.py:392
  229.7 26.2 %copy-start.14 = (bf16[4,1,32,384]{3,2,1,0:T(8,128)(2,1)}, bf16[4,1,32,384]{3,2,1,0:T(8,128)(2,1)S(1)}, u32[]{:S(2)}) copy-start(bf16[4,1,32,384]{3,2,1,0:T(8,128)(2,1)S(1)} %slice.37.refs_0_) | copy-start | bytes 294916
  229.8 21.6 %collective-permute-start.17 = (bf16[4,1,32,384]{3,2,1,0:T(8,128)(2,1)S(1)}, bf16[4,1,32,384]{3,2,1,0:T(8,128)(2,1)S(1)}, u32[]{:S(2)}, u32[]{:S(2)}) collective-permute-start(bf16[4,1,32,384]{3,2,1,0:T(8,128)(2,1)S(1)} %slice.37.refs_0_), channel_id=1, source_target_pairs={{0,1},{1,2},{2,3},{3,0},{4,5},{5,6},{6,7},{7,4},{8,9},{9,10},{10,1... | collective-permute-start | bytes 294920 | tf_op jit(solution)/shard_map/ppermute | solution.py:323
  235.3 20.6 %collective-permute-start.18 = (bf16[4,1,32,384]{3,2,1,0:T(8,128)(2,1)S(1)}, bf16[4,1,32,384]{3,2,1,0:T(8,128)(2,1)S(1)}, u32[]{:S(2)}, u32[]{:S(2)}) collective-permute-start(bf16[4,1,32,384]{3,2,1,0:T(8,128)(2,1)S(1)} %slice.37.refs_0_), channel_id=1, source_target_pairs={{0,2},{1,3},{2,0},{3,1},{4,6},{5,7},{6,4},{7,5},{8,10},{9,11},{10,... | collective-permute-start | bytes 294920 | tf_op jit(solution)/shard_map/ppermute | solution.py:323
  239.8 16.1 %collective-permute-start.19 = (bf16[4,1,32,384]{3,2,1,0:T(8,128)(2,1)S(1)}, bf16[4,1,32,384]{3,2,1,0:T(8,128)(2,1)S(1)}, u32[]{:S(2)}, u32[]{:S(2)}) collective-permute-start(bf16[4,1,32,384]{3,2,1,0:T(8,128)(2,1)S(1)} %slice.37.refs_0_), channel_id=1, source_target_pairs={{0,3},{1,0},{2,1},{3,2},{4,7},{5,4},{6,5},{7,6},{8,11},{9,8},{10,9... | collective-permute-start | bytes 294920 | tf_op jit(solution)/shard_map/ppermute | solution.py:323
  259.1 14.2 %collective-permute-start.20 = (bf16[1,512,384]{2,1,0:T(8,128)(2,1)}, bf16[1,512,384]{2,1,0:T(8,128)(2,1)S(1)}, u32[]{:S(2)}, u32[]{:S(2)}) collective-permute-start(bf16[1,512,384]{2,1,0:T(8,128)(2,1)} %shard_map.99.refs_5_), channel_id=1, source_target_pairs={{0,16},{16,32},{32,48},{48,0},{1,17},{17,33},{33,49},{49,1},{2,18}... | collective-permute-start | bytes 1179656 | tf_op jit(solution)/shard_map/ppermute | solution.py:323
  261.2 14.0 %collective-permute-start.21 = (bf16[1,512,384]{2,1,0:T(8,128)(2,1)}, bf16[1,512,384]{2,1,0:T(8,128)(2,1)S(1)}, u32[]{:S(2)}, u32[]{:S(2)}) collective-permute-start(bf16[1,512,384]{2,1,0:T(8,128)(2,1)} %shard_map.99.refs_5_), channel_id=1, source_target_pairs={{0,48},{16,0},{32,16},{48,32},{1,49},{17,1},{33,17},{49,33},{2,50}... | collective-permute-start | bytes 1179656 | tf_op jit(solution)/shard_map/ppermute | solution.py:323
  273.3 9.0 %collective-permute-start.22 = (bf16[1,256,384]{2,1,0:T(8,128)(2,1)S(1)}, bf16[1,256,384]{2,1,0:T(8,128)(2,1)S(1)}, u32[]{:S(2)}, u32[]{:S(2)}) collective-permute-start(bf16[1,256,384]{2,1,0:T(8,128)(2,1)S(1)} %slice.38), channel_id=1, source_target_pairs={{0,16},{16,32},{32,48},{48,0},{1,17},{17,33},{33,49},{49,1},{2,18}... | collective-permute-start | bytes 589832 | tf_op jit(solution)/shard_map/ppermute | solution.py:323
  275.3 8.3 %collective-permute-start.23 = (bf16[1,256,384]{2,1,0:T(8,128)(2,1)S(1)}, bf16[1,256,384]{2,1,0:T(8,128)(2,1)S(1)}, u32[]{:S(2)}, u32[]{:S(2)}) collective-permute-start(bf16[1,256,384]{2,1,0:T(8,128)(2,1)S(1)} %slice.39), channel_id=1, source_target_pairs={{0,48},{16,0},{32,16},{48,32},{1,49},{17,1},{33,17},{49,33},{2,50}... | collective-permute-start | bytes 589832 | tf_op jit(solution)/shard_map/ppermute | solution.py:323
  290.8 11.9 %collective-permute-start.24 = (bf16[2,24,2048]{2,1,0:T(8,128)(2,1)}, bf16[2,24,2048]{2,1,0:T(8,128)(2,1)S(1)}, u32[]{:S(2)}, u32[]{:S(2)}) collective-permute-start(bf16[2,24,2048]{2,1,0:T(8,128)(2,1)} %get-tuple-element.62), channel_id=1, source_target_pairs={{0,448},{64,0},{128,64},{192,128},{256,192},{320,256},{384,320},{4... | collective-permute-start | bytes 589832 | tf_op jit(solution)/shard_map/ppermute | solution.py:323
  290.8 16.2 %collective-permute-start.25 = (bf16[2,24,2048]{2,1,0:T(8,128)(2,1)}, bf16[2,24,2048]{2,1,0:T(8,128)(2,1)S(1)}, u32[]{:S(2)}, u32[]{:S(2)}) collective-permute-start(bf16[2,24,2048]{2,1,0:T(8,128)(2,1)} %get-tuple-element.63), channel_id=1, source_target_pairs={{0,384},{64,448},{128,0},{192,64},{256,128},{320,192},{384,256},{4... | collective-permute-start | bytes 589832 | tf_op jit(solution)/shard_map/ppermute | solution.py:323
  292.7 19.2 %collective-permute-start.26 = (bf16[2,24,2048]{2,1,0:T(8,128)(2,1)}, bf16[2,24,2048]{2,1,0:T(8,128)(2,1)S(1)}, u32[]{:S(2)}, u32[]{:S(2)}) collective-permute-start(bf16[2,24,2048]{2,1,0:T(8,128)(2,1)} %get-tuple-element.64), channel_id=1, source_target_pairs={{0,320},{64,384},{128,448},{192,0},{256,64},{320,128},{384,192},{4... | collective-permute-start | bytes 589832 | tf_op jit(solution)/shard_map/ppermute | solution.py:323
  296.0 16.0 %collective-permute-start.27 = (bf16[2,24,2048]{2,1,0:T(8,128)(2,1)}, bf16[2,24,2048]{2,1,0:T(8,128)(2,1)S(1)}, u32[]{:S(2)}, u32[]{:S(2)}) collective-permute-start(bf16[2,24,2048]{2,1,0:T(8,128)(2,1)} %get-tuple-element.65), channel_id=1, source_target_pairs={{0,256},{64,320},{128,384},{192,448},{256,0},{320,64},{384,128},{4... | collective-permute-start | bytes 589832 | tf_op jit(solution)/shard_map/ppermute | solution.py:323
  300.2 11.8 %collective-permute-start.28 = (bf16[2,24,2048]{2,1,0:T(8,128)(2,1)}, bf16[2,24,2048]{2,1,0:T(8,128)(2,1)S(1)}, u32[]{:S(2)}, u32[]{:S(2)}) collective-permute-start(bf16[2,24,2048]{2,1,0:T(8,128)(2,1)} %get-tuple-element.66), channel_id=1, source_target_pairs={{0,192},{64,256},{128,320},{192,384},{256,448},{320,0},{384,64},{4... | collective-permute-start | bytes 589832 | tf_op jit(solution)/shard_map/ppermute | solution.py:323
  302.7 12.2 %collective-permute-start.29 = (bf16[2,24,2048]{2,1,0:T(8,128)(2,1)}, bf16[2,24,2048]{2,1,0:T(8,128)(2,1)S(1)}, u32[]{:S(2)}, u32[]{:S(2)}) collective-permute-start(bf16[2,24,2048]{2,1,0:T(8,128)(2,1)} %get-tuple-element.67), channel_id=1, source_target_pairs={{0,128},{64,192},{128,256},{192,320},{256,384},{320,448},{384,0},{... | collective-permute-start | bytes 589832 | tf_op jit(solution)/shard_map/ppermute | solution.py:323
  307.0 10.1 %collective-permute-start.30 = (bf16[2,24,2048]{2,1,0:T(8,128)(2,1)}, bf16[2,24,2048]{2,1,0:T(8,128)(2,1)S(1)}, u32[]{:S(2)}, u32[]{:S(2)}) collective-permute-start(bf16[2,24,2048]{2,1,0:T(8,128)(2,1)} %get-tuple-element.68), channel_id=1, source_target_pairs={{0,64},{64,128},{128,192},{192,256},{256,320},{320,384},{384,448},... | collective-permute-start | bytes 589832 | tf_op jit(solution)/shard_map/ppermute | solution.py:323
  (29 other events, 137.9 us)
